TPU v7x, 32 devices: a whole 2x2x4 slice. The times are simulated.
32 devices in a mesh: grp: 4 (over y, core), gx: 4 (over z), gy: 2 (over x).
Axes of the slice: x: 2, y: 2, z: 4, core: 2. Of those that a mesh axis runs over, the one named last changes fastest.
Arguments:
- previous: float32 [2, 8, 384, 256], P(None, 'grp', 'gx', 'gy'), may hold values from -6 to 6
- current: float32 [2, 8, 384, 256], P(None, 'grp', 'gx', 'gy'), may hold values from -6 to 6
- coeff: float32 [3, 8, 384, 256], P(None, 'grp', 'gx', 'gy'), may hold values from 0.05 to 0.2
- src_index: int32 [1], replicated, may hold values from 0 to 786431
- src_amp: float32 [2, 1], replicated, may hold values from -8 to 8
- rec_index: int32 [2048], replicated, may hold values from 0 to 786431
- rec_amp: float32 [2, 2048], replicated, may hold values from -8 to 8
- offsets: int32 [17], replicated, may hold values from -8 to 8, as said below
Outputs:
- images: float32 [17, 8, 384, 256], P(None, 'grp', ('gx', 'gy'))
- advanced: float32 [2, 8, 384, 256], P(None, 'grp', 'gx', 'gy')
Inputs may be any that keep to these rules, and one draw needn't show every extreme that they name: `offsets`: each whole number from -8 to 8 appears exactly once.
All inputs are finite; a program needn't handle non-finite values.
Results may differ from a plain program's by a relative error of at most 0.0003.
Values sent between devices are 32-bit elements; how exact they have to be, the bound alone decides.
No kernel may reach another device: no remote copies, remote signals or barrier semaphores. Data moves between devices by JAX's collectives and lax.ppermute only.
A program may use at most 64 MiB of HBM per device.

v0:
```python
import jax
import jax.numpy as jnp
from jax import lax
from jax.sharding import PartitionSpec as P

STEPS = 2
NOFF = 17
MAXOFF = 8


STENCIL = (-205.0 / 72.0, 8.0 / 5.0, -1.0 / 5.0, 8.0 / 315.0, -1.0 / 560.0)


def padded_2(block, sides, width):
    for axis, dim in sides:
        count = lax.axis_size(axis)
        forward = [(i, i + 1) for i in range(count - 1)]
        backward = [(target, source) for source, target in forward]
        low = lax.ppermute(
            lax.slice_in_dim(block, block.shape[dim] - width, None, axis=dim), axis, forward
        )
        high = lax.ppermute(lax.slice_in_dim(block, 0, width, axis=dim), axis, backward)
        block = jnp.concatenate([low, block, high], axis=dim)
    return block


def laplace(cur, coeff):
    wide = padded_2(cur, (("gx", 2), ("gy", 3)), 4)
    deep = padded_2(cur, (("grp", 1),), 1)
    rows = cur.shape[2]
    cols = cur.shape[3]
    dxx = STENCIL[0] * cur
    dyy = STENCIL[0] * cur
    for j in range(1, 5):
        dxx = dxx + STENCIL[j] * (
            wide[:, :, 4 + j : 4 + j + rows, 4 : 4 + cols]
            + wide[:, :, 4 - j : 4 - j + rows, 4 : 4 + cols]
        )
        dyy = dyy + STENCIL[j] * (
            wide[:, :, 4 : 4 + rows, 4 + j : 4 + j + cols]
            + wide[:, :, 4 : 4 + rows, 4 - j : 4 - j + cols]
        )
    dzz = deep[:, 2:] + deep[:, :-2] - 2.0 * cur
    return coeff[0] * dxx + coeff[1] * dyy + coeff[2] * dzz


def inject(field, index, amp):
    layers, rows, cols = field.shape
    total_rows = rows * lax.axis_size("gx")
    total_cols = cols * lax.axis_size("gy")
    layer_at = index // (total_rows * total_cols) - lax.axis_index("grp") * layers
    row_at = index // total_cols % total_rows - lax.axis_index("gx") * rows
    col_at = index % total_cols - lax.axis_index("gy") * cols
    inside = (
        (layer_at >= 0)
        & (layer_at < layers)
        & (row_at >= 0)
        & (row_at < rows)
        & (col_at >= 0)
        & (col_at < cols)
    )
    layer_at = jnp.clip(layer_at, 0, layers - 1)
    row_at = jnp.clip(row_at, 0, rows - 1)
    col_at = jnp.clip(col_at, 0, cols - 1)
    return field.at[layer_at, row_at, col_at].add(jnp.where(inside, amp, 0.0))


def correlate(source, padded, offsets, rows):
    pieces = []
    for k in range(NOFF):
        start = offsets[k] + MAXOFF
        moved = lax.dynamic_slice_in_dim(padded, start, rows, axis=2)
        pieces.append(jnp.sum(source * moved, axis=0))
    return jnp.stack(pieces)


def body(previous, current, coeff, src_index, src_amp, rec_index, rec_amp, offsets):
    prev, cur = (previous, current)
    snapshots = []
    for step in range(STEPS):
        nxt = 2.0 * cur - prev + laplace(cur, coeff)
        src_field = inject(nxt[0], src_index, src_amp[step])
        rec_field = inject(nxt[1], rec_index, rec_amp[step])
        nxt = jnp.stack([src_field, rec_field])
        snapshots.append(nxt)
        prev, cur = (cur, nxt)
    snaps = jnp.stack(snapshots)
    moved = lax.all_to_all(snaps, "gy", split_axis=3, concat_axis=4, tiled=True)
    source = moved[:, 0]
    padded = padded_2(moved[:, 1], ((("gx", "gy"), 2),), MAXOFF)
    images = correlate(source, padded, offsets, source.shape[2])
    return (images, cur)


def solution(mesh):
    return jax.shard_map(
        body,
        mesh=mesh,
        in_specs=(
            P(None, "grp", "gx", "gy"),
            P(None, "grp", "gx", "gy"),
            P(None, "grp", "gx", "gy"),
            P(),
            P(),
            P(),
            P(),
            P(),
        ),
        out_specs=(P(None, "grp", ("gx", "gy"), None), P(None, "grp", "gx", "gy")),
        check_vma=False,
    )
```

profile of v0, /device:TPU:0, one launch (start us, length us, event | category | flops | bytes accessed | tf_op | source)
XLA Modules:
  0.0 125.8 jit_solution(10291057731120663944)
XLA Ops:
  0.7 0.8 fusion.71
  1.4 1.3 %collective-permute-start = (f32[2,2,4,128]{3,2,1,0:T(4,128)S(1)}, f32[2,2,4,128]{3,2,1,0:T(4,128)S(1)}, u32[]{:S(2)}, u32[]{:S(2)}) collective-permute-start(f32[2,2,4,128]{3,2,1,0:T(4,128)S(1)} %get-tuple-element.70), channel_id=1, source_target_pairs={{2,0},{4,2},{6,4},{3,1},{5,3},{7,5},{10,8},{12,10},{14,12},{11,9},... | collective-permute-start | bytes 24584 | tf_op jit(solution)/shard_map/ppermute | solution.py:22
  2.7 5.6 %collective-permute-start.1 = (f32[2,2,4,128]{3,2,1,0:T(4,128)S(1)}, f32[2,2,4,128]{3,2,1,0:T(4,128)S(1)}, u32[]{:S(2)}, u32[]{:S(2)}) collective-permute-start(f32[2,2,4,128]{3,2,1,0:T(4,128)S(1)} %get-tuple-element.71), channel_id=1, source_target_pairs={{0,2},{2,4},{4,6},{1,3},{3,5},{5,7},{8,10},{10,12},{12,14},{9,11},... | collective-permute-start | bytes 24584 | tf_op jit(solution)/shard_map/ppermute | solution.py:19
  8.3 1.0 fusion.72
  9.3 1.3 %collective-permute-start.4 = (f32[2,1,96,128]{3,2,1,0:T(8,128)S(1)}, f32[2,1,96,128]{3,2,1,0:T(8,128)S(1)}, u32[]{:S(2)}, u32[]{:S(2)}) collective-permute-start(f32[2,1,96,128]{3,2,1,0:T(8,128)S(1)} %get-tuple-element.72), channel_id=1, source_target_pairs={{8,0},{16,8},{24,16},{9,1},{17,9},{25,17},{10,2},{18,10},{26,18},{... | collective-permute-start | bytes 294920 | tf_op jit(solution)/shard_map/ppermute | solution.py:22
  10.6 3.0 %collective-permute-start.5 = (f32[2,1,96,128]{3,2,1,0:T(8,128)S(1)}, f32[2,1,96,128]{3,2,1,0:T(8,128)S(1)}, u32[]{:S(2)}, u32[]{:S(2)}) collective-permute-start(f32[2,1,96,128]{3,2,1,0:T(8,128)S(1)} %get-tuple-element.73), channel_id=1, source_target_pairs={{0,8},{8,16},{16,24},{1,9},{9,17},{17,25},{2,10},{10,18},{18,26},{... | collective-permute-start | bytes 294920 | tf_op jit(solution)/shard_map/ppermute | solution.py:19
  14.3 0.9 constant_dynamic-update-slice_fusion.1
  15.3 1.0 slice_bitcast_fusion.4
  16.4 0.8 compare_select_fusion.2
  17.2 0.7 multiply_reduce_fusion.17
  17.9 0.8 and_reduce_fusion
  18.7 0.8 fusion.73
  19.5 0.7 broadcast_select_fusion
  20.3 0.7 and_reduce_fusion.1
  21.0 0.6 fusion.75
  23.0 1.3 %collective-permute-start.2 = (f32[2,2,104,4]{3,2,1,0:T(8,128)S(1)}, f32[2,2,104,4]{3,2,1,0:T(8,128)S(1)}, u32[]{:S(2)}, u32[]{:S(2)}) collective-permute-start(f32[2,2,104,4]{3,2,1,0:T(8,128)S(1)} %get-tuple-element.56), channel_id=1, source_target_pairs={{1,0},{3,2},{5,4},{7,6},{9,8},{11,10},{13,12},{15,14},{17,16},{19,... | collective-permute-start | bytes 19976 | tf_op jit(solution)/shard_map/ppermute | solution.py:22
  24.3 4.6 %collective-permute-start.3 = (f32[2,2,104,4]{3,2,1,0:T(8,128)S(1)}, f32[2,2,104,4]{3,2,1,0:T(8,128)S(1)}, u32[]{:S(2)}, u32[]{:S(2)}) collective-permute-start(f32[2,2,104,4]{3,2,1,0:T(8,128)S(1)} %get-tuple-element.57), channel_id=1, source_target_pairs={{0,1},{2,3},{4,5},{6,7},{8,9},{10,11},{12,13},{14,15},{16,17},{18,... | collective-permute-start | bytes 19976 | tf_op jit(solution)/shard_map/ppermute | solution.py:19
  28.9 3.5 %collective-permute-done.2 = f32[2,2,104,4]{3,2,1,0:T(8,128)S(1)} collective-permute-done((f32[2,2,104,4]{3,2,1,0:T(8,128)S(1)}, f32[2,2,104,4]{3,2,1,0:T(8,128)S(1)}, u32[]{:S(2)}, u32[]{:S(2)}) %collective-permute-start.2) | collective-permute-done | bytes 6688 | tf_op jit(solution)/shard_map/ppermute | solution.py:22
  32.4 1.7 %collective-permute-done.3 = f32[2,2,104,4]{3,2,1,0:T(8,128)S(1)} collective-permute-done((f32[2,2,104,4]{3,2,1,0:T(8,128)S(1)}, f32[2,2,104,4]{3,2,1,0:T(8,128)S(1)}, u32[]{:S(2)}, u32[]{:S(2)}) %collective-permute-start.3) | collective-permute-done | bytes 6688 | tf_op jit(solution)/shard_map/ppermute | solution.py:19
  34.2 0.2 pad_maximum_fusion
  34.4 0.5 fusion.8
  34.9 0.6 constant_dynamic-slice_fusion.1
  37.3 0.1 scatter-add.24
  37.5 11.7 %scatter_fusion = f32[24576]{0:T(1024)S(1)} fusion(f32[24576]{0:T(1024)S(1)} %bitcast.146, s32[2048]{0:T(1024)S(1)} %broadcast_select_fusion.2, f32[2048]{0:T(1024)S(1)} %broadcast_select_fusion.1), kind=kCustom, calls=%fused_computation | custom fusion | flops 2048 | bytes 32768
  49.2 1.3 %collective-permute-start.6 = (f32[2,2,4,128]{3,2,1,0:T(4,128)S(1)}, f32[2,2,4,128]{3,2,1,0:T(4,128)S(1)}, u32[]{:S(2)}, u32[]{:S(2)}) collective-permute-start(f32[2,2,4,128]{3,2,1,0:T(4,128)S(1)} %get-tuple-element.65), channel_id=1, source_target_pairs={{2,0},{4,2},{6,4},{3,1},{5,3},{7,5},{10,8},{12,10},{14,12},{11,9},... | collective-permute-start | bytes 24584 | tf_op jit(solution)/shard_map/ppermute | solution.py:22
  50.5 4.6 %collective-permute-start.7 = (f32[2,2,4,128]{3,2,1,0:T(4,128)S(1)}, f32[2,2,4,128]{3,2,1,0:T(4,128)S(1)}, u32[]{:S(2)}, u32[]{:S(2)}) collective-permute-start(f32[2,2,4,128]{3,2,1,0:T(4,128)S(1)} %get-tuple-element.64), channel_id=1, source_target_pairs={{0,2},{2,4},{4,6},{1,3},{3,5},{5,7},{8,10},{10,12},{12,14},{9,11},... | collective-permute-start | bytes 24584 | tf_op jit(solution)/shard_map/ppermute | solution.py:19
  55.2 1.3 %collective-permute-start.10 = (f32[2,1,96,128]{3,2,1,0:T(8,128)S(1)}, f32[2,1,96,128]{3,2,1,0:T(8,128)S(1)}, u32[]{:S(2)}, u32[]{:S(2)}) collective-permute-start(f32[2,1,96,128]{3,2,1,0:T(8,128)S(1)} %get-tuple-element.66), channel_id=1, source_target_pairs={{8,0},{16,8},{24,16},{9,1},{17,9},{25,17},{10,2},{18,10},{26,18},{... | collective-permute-start | bytes 294920 | tf_op jit(solution)/shard_map/ppermute | solution.py:22
  56.5 3.0 %collective-permute-start.11 = (f32[2,1,96,128]{3,2,1,0:T(8,128)S(1)}, f32[2,1,96,128]{3,2,1,0:T(8,128)S(1)}, u32[]{:S(2)}, u32[]{:S(2)}) collective-permute-start(f32[2,1,96,128]{3,2,1,0:T(8,128)S(1)} %get-tuple-element.67), channel_id=1, source_target_pairs={{0,8},{8,16},{16,24},{1,9},{9,17},{17,25},{2,10},{10,18},{18,26},{... | collective-permute-start | bytes 294920 | tf_op jit(solution)/shard_map/ppermute | solution.py:19
  59.7 1.3 %collective-permute-start.8 = (f32[2,2,104,4]{3,2,1,0:T(8,128)S(1)}, f32[2,2,104,4]{3,2,1,0:T(8,128)S(1)}, u32[]{:S(2)}, u32[]{:S(2)}) collective-permute-start(f32[2,2,104,4]{3,2,1,0:T(8,128)S(1)} %get-tuple-element.52), channel_id=1, source_target_pairs={{1,0},{3,2},{5,4},{7,6},{9,8},{11,10},{13,12},{15,14},{17,16},{19,... | collective-permute-start | bytes 19976 | tf_op jit(solution)/shard_map/ppermute | solution.py:22
  61.0 4.6 %collective-permute-start.9 = (f32[2,2,104,4]{3,2,1,0:T(8,128)S(1)}, f32[2,2,104,4]{3,2,1,0:T(8,128)S(1)}, u32[]{:S(2)}, u32[]{:S(2)}) collective-permute-start(f32[2,2,104,4]{3,2,1,0:T(8,128)S(1)} %get-tuple-element.53), channel_id=1, source_target_pairs={{0,1},{2,3},{4,5},{6,7},{8,9},{10,11},{12,13},{14,15},{16,17},{18,... | collective-permute-start | bytes 19976 | tf_op jit(solution)/shard_map/ppermute | solution.py:19
  65.6 4.1 %collective-permute-done.8 = f32[2,2,104,4]{3,2,1,0:T(8,128)S(1)} collective-permute-done((f32[2,2,104,4]{3,2,1,0:T(8,128)S(1)}, f32[2,2,104,4]{3,2,1,0:T(8,128)S(1)}, u32[]{:S(2)}, u32[]{:S(2)}) %collective-permute-start.8) | collective-permute-done | bytes 6688 | tf_op jit(solution)/shard_map/ppermute | solution.py:22
  69.7 1.3 %collective-permute-done.9 = f32[2,2,104,4]{3,2,1,0:T(8,128)S(1)} collective-permute-done((f32[2,2,104,4]{3,2,1,0:T(8,128)S(1)}, f32[2,2,104,4]{3,2,1,0:T(8,128)S(1)}, u32[]{:S(2)}, u32[]{:S(2)}) %collective-permute-start.9) | collective-permute-done | bytes 6688 | tf_op jit(solution)/shard_map/ppermute | solution.py:19
  70.9 0.2 pad_maximum_fusion.1
  71.2 0.5 fusion.21
  71.7 0.7 constant_dynamic-slice_fusion
  74.3 11.7 %scatter_fusion.1 = f32[24576]{0:T(1024)S(1)} fusion(f32[24576]{0:T(1024)S(1)} %bitcast.154, s32[2048]{0:T(1024)S(1)} %broadcast_select_fusion.2, f32[2048]{0:T(1024)S(1)} %get-tuple-element.45), kind=kCustom, calls=%fused_computation.1 | custom fusion | flops 2048 | bytes 32768
  86.1 1.1 copy.34
  87.2 3.7 %all-to-all-start = ((f32[2,2,2,96,128]{4,2,1,0,3:T(2,128)}), f32[2,2,2,96,128]{4,2,1,0,3:T(2,128)S(1)}, u32[]{:S(2)}, u32[]{:S(2)}) async-start(f32[2,2,2,96,128]{4,2,1,0,3:T(2,128)} %copy.34), calls=%async_computation | async-start | bytes 786432 | tf_op jit(solution)/shard_map/all_to_all | solution.py:88
  90.9 0.7 fusion.74
  113.1 0.3 copy.39
  113.4 0.3 all_to_all.16
  113.8 4.1 %collective-permute-start.12 = (f32[2,2,8,256]{3,2,1,0:T(8,128)S(1)}, f32[2,2,8,256]{3,2,1,0:T(8,128)S(1)}, u32[]{:S(2)}, u32[]{:S(2)}) collective-permute-start(f32[2,2,8,256]{3,2,1,0:T(8,128)S(1)} %get-tuple-element.58), channel_id=1, source_target_pairs={{0,1},{1,2},{2,3},{3,4},{4,5},{5,6},{6,7},{8,9},{9,10},{10,11},{11... | collective-permute-start | bytes 98312 | tf_op jit(solution)/shard_map/ppermute | solution.py:19
  117.9 1.3 %collective-permute-start.13 = (f32[2,2,8,256]{3,2,1,0:T(8,128)S(1)}, f32[2,2,8,256]{3,2,1,0:T(8,128)S(1)}, u32[]{:S(2)}, u32[]{:S(2)}) collective-permute-start(f32[2,2,8,256]{3,2,1,0:T(8,128)S(1)} %get-tuple-element.59), channel_id=1, source_target_pairs={{1,0},{2,1},{3,2},{4,3},{5,4},{6,5},{7,6},{9,8},{10,9},{11,10},{12... | collective-permute-start | bytes 98312 | tf_op jit(solution)/shard_map/ppermute | solution.py:22
  119.2 0.7 pad_maximum_fusion.15
  119.9 3.8 %collective-permute-done.13 = f32[2,2,8,256]{3,2,1,0:T(8,128)S(1)} collective-permute-done((f32[2,2,8,256]{3,2,1,0:T(8,128)S(1)}, f32[2,2,8,256]{3,2,1,0:T(8,128)S(1)}, u32[]{:S(2)}, u32[]{:S(2)}) %collective-permute-start.13) | collective-permute-done | bytes 32800 | tf_op jit(solution)/shard_map/ppermute | solution.py:22
  123.7 0.3 multiply_reduce_fusion.9
  124.2 0.3 multiply_reduce_fusion
  124.7 1.2 copy-done.3
  (57 shorter events, 0.8 us)
Async XLA Ops:
  0.6 19.6 %copy-start.5 = (s32[3]{0:T(128)S(1)}, s32[3]{0:T(128)}, u32[]{:S(2)}) copy-start(s32[3]{0:T(128)} %constant.241.clone.1) | copy-start | bytes 40
  0.6 22.2 %copy-start = (f32[2,2,96,128]{3,2,1,0:T(8,128)S(1)}, f32[2,2,96,128]{3,2,1,0:T(8,128)}, u32[]{:S(2)}) copy-start(f32[2,2,96,128]{3,2,1,0:T(8,128)} %param.13) | copy-start | bytes 589828
  0.7 20.3 %copy-start.4 = (f32[2,1]{0,1:T(1,128)S(1)}, f32[2,1]{0,1:T(1,128)}, u32[]{:S(2)}) copy-start(f32[2,1]{0,1:T(1,128)} %param.16) | copy-start | bytes 28
  1.4 21.4 %collective-permute-start = (f32[2,2,4,128]{3,2,1,0:T(4,128)S(1)}, f32[2,2,4,128]{3,2,1,0:T(4,128)S(1)}, u32[]{:S(2)}, u32[]{:S(2)}) collective-permute-start(f32[2,2,4,128]{3,2,1,0:T(4,128)S(1)} %get-tuple-element.70), channel_id=1, source_target_pairs={{2,0},{4,2},{6,4},{3,1},{5,3},{7,5},{10,8},{12,10},{14,12},{11,9},... | collective-permute-start | bytes 24584 | tf_op jit(solution)/shard_map/ppermute | solution.py:22
  2.7 20.1 %collective-permute-start.1 = (f32[2,2,4,128]{3,2,1,0:T(4,128)S(1)}, f32[2,2,4,128]{3,2,1,0:T(4,128)S(1)}, u32[]{:S(2)}, u32[]{:S(2)}) collective-permute-start(f32[2,2,4,128]{3,2,1,0:T(4,128)S(1)} %get-tuple-element.71), channel_id=1, source_target_pairs={{0,2},{2,4},{4,6},{1,3},{3,5},{5,7},{8,10},{10,12},{12,14},{9,11},... | collective-permute-start | bytes 24584 | tf_op jit(solution)/shard_map/ppermute | solution.py:19
  9.3 25.1 %collective-permute-start.4 = (f32[2,1,96,128]{3,2,1,0:T(8,128)S(1)}, f32[2,1,96,128]{3,2,1,0:T(8,128)S(1)}, u32[]{:S(2)}, u32[]{:S(2)}) collective-permute-start(f32[2,1,96,128]{3,2,1,0:T(8,128)S(1)} %get-tuple-element.72), channel_id=1, source_target_pairs={{8,0},{16,8},{24,16},{9,1},{17,9},{25,17},{10,2},{18,10},{26,18},{... | collective-permute-start | bytes 294920 | tf_op jit(solution)/shard_map/ppermute | solution.py:22
  10.6 23.8 %collective-permute-start.5 = (f32[2,1,96,128]{3,2,1,0:T(8,128)S(1)}, f32[2,1,96,128]{3,2,1,0:T(8,128)S(1)}, u32[]{:S(2)}, u32[]{:S(2)}) collective-permute-start(f32[2,1,96,128]{3,2,1,0:T(8,128)S(1)} %get-tuple-element.73), channel_id=1, source_target_pairs={{0,8},{8,16},{16,24},{1,9},{9,17},{17,25},{2,10},{10,18},{18,26},{... | collective-permute-start | bytes 294920 | tf_op jit(solution)/shard_map/ppermute | solution.py:19
  16.3 18.1 %copy-start.1 = (f32[2,2,96,128]{3,2,1,0:T(8,128)S(1)}, f32[2,2,96,128]{3,2,1,0:T(8,128)}, u32[]{:S(2)}) copy-start(f32[2,2,96,128]{3,2,1,0:T(8,128)} %param.12) | copy-start | bytes 589828
  23.0 9.4 %collective-permute-start.2 = (f32[2,2,104,4]{3,2,1,0:T(8,128)S(1)}, f32[2,2,104,4]{3,2,1,0:T(8,128)S(1)}, u32[]{:S(2)}, u32[]{:S(2)}) collective-permute-start(f32[2,2,104,4]{3,2,1,0:T(8,128)S(1)} %get-tuple-element.56), channel_id=1, source_target_pairs={{1,0},{3,2},{5,4},{7,6},{9,8},{11,10},{13,12},{15,14},{17,16},{19,... | collective-permute-start | bytes 19976 | tf_op jit(solution)/shard_map/ppermute | solution.py:22
  24.3 9.9 %collective-permute-start.3 = (f32[2,2,104,4]{3,2,1,0:T(8,128)S(1)}, f32[2,2,104,4]{3,2,1,0:T(8,128)S(1)}, u32[]{:S(2)}, u32[]{:S(2)}) collective-permute-start(f32[2,2,104,4]{3,2,1,0:T(8,128)S(1)} %get-tuple-element.57), channel_id=1, source_target_pairs={{0,1},{2,3},{4,5},{6,7},{8,9},{10,11},{12,13},{14,15},{16,17},{18,... | collective-permute-start | bytes 19976 | tf_op jit(solution)/shard_map/ppermute | solution.py:19
  49.2 10.3 %collective-permute-start.6 = (f32[2,2,4,128]{3,2,1,0:T(4,128)S(1)}, f32[2,2,4,128]{3,2,1,0:T(4,128)S(1)}, u32[]{:S(2)}, u32[]{:S(2)}) collective-permute-start(f32[2,2,4,128]{3,2,1,0:T(4,128)S(1)} %get-tuple-element.65), channel_id=1, source_target_pairs={{2,0},{4,2},{6,4},{3,1},{5,3},{7,5},{10,8},{12,10},{14,12},{11,9},... | collective-permute-start | bytes 24584 | tf_op jit(solution)/shard_map/ppermute | solution.py:22
  50.5 9.0 %collective-permute-start.7 = (f32[2,2,4,128]{3,2,1,0:T(4,128)S(1)}, f32[2,2,4,128]{3,2,1,0:T(4,128)S(1)}, u32[]{:S(2)}, u32[]{:S(2)}) collective-permute-start(f32[2,2,4,128]{3,2,1,0:T(4,128)S(1)} %get-tuple-element.64), channel_id=1, source_target_pairs={{0,2},{2,4},{4,6},{1,3},{3,5},{5,7},{8,10},{10,12},{12,14},{9,11},... | collective-permute-start | bytes 24584 | tf_op jit(solution)/shard_map/ppermute | solution.py:19
  55.2 16.0 %collective-permute-start.10 = (f32[2,1,96,128]{3,2,1,0:T(8,128)S(1)}, f32[2,1,96,128]{3,2,1,0:T(8,128)S(1)}, u32[]{:S(2)}, u32[]{:S(2)}) collective-permute-start(f32[2,1,96,128]{3,2,1,0:T(8,128)S(1)} %get-tuple-element.66), channel_id=1, source_target_pairs={{8,0},{16,8},{24,16},{9,1},{17,9},{25,17},{10,2},{18,10},{26,18},{... | collective-permute-start | bytes 294920 | tf_op jit(solution)/shard_map/ppermute | solution.py:22
  56.5 14.7 %collective-permute-start.11 = (f32[2,1,96,128]{3,2,1,0:T(8,128)S(1)}, f32[2,1,96,128]{3,2,1,0:T(8,128)S(1)}, u32[]{:S(2)}, u32[]{:S(2)}) collective-permute-start(f32[2,1,96,128]{3,2,1,0:T(8,128)S(1)} %get-tuple-element.67), channel_id=1, source_target_pairs={{0,8},{8,16},{16,24},{1,9},{9,17},{17,25},{2,10},{10,18},{18,26},{... | collective-permute-start | bytes 294920 | tf_op jit(solution)/shard_map/ppermute | solution.py:19
  59.7 10.0 %collective-permute-start.8 = (f32[2,2,104,4]{3,2,1,0:T(8,128)S(1)}, f32[2,2,104,4]{3,2,1,0:T(8,128)S(1)}, u32[]{:S(2)}, u32[]{:S(2)}) collective-permute-start(f32[2,2,104,4]{3,2,1,0:T(8,128)S(1)} %get-tuple-element.52), channel_id=1, source_target_pairs={{1,0},{3,2},{5,4},{7,6},{9,8},{11,10},{13,12},{15,14},{17,16},{19,... | collective-permute-start | bytes 19976 | tf_op jit(solution)/shard_map/ppermute | solution.py:22
  61.0 9.9 %collective-permute-start.9 = (f32[2,2,104,4]{3,2,1,0:T(8,128)S(1)}, f32[2,2,104,4]{3,2,1,0:T(8,128)S(1)}, u32[]{:S(2)}, u32[]{:S(2)}) collective-permute-start(f32[2,2,104,4]{3,2,1,0:T(8,128)S(1)} %get-tuple-element.53), channel_id=1, source_target_pairs={{0,1},{2,3},{4,5},{6,7},{8,9},{10,11},{12,13},{14,15},{16,17},{18,... | collective-permute-start | bytes 19976 | tf_op jit(solution)/shard_map/ppermute | solution.py:19
  86.0 4.8 %copy-start.2 = (s32[17]{0:T(128)S(1)}, s32[17]{0:T(128)}, u32[]{:S(2)}) copy-start(s32[17]{0:T(128)} %param.19) | copy-start | bytes 208
  87.2 25.9 %all-to-all-start = ((f32[2,2,2,96,128]{4,2,1,0,3:T(2,128)}), f32[2,2,2,96,128]{4,2,1,0,3:T(2,128)S(1)}, u32[]{:S(2)}, u32[]{:S(2)}) async-start(f32[2,2,2,96,128]{4,2,1,0,3:T(2,128)} %copy.34), calls=%async_computation | async-start | bytes 786432 | tf_op jit(solution)/shard_map/all_to_all | solution.py:88
  113.8 6.1 %collective-permute-start.12 = (f32[2,2,8,256]{3,2,1,0:T(8,128)S(1)}, f32[2,2,8,256]{3,2,1,0:T(8,128)S(1)}, u32[]{:S(2)}, u32[]{:S(2)}) collective-permute-start(f32[2,2,8,256]{3,2,1,0:T(8,128)S(1)} %get-tuple-element.58), channel_id=1, source_target_pairs={{0,1},{1,2},{2,3},{3,4},{4,5},{5,6},{6,7},{8,9},{9,10},{10,11},{11... | collective-permute-start | bytes 98312 | tf_op jit(solution)/shard_map/ppermute | solution.py:19
  117.9 5.8 %collective-permute-start.13 = (f32[2,2,8,256]{3,2,1,0:T(8,128)S(1)}, f32[2,2,8,256]{3,2,1,0:T(8,128)S(1)}, u32[]{:S(2)}, u32[]{:S(2)}) collective-permute-start(f32[2,2,8,256]{3,2,1,0:T(8,128)S(1)} %get-tuple-element.59), channel_id=1, source_target_pairs={{1,0},{2,1},{3,2},{4,3},{5,4},{6,5},{7,6},{9,8},{10,9},{11,10},{12... | collective-permute-start | bytes 98312 | tf_op jit(solution)/shard_map/ppermute | solution.py:22
  124.7 1.2 copy-start.3
where the time goes:
time: 127 us; the launch traced here: 126 us
  starting transfers between devices  42.2 us (33%)
  other arithmetic  30 us (24%)
  between operations  28.4 us (22%)
  waiting for transfers between devices  14.5 us (11%)
  local copies, waits for them, and re-layouts  10.7 us (8%)
    ppermute x7, starting transfers between devices, padded_2(): lax.ppermute(lax.slice_in_dim(block, block.shape[dim] - width, None, axis...  29.5 us
    unnamed x5, other arithmetic  24.9 us
    ppermute x7, waiting for transfers between devices, padded_2(): lax.ppermute(lax.slice_in_dim(block, 0, width, axis=dim), axis, backward)  11.4 us
    ppermute x7, starting transfers between devices, padded_2(): lax.ppermute(lax.slice_in_dim(block, 0, width, axis=dim), axis, backward)  9.03 us
    all_to_all x1, starting transfers between devices, body(): moved = lax.all_to_all(snaps, 'gy', split_axis=3, concat_axis=4, tiled=True)  3.68 us
    ppermute x7, waiting for transfers between devices, padded_2(): lax.ppermute(lax.slice_in_dim(block, block.shape[dim] - width, None, axis...  3.03 us
  transfers between devices with their start and end apart: 15, of which 5 were waited for; matrix products, arithmetic and copies ran while one was open for 8% of the time, Pallas kernels for 0%

commit v1 on v0

--- a/solution.py
+++ b/solution.py
@@ -1,11 +1,16 @@
+import functools
+
 import jax
 import jax.numpy as jnp
 from jax import lax
+from jax.experimental import pallas as pl
+from jax.experimental.pallas import tpu as pltpu
 from jax.sharding import PartitionSpec as P
 
 STEPS = 2
 NOFF = 17
 MAXOFF = 8
+REACH = 4
 
 
 STENCIL = (-205.0 / 72.0, 8.0 / 5.0, -1.0 / 5.0, 8.0 / 315.0, -1.0 / 560.0)
@@ -74,7 +79,7 @@
     return jnp.stack(pieces)
 
 
-def body(previous, current, coeff, src_index, src_amp, rec_index, rec_amp, offsets):
+def body_tiles(previous, current, coeff, src_index, src_amp, rec_index, rec_amp, offsets):
     prev, cur = (previous, current)
     snapshots = []
     for step in range(STEPS):
@@ -92,7 +97,476 @@
     return (images, cur)
 
 
+VMEM = pl.BlockSpec(memory_space=pltpu.VMEM)
+SMEM = pl.BlockSpec(memory_space=pltpu.SMEM)
+HBM = pl.BlockSpec(memory_space=pl.ANY)
+
+
+class Plan:
+    def __init__(self, shape, mesh_shape):
+        self.fields, self.lays, self.rows, self.cols = shape
+        self.n_grp, self.n_gx, self.n_gy = (mesh_shape[k] for k in ("grp", "gx", "gy"))
+        self.nx = self.rows * self.n_gx
+        self.ny = self.cols * self.n_gy
+        self.half = self.rows // self.n_gy
+        self.d2 = MAXOFF
+        self.d1 = MAXOFF + REACH
+        self.d0 = MAXOFF + 2 * REACH
+        self.inside = self.half + self.d0
+        self.e0 = self.half + 2 * self.d0
+        self.e1 = self.half + 2 * self.d1
+        self.e2 = self.half + 2 * self.d2
+
+    def fits(self):
+        return (
+            self.n_gy == 2
+            and self.n_grp % 2 == 0
+            and self.n_gx % 2 == 0
+            and self.rows % 16 == 0
+            and self.cols % 128 == 0
+            and self.inside <= self.rows
+            and STEPS == 2
+        )
+
+    def base_row(self):
+        return lax.axis_index("gx") * self.rows + lax.axis_index("gy") * self.half
+
+
+def cost(flops, moved):
+    return pl.CostEstimate(flops=flops, bytes_accessed=moved, transcendentals=0)
+
+
+def f32(*shape):
+    return jax.ShapeDtypeStruct(shape, jnp.float32)
+
+
+def pack_kernel(p, count, *refs):
+    sources = refs[:count]
+    outs = refs[count : count + 4]
+    sems = refs[count + 4]
+    b = lax.axis_index("gy")
+    starts = (
+        (b * (p.rows - p.inside), p.inside),
+        ((1 - b) * (p.rows - p.inside), p.inside),
+        ((1 - b) * (p.rows - p.d0), p.d0),
+        (b * (p.rows - p.d0), p.d0),
+    )
+    copies = []
+    plane = 0
+    for i, source in enumerate(sources):
+        planes = source.shape[0]
+        for j, (start, size) in enumerate(starts):
+            copies.append(
+                pltpu.make_async_copy(
+                    source.at[:, pl.ds(pl.multiple_of(start, 8), size), :],
+                    outs[j].at[pl.ds(plane, planes)],
+                    sems.at[i, j],
+                )
+            )
+        plane += planes
+    for copy in copies:
+        copy.start()
+    for copy in copies:
+        copy.wait()
+
+
+def pack(p, *sources):
+    planes = sum(s.shape[0] for s in sources)
+    return pl.pallas_call(
+        functools.partial(pack_kernel, p, len(sources)),
+        out_shape=(
+            f32(planes, p.inside, p.cols),
+            f32(planes, p.inside, p.cols),
+            f32(planes, p.d0, p.cols),
+            f32(planes, p.d0, p.cols),
+        ),
+        in_specs=[HBM] * len(sources),
+        out_specs=(VMEM,) * 4,
+        scratch_shapes=[pltpu.SemaphoreType.DMA((len(sources), 4))],
+        cost_estimate=cost(0, 4 * planes * p.rows * p.cols * 3),
+    )(*sources)
+
+
+def lay_out(p, target, own, other, halo_own, halo_other):
+    a = lax.axis_index("gx")
+    b = lax.axis_index("gy")
+    mine = pl.ds(pl.multiple_of(b * p.cols, p.cols), p.cols)
+    theirs = pl.ds(pl.multiple_of((1 - b) * p.cols, p.cols), p.cols)
+    inner = pl.ds(pl.multiple_of((1 - b) * p.d0, 8), p.inside)
+    outer = pl.ds(pl.multiple_of(b * p.inside, 8), p.d0)
+    there = jnp.where(b == 0, a > 0, a < p.n_gx - 1)
+    target[:, inner, mine] = own[...]
+    target[:, inner, theirs] = other[...]
+    target[:, outer, mine] = jnp.where(there, halo_own[...], 0.0)
+    target[:, outer, theirs] = jnp.where(there, halo_other[...], 0.0)
+
+
+def send_layers(p, whole, send_a, send_b, shift, count):
+    odd = lax.rem(lax.axis_index("grp"), 2)
+    lay_a = (1 - odd) * (p.lays - 1)
+    lay_b = odd * (p.lays - 1)
+    for f in range(p.fields):
+        send_a[f] = whole[f * p.lays + lay_a, shift : shift + count, :]
+        send_b[f] = whole[f * p.lays + lay_b, shift : shift + count, :]
+
+
+def join_kernel(p, own, other, halo_own, halo_other, whole, send_a, send_b):
+    lay_out(p, whole, own, other, halo_own, halo_other)
+    send_layers(p, whole, send_a, send_b, p.d0 - p.d1, p.e1)
+
+
+def join(p, own, other, halo_own, halo_other):
+    planes = own.shape[0]
+    return pl.pallas_call(
+        functools.partial(join_kernel, p),
+        out_shape=(
+            f32(planes, p.e0, p.ny),
+            f32(p.fields, p.e1, p.ny),
+            f32(p.fields, p.e1, p.ny),
+        ),
+        in_specs=[VMEM] * 4,
+        out_specs=(VMEM,) * 3,
+        cost_estimate=cost(0, 8 * planes * p.e0 * p.ny),
+    )(own, other, halo_own, halo_other)
+
+
+def spread_kernel(p, index, amp, out, row_hot, col_hot, total):
+    lays, stride = p.lays, p.e0
+    g = lax.axis_index("grp")
+    first = p.base_row() - p.d1
+    wide = index.shape[0]
+    grid_row = first + lax.broadcasted_iota(jnp.int32, (stride, 128), 0)
+    known = (grid_row >= 0) & (grid_row < p.nx)
+    wanted = [
+        jnp.where(known, (g * lays + lay) * p.nx + grid_row, -1) for lay in range(lays)
+    ]
+    column = lax.broadcasted_iota(jnp.int32, (p.ny, 128), 0)
+    for k in range(wide):
+        at = pl.ds(k * 128, 128)
+        flat = index[k : k + 1, :]
+        row = jnp.floor((flat.astype(jnp.float32) + 0.5) * (1.0 / p.ny)).astype(jnp.int32)
+        col = flat - row * p.ny
+        col_hot[:, at] = jnp.where(column == col, 1.0, 0.0).astype(jnp.bfloat16)
+        for step in range(STEPS):
+            rest = amp[step, k : k + 1, :]
+            parts = []
+            for _ in range(3):
+                part = rest.astype(jnp.bfloat16).astype(jnp.float32)
+                parts.append(part)
+                rest = rest - part
+            for lay in range(lays):
+                hit = wanted[lay] == row
+                for i, part in enumerate(parts):
+                    start = ((step * 3 + i) * lays + lay) * stride
+                    row_hot[start : start + stride, at] = jnp.where(
+                        hit, part, 0.0
+                    ).astype(jnp.bfloat16)
+    total[...] = lax.dot_general(
+        row_hot[...],
+        col_hot[...],
+        (((1,), (1,)), ((), ())),
+        preferred_element_type=jnp.float32,
+    )
+    for step in range(STEPS):
+        for lay in range(lays):
+            rows = [((step * 3 + i) * lays + lay) * stride for i in range(3)]
+            out[step, lay] = (
+                total[rows[0] : rows[0] + p.e1]
+                + total[rows[1] : rows[1] + p.e1]
+                + total[rows[2] : rows[2] + p.e1]
+            )
+
+
+def spread(p, index, amp):
+    count = index.shape[0]
+    wide = -(-count // 128)
+    extra = wide * 128 - count
+    if extra:
+        index = jnp.pad(index, (0, extra))
+        amp = jnp.pad(amp, ((0, 0), (0, extra)))
+    tall = STEPS * 3 * p.lays * p.e0
+    return pl.pallas_call(
+        functools.partial(spread_kernel, p),
+        out_shape=f32(STEPS, p.lays, p.e1, p.ny),
+        in_specs=[VMEM] * 2,
+        out_specs=VMEM,
+        scratch_shapes=[
+            pltpu.VMEM((tall, wide * 128), jnp.bfloat16),
+            pltpu.VMEM((p.ny, wide * 128), jnp.bfloat16),
+            pltpu.VMEM((tall, p.ny), jnp.float32),
+        ],
+        cost_estimate=cost(2 * tall * wide * 128 * p.ny, 4 * wide * 128 * 3),
+    )(index.reshape(wide, 128), amp.reshape(STEPS, wide, 128))
+
+
+def advance(p, now, before, before_at, coeff, coeff_at, recv_a, recv_b, added, added_at, out, margin):
+    g = lax.axis_index("grp")
+    even = lax.rem(g, 2) == 0
+    beyond = jnp.where(even, g > 0, g < p.n_grp - 1)
+    first = p.base_row() - margin
+    count = p.half + 2 * margin
+    column = lax.broadcasted_iota(jnp.int32, (8, p.ny), 1)
+    line = lax.broadcasted_iota(jnp.int32, (8, p.ny), 0)
+    for r in range(0, count, 8):
+        rows = slice(r, r + 8)
+        weights = [
+            [coeff[i * p.lays + lay, coeff_at + r : coeff_at + r + 8, :] for i in range(3)]
+            for lay in range(p.lays)
+        ]
+        edge = r < margin or r + 8 > p.half + margin
+        if edge:
+            grid_row = first + r + line
+            known = (grid_row >= 0) & (grid_row < p.nx)
+        for f in range(p.fields):
+            far = jnp.where(beyond, recv_b[f, rows, :], 0.0)
+            near = recv_a[f, rows, :]
+            below = jnp.where(even, far, near)
+            above = jnp.where(even, near, far)
+            mids = [
+                now[f * p.lays + lay, REACH + r : REACH + r + 8, :] for lay in range(p.lays)
+            ]
+            column_of = [below] + mids + [above]
+            for lay in range(p.lays):
+                plane = f * p.lays + lay
+                x = mids[lay]
+                dxx = STENCIL[0] * x
+                dyy = STENCIL[0] * x
+                for j in range(1, REACH + 1):
+                    dxx = dxx + STENCIL[j] * (
+                        now[plane, REACH + r + j : REACH + r + j + 8, :]
+                        + now[plane, REACH + r - j : REACH + r - j + 8, :]
+                    )
+                    right = jnp.where(column < p.ny - j, pltpu.roll(x, p.ny - j, 1), 0.0)
+                    left = jnp.where(column >= j, pltpu.roll(x, j, 1), 0.0)
+                    dyy = dyy + STENCIL[j] * (right + left)
+                dzz = column_of[lay] + column_of[lay + 2] - 2.0 * x
+                w = weights[lay]
+                new = (
+                    2.0 * x
+                    - before[plane, before_at + r : before_at + r + 8, :]
+                    + (w[0] * dxx + w[1] * dyy + w[2] * dzz)
+                )
+                if f == 1:
+                    new = new + added[lay, added_at + r : added_at + r + 8, :]
+                if edge:
+                    new = jnp.where(known, new, 0.0)
+                out[plane, rows, :] = new
+
+
+def add_source(p, step, index, amp, out, margin):
+    g = lax.axis_index("grp")
+    first = p.base_row() - margin
+    count = p.half + 2 * margin
+    for s in range(index.shape[0]):
+        flat = index[s]
+        line = lax.div(flat, p.ny)
+        lay = lax.div(line, p.nx) - g * p.lays
+        row = lax.rem(line, p.nx) - first
+        col = lax.rem(flat, p.ny)
+
+        @pl.when((lay >= 0) & (lay < p.lays) & (row >= 0) & (row < count))
+        def _():
+            spot = lax.broadcasted_iota(jnp.int32, (1, p.ny), 1) == col
+            out[lay, pl.ds(row, 1), :] += jnp.where(spot, amp[step, s], 0.0)
+
+
+def first_kernel(
+    p, now, recv_a, recv_b, own, other, halo_own, halo_other, added, index, amp,
+    out, coeff_out, send_a, send_b, rest,
+):
+    lay_out(p, rest, own, other, halo_own, halo_other)
+    planes = p.fields * p.lays
+    gap = p.d0 - p.d1
+    coeff_out[...] = rest[planes:, p.d0 - p.d2 : p.d0 - p.d2 + p.e2, :]
+    advance(
+        p, now, rest, gap, rest.at[planes:], gap, recv_a, recv_b, added.at[0], 0, out, p.d1
+    )
+    add_source(p, 0, index, amp, out, p.d1)
+    send_layers(p, out, send_a, send_b, p.d1 - p.d2, p.e2)
+
+
+def first_step(p, now, recv_a, recv_b, rest, added, index, amp):
+    planes = p.fields * p.lays
+    return pl.pallas_call(
+        functools.partial(first_kernel, p),
+        out_shape=(
+            f32(planes, p.e1, p.ny),
+            f32(3 * p.lays, p.e2, p.ny),
+            f32(p.fields, p.e2, p.ny),
+            f32(p.fields, p.e2, p.ny),
+        ),
+        in_specs=[VMEM] * 8 + [SMEM] * 2,
+        out_specs=(VMEM,) * 4,
+        scratch_shapes=[pltpu.VMEM((planes + 3 * p.lays, p.e0, p.ny), jnp.float32)],
+        cost_estimate=cost(60 * planes * p.e1 * p.ny, 8 * planes * p.e1 * p.ny),
+    )(now, recv_a, recv_b, *rest, added, index, amp)
+
+
+def second_kernel(p, now, before, coeff, recv_a, recv_b, added, index, amp, out, keep, give):
+    gap = p.d1 - p.d2
+    advance(
+        p, now, before, p.d0 - p.d2, coeff, 0, recv_a, recv_b, added.at[1], gap, out, p.d2
+    )
+    add_source(p, 1, index, amp, out, p.d2)
+    b = lax.axis_index("gy")
+    mine = pl.ds(pl.multiple_of(b * p.cols, p.cols), p.cols)
+    theirs = pl.ds(pl.multiple_of((1 - b) * p.cols, p.cols), p.cols)
+    keep[...] = out[:, p.d2 : p.d2 + p.half, mine]
+    give[...] = out[:, p.d2 : p.d2 + p.half, theirs]
+
+
+def second_step(p, now, before, coeff, recv_a, recv_b, added, index, amp):
+    planes = p.fields * p.lays
+    return pl.pallas_call(
+        functools.partial(second_kernel, p),
+        out_shape=(
+            f32(planes, p.e2, p.ny),
+            f32(planes, p.half, p.cols),
+            f32(planes, p.half, p.cols),
+        ),
+        in_specs=[VMEM] * 6 + [SMEM] * 2,
+        out_specs=(VMEM,) * 3,
+        cost_estimate=cost(60 * planes * p.e2 * p.ny, 8 * planes * p.e2 * p.ny),
+    )(now, before, coeff, recv_a, recv_b, added, index, amp)
+
+
+def image_kernel(p, one, two, offsets, out, held, place, sems):
+    for k in range(NOFF):
+        place[offsets[k] + MAXOFF] = k
+    copies = []
+    for d in range(NOFF):
+        shift = d - MAXOFF
+        for lay in range(p.lays):
+            for r in range(0, p.half, 8):
+                s1 = one[lay, p.d1 + r : p.d1 + r + 8, :]
+                r1 = one[p.lays + lay, p.d1 + r + shift : p.d1 + r + shift + 8, :]
+                s2 = two[lay, p.d2 + r : p.d2 + r + 8, :]
+                r2 = two[p.lays + lay, p.d2 + r + shift : p.d2 + r + shift + 8, :]
+                held[d, lay, r : r + 8, :] = s1 * r1 + s2 * r2
+        copy = pltpu.make_async_copy(held.at[d], out.at[place[d]], sems.at[d])
+        copy.start()
+        copies.append(copy)
+    for copy in copies:
+        copy.wait()
+
+
+def correlate_rows(p, one, two, offsets):
+    size = NOFF * p.lays * p.half * p.ny
+    return pl.pallas_call(
+        functools.partial(image_kernel, p),
+        out_shape=f32(NOFF, p.lays, p.half, p.ny),
+        in_specs=[VMEM] * 2 + [SMEM],
+        out_specs=HBM,
+        scratch_shapes=[
+            pltpu.VMEM((NOFF, p.lays, p.half, p.ny), jnp.float32),
+            pltpu.SMEM((NOFF,), jnp.int32),
+            pltpu.SemaphoreType.DMA((NOFF,)),
+        ],
+        cost_estimate=cost(3 * size, 4 * size),
+    )(one, two, offsets)
+
+
+def settle_kernel(p, keep, got, out, sems):
+    b = lax.axis_index("gy")
+    copies = [
+        pltpu.make_async_copy(
+            source,
+            out.at[:, pl.ds(pl.multiple_of(at * p.half, 8), p.half), :],
+            sems.at[i],
+        )
+        for i, (source, at) in enumerate(((keep, b), (got, 1 - b)))
+    ]
+    for copy in copies:
+        copy.start()
+    for copy in copies:
+        copy.wait()
+
+
+def settle(p, keep, got):
+    planes = p.fields * p.lays
+    return pl.pallas_call(
+        functools.partial(settle_kernel, p),
+        out_shape=f32(planes, p.rows, p.cols),
+        in_specs=[VMEM] * 2,
+        out_specs=HBM,
+        scratch_shapes=[pltpu.SemaphoreType.DMA((2,))],
+        cost_estimate=cost(0, 8 * planes * p.rows * p.cols),
+    )(keep, got)
+
+
+def pairs_grp(p):
+    return [(g, g ^ 1) for g in range(p.n_grp)]
+
+
+def pairs_between(p):
+    pairs = []
+    for g in range(p.n_grp):
+        to = g + 1 if g % 2 else g - 1
+        for a in range(p.n_gx):
+            goal = (to, a) if 0 <= to < p.n_grp else (g, a ^ 1)
+            pairs.append((g * p.n_gx + a, goal[0] * p.n_gx + goal[1]))
+    return pairs
+
+
+def halo_straight(p):
+    pairs = []
+    for a in range(p.n_gx):
+        for b in range(2):
+            to = (a + 1 if b == 0 else a - 1) % p.n_gx
+            pairs.append((a * 2 + b, to * 2 + b))
+    return pairs
+
+
+def halo_across(p):
+    pairs = []
+    for a in range(p.n_gx):
+        for b in range(2):
+            to = (a - 1 if b == 0 else a + 1) % p.n_gx
+            pairs.append((a * 2 + b, to * 2 + 1 - b))
+    return pairs
+
+
+def body_rows(p, previous, current, coeff, src_index, src_amp, rec_index, rec_amp, offsets):
+    planes = p.fields * p.lays
+    tile = (p.rows, p.cols)
+
+    def redistribute(*sources):
+        own, give, edge, corner = pack(p, *sources)
+        other = lax.ppermute(give, "gy", [(0, 1), (1, 0)])
+        halo_own = lax.ppermute(edge, ("gx", "gy"), halo_straight(p))
+        halo_other = lax.ppermute(corner, ("gx", "gy"), halo_across(p))
+        return own, other, halo_own, halo_other
+
+    def swap_layers(send_a, send_b):
+        recv_a = lax.ppermute(send_a, "grp", pairs_grp(p))
+        recv_b = lax.ppermute(send_b, ("grp", "gx"), pairs_between(p))
+        return recv_a, recv_b
+
+    now = redistribute(current.reshape(planes, *tile))
+    rest = redistribute(previous.reshape(planes, *tile), coeff.reshape(3 * p.lays, *tile))
+    added = spread(p, rec_index, rec_amp)
+    whole, send_a, send_b = join(p, *now)
+    recv_a, recv_b = swap_layers(send_a, send_b)
+    one, weights, send_a, send_b = first_step(
+        p, whole, recv_a, recv_b, rest, added, src_index, src_amp
+    )
+    recv_a, recv_b = swap_layers(send_a, send_b)
+    two, keep, give = second_step(
+        p, one, whole, weights, recv_a, recv_b, added, src_index, src_amp
+    )
+    got = lax.ppermute(give, "gy", [(0, 1), (1, 0)])
+    images = correlate_rows(p, one, two, offsets)
+    advanced = settle(p, keep, got)
+    return images, advanced.reshape(p.fields, p.lays, *tile)
+
+
 def solution(mesh):
+    def body(previous, *others):
+        p = Plan(previous.shape, mesh.shape)
+        if p.fits():
+            return body_rows(p, previous, *others)
+        return body_tiles(previous, *others)
+
     return jax.shard_map(
         body,
         mesh=mesh,

time: 127 us -> 54.1 us (0.43)
  other arithmetic: 30 us -> 0 us
  between operations: 28.4 us -> 1.39 us
  starting transfers between devices: 42.2 us -> 16.5 us
  Pallas kernels: 0 us -> 19.8 us
  local copies, waits for them, and re-layouts: 10.7 us -> 5.37 us
  waiting for transfers between devices: 14.5 us -> 10.7 us
    unnamed x5 -> x0, other arithmetic: 24.9 us -> none
    ppermute x14 -> x11, starting transfers between devices: 38.6 us -> 16.5 us  [the longest x2 8.18 us: redistribute(): halo_other = lax.ppermute(corner, ('gx', 'gy'), halo_across(p))]
    pallas_call x0 -> x8, Pallas kernels: none -> 19.8 us  [the longest x2 3.87 us: pack(): pl.pallas_call(functools.partial(pack_kernel, p, len(sources)), out_shape...]
    slice x10 -> x0, local copies, waits for them, and re-layouts: 4.15 us -> none  [the longest x4 1.97 us: padded_2(): lax.slice_in_dim(block, 0, width, axis=dim)]
    ppermute x14 -> x11, waiting for transfers between devices: 14.4 us -> 10.7 us  [the longest x2 3.67 us: swap_layers(): recv_b = lax.ppermute(send_b, ('grp', 'gx'), pairs_between(p))]
    all_to_all x1 -> x0, starting transfers between devices: 3.68 us -> none  [body(): moved = lax.all_to_all(snaps, 'gy', split_axis=3, concat_axis=4, tiled=True)]
    unnamed x29 -> x24, local copies, waits for them, and re-layouts: 2.29 us -> 5.37 us
    another operation x4 -> x0, local copies, waits for them, and re-layouts: 2.34 us -> none
  transfers between devices with their start and end apart: 15 -> 11, of which waited for: 5 -> 6; matrix products, arithmetic and copies ran while one was open for 8% -> 5% of each run, Pallas kernels for 0% -> 17%
where the time goes in v1:
time: 54.1 us; the launch traced here: 53.7 us
  Pallas kernels  19.8 us (37%)
  starting transfers between devices  16.5 us (30%)
  waiting for transfers between devices  10.7 us (20%)
  local copies, waits for them, and re-layouts  5.37 us (10%)
  between operations  1.39 us (3%)
    ppermute x2, starting transfers between devices, redistribute(): halo_other = lax.ppermute(corner, ('gx', 'gy'), halo_across(p))  8.18 us
    unnamed x24, local copies, waits for them, and re-layouts  5.37 us
    pallas_call x2, Pallas kernels, pack(): pl.pallas_call(functools.partial(pack_kernel, p, len(sources)), out_shape...  3.87 us
    ppermute x2, waiting for transfers between devices, swap_layers(): recv_b = lax.ppermute(send_b, ('grp', 'gx'), pairs_between(p))  3.67 us
    pallas_call x1, Pallas kernels, first_step(): pl.pallas_call(functools.partial(first_kernel, p), out_shape=(f32(planes,...  3.55 us
    pallas_call x1, Pallas kernels, second_step(): pl.pallas_call(functools.partial(second_kernel, p), out_shape=(f32(planes...  3.18 us
    pallas_call x1, Pallas kernels, spread(): pl.pallas_call(functools.partial(spread_kernel, p), out_shape=f32(STEPS,...  3.12 us
    ppermute x2, starting transfers between devices, redistribute(): other = lax.ppermute(give, 'gy', [(0, 1), (1, 0)])  3.12 us
  transfers between devices with their start and end apart: 11, of which 6 were waited for; matrix products, arithmetic and copies ran while one was open for 5% of the time, Pallas kernels for 17%

profile of v1, /device:TPU:0, one launch (start us, length us, event | category | flops | bytes accessed | tf_op | source)
XLA Modules:
  0.0 53.7 jit_solution(11624193367802997043)
XLA Ops:
  0.6 2.1 %shard_map.97 = (f32[10,64,128]{2,1,0:T(8,128)}, f32[10,64,128]{2,1,0:T(8,128)}, f32[10,16,128]{2,1,0:T(8,128)}, f32[10,16,128]{2,1,0:T(8,128)}) custom-call(f32[4,96,128]{2,1,0:T(8,128)} %bitcast.12, f32[6,96,128]{2,1,0:T(8,128)} %bitcast.9), custom_call_target="tpu_custom_call" | custom-call | bytes 1474560 | tf_op jit(solution)/shard_map/pallas_call | solution.py:175
  2.8 3.0 %collective-permute-start.5 = (f32[10,64,128]{2,1,0:T(8,128)}, f32[10,64,128]{2,1,0:T(8,128)S(1)}, u32[]{:S(2)}, u32[]{:S(2)}) collective-permute-start(f32[10,64,128]{2,1,0:T(8,128)} %get-tuple-element.28), channel_id=1, source_target_pairs={{0,1},{1,0},{2,3},{3,2},{4,5},{5,4},{6,7},{7,6},{8,9},{9,8},{10,11... | collective-permute-start | bytes 983048 | tf_op jit(solution)/shard_map/ppermute | solution.py:535
  5.8 1.7 %shard_map.95 = (f32[4,64,128]{2,1,0:T(8,128)}, f32[4,64,128]{2,1,0:T(8,128)}, f32[4,16,128]{2,1,0:T(8,128)}, f32[4,16,128]{2,1,0:T(8,128)}) custom-call(f32[4,96,128]{2,1,0:T(8,128)} %bitcast.10), custom_call_target="tpu_custom_call" | custom-call | bytes 589824 | tf_op jit(solution)/shard_map/pallas_call | solution.py:175
  7.5 0.1 collective-permute-start
  7.6 2.1 %collective-permute-start.1 = (f32[4,16,128]{2,1,0:T(8,128)}, f32[4,16,128]{2,1,0:T(8,128)S(1)}, u32[]{:S(2)}, u32[]{:S(2)}) collective-permute-start(f32[4,16,128]{2,1,0:T(8,128)} %get-tuple-element.22), channel_id=1, source_target_pairs={{0,2},{1,7},{2,4},{3,1},{4,6},{5,3},{6,0},{7,5},{8,10},{9,15},{10,... | collective-permute-start | bytes 98312 | tf_op jit(solution)/shard_map/ppermute | solution.py:536
  9.7 3.4 %collective-permute-start.2 = (f32[4,16,128]{2,1,0:T(8,128)}, f32[4,16,128]{2,1,0:T(8,128)S(1)}, u32[]{:S(2)}, u32[]{:S(2)}) collective-permute-start(f32[4,16,128]{2,1,0:T(8,128)} %get-tuple-element.23), channel_id=1, source_target_pairs={{0,7},{1,2},{2,1},{3,4},{4,3},{5,6},{6,5},{7,0},{8,15},{9,10},{10,... | collective-permute-start | bytes 98312 | tf_op jit(solution)/shard_map/ppermute | solution.py:537
  13.1 0.9 %collective-permute-done.1.halo_own = f32[4,16,128]{2,1,0:T(8,128)S(1)} collective-permute-done((f32[4,16,128]{2,1,0:T(8,128)}, f32[4,16,128]{2,1,0:T(8,128)S(1)}, u32[]{:S(2)}, u32[]{:S(2)}) %collective-permute-start.1) | collective-permute-done | bytes 32800 | tf_op jit(solution)/shard_map/ppermute | solution.py:536
  14.0 0.0 copy-start.9
  14.0 2.6 %collective-permute-done.2.halo_other = f32[4,16,128]{2,1,0:T(8,128)S(1)} collective-permute-done((f32[4,16,128]{2,1,0:T(8,128)}, f32[4,16,128]{2,1,0:T(8,128)S(1)}, u32[]{:S(2)}, u32[]{:S(2)}) %collective-permute-start.2) | collective-permute-done | bytes 32800 | tf_op jit(solution)/shard_map/ppermute | solution.py:537
  16.6 0.6 %collective-permute-done.other = f32[4,64,128]{2,1,0:T(8,128)S(1)} collective-permute-done((f32[4,64,128]{2,1,0:T(8,128)}, f32[4,64,128]{2,1,0:T(8,128)S(1)}, u32[]{:S(2)}, u32[]{:S(2)}) %collective-permute-start) | collective-permute-done | bytes 131104 | tf_op jit(solution)/shard_map/ppermute | solution.py:535
  17.2 0.0 copy-done.9
  17.2 0.0 copy-done.10
  17.3 0.6 %copy-done.5 = f32[4,64,128]{2,1,0:T(8,128)} copy-done((f32[4,64,128]{2,1,0:T(8,128)}, f32[4,64,128]{2,1,0:T(8,128)S(1)}, u32[]{:S(2)}) %copy-start.5) | copy-done | bytes 131096
  17.9 1.8 %shard_map.96 = (f32[4,80,256]{2,1,0:T(8,128)}, f32[2,72,256]{2,1,0:T(8,128)}, f32[2,72,256]{2,1,0:T(8,128)}) custom-call(f32[4,64,128]{2,1,0:T(8,128)} %get-tuple-element.20.own, f32[4,64,128]{2,1,0:T(8,128)} %copy-done.5, f32[4,16,128]{2,1,0:T(8,128)} %copy-done.9, f32[4,16,128]{2,1,0:T(8,128)} %copy-done.10), custom_call_target="tpu_custom_call" | custom-call | bytes 655360 | tf_op jit(solution)/shard_map/pallas_call | solution.py:220
  19.7 0.0 collective-permute-start.3
  19.7 1.8 %collective-permute-start.4 = (f32[2,72,256]{2,1,0:T(8,128)}, f32[2,72,256]{2,1,0:T(8,128)S(1)}, u32[]{:S(2)}, u32[]{:S(2)}) collective-permute-start(f32[2,72,256]{2,1,0:T(8,128)} %get-tuple-element.26), channel_id=1, source_target_pairs={{0,2},{2,0},{4,6},{6,4},{8,16},{10,18},{12,20},{14,22},{16,8},{18,... | collective-permute-start | bytes 442376 | tf_op jit(solution)/shard_map/ppermute | solution.py:542
  21.5 0.2 collective-permute-start.6
  21.7 4.8 %collective-permute-start.7 = (f32[10,16,128]{2,1,0:T(8,128)}, f32[10,16,128]{2,1,0:T(8,128)S(1)}, u32[]{:S(2)}, u32[]{:S(2)}) collective-permute-start(f32[10,16,128]{2,1,0:T(8,128)} %get-tuple-element.30), channel_id=1, source_target_pairs={{0,7},{1,2},{2,1},{3,4},{4,3},{5,6},{6,5},{7,0},{8,15},{9,10},{10,... | collective-permute-start | bytes 245768 | tf_op jit(solution)/shard_map/ppermute | solution.py:537
  27.2 1.3 %copy.10.amp = f32[2,1]{1,0:T(2,128)} copy(f32[2,1]{0,1:T(1,128)} %param.12) | data formatting | bytes 16 | tf_op args[4]
  28.5 1.3 %copy.14 = f32[1,2,16,128]{3,2,1,0:T(8,128)} copy(f32[1,2,16,128]{3,1,2,0:T(2,128)} %bitcast.13) | data formatting | bytes 32768
  29.8 3.1 %shard_map.98.added = f32[2,2,72,256]{3,2,1,0:T(8,128)} custom-call(s32[16,128]{1,0:T(8,128)} %bitcast.15, f32[2,16,128]{2,1,0:T(8,128)} %bitcast.14), custom_call_target="tpu_custom_call" | custom-call | flops 1006632960 | bytes 24576 | tf_op jit(solution)/shard_map/pallas_call | solution.py:288
  32.9 0.0 collective-permute-done.6.halo_own
  32.9 0.0 collective-permute-done.7.halo_other
  32.9 0.0 copy-start.8
  32.9 0.0 collective-permute-done.3.recv_a
  33.0 0.0 copy-start.1
  33.0 0.0 collective-permute-done.4.recv_b
  33.0 0.0 copy-start.2
  33.0 0.0 collective-permute-done.5.other
  33.0 0.0 copy-start
  33.0 0.6 %copy-done.7 = f32[10,16,128]{2,1,0:T(8,128)} copy-done((f32[10,16,128]{2,1,0:T(8,128)}, f32[10,16,128]{2,1,0:T(8,128)S(1)}, u32[]{:S(2)}) %copy-start.7) | copy-done | bytes 81944
  33.6 0.0 copy-done.8
  33.6 0.1 copy-done.1
  33.6 0.0 copy-done.2
  33.7 0.1 copy-done
  33.8 3.5 %shard_map.99 = (f32[4,72,256]{2,1,0:T(8,128)}, f32[6,64,256]{2,1,0:T(8,128)}, f32[2,64,256]{2,1,0:T(8,128)}, f32[2,64,256]{2,1,0:T(8,128)}) custom-call(f32[4,80,256]{2,1,0:T(8,128)} %get-tuple-element.24.now.before, f32[2,72,256]{2,1,0:T(8,128)} %copy-done.1, f32[2,72,256]{2,1,0:T(8,128)} %copy-done.2, f32[10,64,128]{2,1,0:T(8,128)} %get-tuple-element.27.own, ...), custom_call_target="tpu_custom_call" | custom-call | flops 4423680 | bytes 589824 | tf_op jit(solution)/shard_map/pallas_call | solution.py:390
  37.4 0.0 collective-permute-start.8
  37.4 1.1 %collective-permute-start.9 = (f32[2,64,256]{2,1,0:T(8,128)}, f32[2,64,256]{2,1,0:T(8,128)S(1)}, u32[]{:S(2)}, u32[]{:S(2)}) collective-permute-start(f32[2,64,256]{2,1,0:T(8,128)} %get-tuple-element.34), channel_id=1, source_target_pairs={{0,2},{2,0},{4,6},{6,4},{8,16},{10,18},{12,20},{14,22},{16,8},{18,... | collective-permute-start | bytes 393224 | tf_op jit(solution)/shard_map/ppermute | solution.py:542
  38.4 0.5 collective-permute-done.8.recv_a
  38.9 3.7 %collective-permute-done.9.recv_b = f32[2,64,256]{2,1,0:T(8,128)S(1)} collective-permute-done((f32[2,64,256]{2,1,0:T(8,128)}, f32[2,64,256]{2,1,0:T(8,128)S(1)}, u32[]{:S(2)}, u32[]{:S(2)}) %collective-permute-start.9) | collective-permute-done | bytes 131104 | tf_op jit(solution)/shard_map/ppermute | solution.py:542
  42.6 0.0 copy-done.3
  42.6 0.6 %copy-done.4 = f32[2,64,256]{2,1,0:T(8,128)} copy-done((f32[2,64,256]{2,1,0:T(8,128)}, f32[2,64,256]{2,1,0:T(8,128)S(1)}, u32[]{:S(2)}) %copy-start.4) | copy-done | bytes 131096
  43.2 3.2 %shard_map.100 = (f32[4,64,256]{2,1,0:T(8,128)}, f32[4,48,128]{2,1,0:T(8,128)}, f32[4,48,128]{2,1,0:T(8,128)}) custom-call(f32[4,72,256]{2,1,0:T(8,128)} %get-tuple-element.31.now.one, f32[4,80,256]{2,1,0:T(8,128)} %get-tuple-element.24.now.before, f32[6,64,256]{2,1,0:T(8,128)} %get-tuple-element.32.coeff, f32[2,64,256]{2,1,0:T(8,128)} %copy-done.3, ...), custom_call_target="tpu_custom_call" | custom-call | flops 3932160 | bytes 524288 | tf_op jit(solution)/shard_map/pallas_call | solution.py:420
  46.4 0.0 collective-permute-start.10
  46.4 2.6 %shard_map.101 = f32[17,2,48,256]{3,2,1,0:T(8,128)} custom-call(f32[4,72,256]{2,1,0:T(8,128)} %get-tuple-element.31.now.one, f32[4,64,256]{2,1,0:T(8,128)} %get-tuple-element.35.two, s32[17]{0:T(128)} %offsets.1), custom_call_target="tpu_custom_call" | custom-call | flops 1253376 | bytes 1671168 | tf_op jit(solution)/shard_map/pallas_call | solution.py:455
  49.0 2.4 %collective-permute-done.10.got = f32[4,48,128]{2,1,0:T(8,128)S(1)} collective-permute-done((f32[4,48,128]{2,1,0:T(8,128)}, f32[4,48,128]{2,1,0:T(8,128)S(1)}, u32[]{:S(2)}, u32[]{:S(2)}) %collective-permute-start.10) | collective-permute-done | bytes 98336 | tf_op jit(solution)/shard_map/ppermute | solution.py:557
  51.4 0.6 %copy-done.6 = f32[4,48,128]{2,1,0:T(8,128)} copy-done((f32[4,48,128]{2,1,0:T(8,128)}, f32[4,48,128]{2,1,0:T(8,128)S(1)}, u32[]{:S(2)}) %copy-start.6) | copy-done | bytes 98328
  52.1 1.6 %shard_map.102 = f32[4,96,128]{2,1,0:T(8,128)} custom-call(f32[4,48,128]{2,1,0:T(8,128)} %get-tuple-element.36.keep, f32[4,48,128]{2,1,0:T(8,128)} %copy-done.6), custom_call_target="tpu_custom_call" | custom-call | bytes 393216 | tf_op jit(solution)/shard_map/pallas_call | solution.py:487
  (6 shorter events, 0.0 us)
Async XLA Ops:
  2.8 30.2 %collective-permute-start.5 = (f32[10,64,128]{2,1,0:T(8,128)}, f32[10,64,128]{2,1,0:T(8,128)S(1)}, u32[]{:S(2)}, u32[]{:S(2)}) collective-permute-start(f32[10,64,128]{2,1,0:T(8,128)} %get-tuple-element.28), channel_id=1, source_target_pairs={{0,1},{1,0},{2,3},{3,2},{4,5},{5,4},{6,7},{7,6},{8,9},{9,8},{10,11... | collective-permute-start | bytes 983048 | tf_op jit(solution)/shard_map/ppermute | solution.py:535
  7.5 9.7 %collective-permute-start = (f32[4,64,128]{2,1,0:T(8,128)}, f32[4,64,128]{2,1,0:T(8,128)S(1)}, u32[]{:S(2)}, u32[]{:S(2)}) collective-permute-start(f32[4,64,128]{2,1,0:T(8,128)} %get-tuple-element.21), channel_id=1, source_target_pairs={{0,1},{1,0},{2,3},{3,2},{4,5},{5,4},{6,7},{7,6},{8,9},{9,8},{10,11... | collective-permute-start | bytes 393224 | tf_op jit(solution)/shard_map/ppermute | solution.py:535
  7.6 6.4 %collective-permute-start.1 = (f32[4,16,128]{2,1,0:T(8,128)}, f32[4,16,128]{2,1,0:T(8,128)S(1)}, u32[]{:S(2)}, u32[]{:S(2)}) collective-permute-start(f32[4,16,128]{2,1,0:T(8,128)} %get-tuple-element.22), channel_id=1, source_target_pairs={{0,2},{1,7},{2,4},{3,1},{4,6},{5,3},{6,0},{7,5},{8,10},{9,15},{10,... | collective-permute-start | bytes 98312 | tf_op jit(solution)/shard_map/ppermute | solution.py:536
  9.7 6.9 %collective-permute-start.2 = (f32[4,16,128]{2,1,0:T(8,128)}, f32[4,16,128]{2,1,0:T(8,128)S(1)}, u32[]{:S(2)}, u32[]{:S(2)}) collective-permute-start(f32[4,16,128]{2,1,0:T(8,128)} %get-tuple-element.23), channel_id=1, source_target_pairs={{0,7},{1,2},{2,1},{3,4},{4,3},{5,6},{6,5},{7,0},{8,15},{9,10},{10,... | collective-permute-start | bytes 98312 | tf_op jit(solution)/shard_map/ppermute | solution.py:537
  14.0 3.2 %copy-start.9 = (f32[4,16,128]{2,1,0:T(8,128)}, f32[4,16,128]{2,1,0:T(8,128)S(1)}, u32[]{:S(2)}) copy-start(f32[4,16,128]{2,1,0:T(8,128)S(1)} %collective-permute-done.1.halo_own) | copy-start | bytes 98308
  16.6 0.6 %copy-start.10 = (f32[4,16,128]{2,1,0:T(8,128)}, f32[4,16,128]{2,1,0:T(8,128)S(1)}, u32[]{:S(2)}) copy-start(f32[4,16,128]{2,1,0:T(8,128)S(1)} %collective-permute-done.2.halo_other) | copy-start | bytes 98308
  17.2 0.7 %copy-start.5 = (f32[4,64,128]{2,1,0:T(8,128)}, f32[4,64,128]{2,1,0:T(8,128)S(1)}, u32[]{:S(2)}) copy-start(f32[4,64,128]{2,1,0:T(8,128)S(1)} %collective-permute-done.other) | copy-start | bytes 393220
  19.7 13.2 %collective-permute-start.3 = (f32[2,72,256]{2,1,0:T(8,128)}, f32[2,72,256]{2,1,0:T(8,128)S(1)}, u32[]{:S(2)}, u32[]{:S(2)}) collective-permute-start(f32[2,72,256]{2,1,0:T(8,128)} %get-tuple-element.25), channel_id=1, source_target_pairs={{0,8},{8,0},{16,24},{24,16},{1,9},{9,1},{17,25},{25,17},{2,10},{10... | collective-permute-start | bytes 442376 | tf_op jit(solution)/shard_map/ppermute | solution.py:541
  19.7 13.3 %collective-permute-start.4 = (f32[2,72,256]{2,1,0:T(8,128)}, f32[2,72,256]{2,1,0:T(8,128)S(1)}, u32[]{:S(2)}, u32[]{:S(2)}) collective-permute-start(f32[2,72,256]{2,1,0:T(8,128)} %get-tuple-element.26), channel_id=1, source_target_pairs={{0,2},{2,0},{4,6},{6,4},{8,16},{10,18},{12,20},{14,22},{16,8},{18,... | collective-permute-start | bytes 442376 | tf_op jit(solution)/shard_map/ppermute | solution.py:542
  21.5 11.4 %collective-permute-start.6 = (f32[10,16,128]{2,1,0:T(8,128)}, f32[10,16,128]{2,1,0:T(8,128)S(1)}, u32[]{:S(2)}, u32[]{:S(2)}) collective-permute-start(f32[10,16,128]{2,1,0:T(8,128)} %get-tuple-element.29), channel_id=1, source_target_pairs={{0,2},{1,7},{2,4},{3,1},{4,6},{5,3},{6,0},{7,5},{8,10},{9,15},{10,... | collective-permute-start | bytes 245768 | tf_op jit(solution)/shard_map/ppermute | solution.py:536
  21.7 11.2 %collective-permute-start.7 = (f32[10,16,128]{2,1,0:T(8,128)}, f32[10,16,128]{2,1,0:T(8,128)S(1)}, u32[]{:S(2)}, u32[]{:S(2)}) collective-permute-start(f32[10,16,128]{2,1,0:T(8,128)} %get-tuple-element.30), channel_id=1, source_target_pairs={{0,7},{1,2},{2,1},{3,4},{4,3},{5,6},{6,5},{7,0},{8,15},{9,10},{10,... | collective-permute-start | bytes 245768 | tf_op jit(solution)/shard_map/ppermute | solution.py:537
  32.9 0.6 %copy-start.7 = (f32[10,16,128]{2,1,0:T(8,128)}, f32[10,16,128]{2,1,0:T(8,128)S(1)}, u32[]{:S(2)}) copy-start(f32[10,16,128]{2,1,0:T(8,128)S(1)} %collective-permute-done.6.halo_own) | copy-start | bytes 245764
  32.9 0.7 %copy-start.8 = (f32[10,16,128]{2,1,0:T(8,128)}, f32[10,16,128]{2,1,0:T(8,128)S(1)}, u32[]{:S(2)}) copy-start(f32[10,16,128]{2,1,0:T(8,128)S(1)} %collective-permute-done.7.halo_other) | copy-start | bytes 245764
  33.0 0.7 %copy-start.1 = (f32[2,72,256]{2,1,0:T(8,128)}, f32[2,72,256]{2,1,0:T(8,128)S(1)}, u32[]{:S(2)}) copy-start(f32[2,72,256]{2,1,0:T(8,128)S(1)} %collective-permute-done.3.recv_a) | copy-start | bytes 442372
  33.0 0.7 %copy-start.2 = (f32[2,72,256]{2,1,0:T(8,128)}, f32[2,72,256]{2,1,0:T(8,128)S(1)}, u32[]{:S(2)}) copy-start(f32[2,72,256]{2,1,0:T(8,128)S(1)} %collective-permute-done.4.recv_b) | copy-start | bytes 442372
  33.0 0.8 %copy-start = (f32[10,64,128]{2,1,0:T(8,128)}, f32[10,64,128]{2,1,0:T(8,128)S(1)}, u32[]{:S(2)}) copy-start(f32[10,64,128]{2,1,0:T(8,128)S(1)} %collective-permute-done.5.other) | copy-start | bytes 983044
  37.4 1.6 %collective-permute-start.8 = (f32[2,64,256]{2,1,0:T(8,128)}, f32[2,64,256]{2,1,0:T(8,128)S(1)}, u32[]{:S(2)}, u32[]{:S(2)}) collective-permute-start(f32[2,64,256]{2,1,0:T(8,128)} %get-tuple-element.33), channel_id=1, source_target_pairs={{0,8},{8,0},{16,24},{24,16},{1,9},{9,1},{17,25},{25,17},{2,10},{10... | collective-permute-start | bytes 393224 | tf_op jit(solution)/shard_map/ppermute | solution.py:541
  37.4 5.2 %collective-permute-start.9 = (f32[2,64,256]{2,1,0:T(8,128)}, f32[2,64,256]{2,1,0:T(8,128)S(1)}, u32[]{:S(2)}, u32[]{:S(2)}) collective-permute-start(f32[2,64,256]{2,1,0:T(8,128)} %get-tuple-element.34), channel_id=1, source_target_pairs={{0,2},{2,0},{4,6},{6,4},{8,16},{10,18},{12,20},{14,22},{16,8},{18,... | collective-permute-start | bytes 393224 | tf_op jit(solution)/shard_map/ppermute | solution.py:542
  38.9 3.7 %copy-start.3 = (f32[2,64,256]{2,1,0:T(8,128)}, f32[2,64,256]{2,1,0:T(8,128)S(1)}, u32[]{:S(2)}) copy-start(f32[2,64,256]{2,1,0:T(8,128)S(1)} %collective-permute-done.8.recv_a) | copy-start | bytes 393220
  42.6 0.6 %copy-start.4 = (f32[2,64,256]{2,1,0:T(8,128)}, f32[2,64,256]{2,1,0:T(8,128)S(1)}, u32[]{:S(2)}) copy-start(f32[2,64,256]{2,1,0:T(8,128)S(1)} %collective-permute-done.9.recv_b) | copy-start | bytes 393220
  46.4 5.0 %collective-permute-start.10 = (f32[4,48,128]{2,1,0:T(8,128)}, f32[4,48,128]{2,1,0:T(8,128)S(1)}, u32[]{:S(2)}, u32[]{:S(2)}) collective-permute-start(f32[4,48,128]{2,1,0:T(8,128)} %get-tuple-element.37), channel_id=1, source_target_pairs={{0,1},{1,0},{2,3},{3,2},{4,5},{5,4},{6,7},{7,6},{8,9},{9,8},{10,11... | collective-permute-start | bytes 294920 | tf_op jit(solution)/shard_map/ppermute | solution.py:557
  51.4 0.6 %copy-start.6 = (f32[4,48,128]{2,1,0:T(8,128)}, f32[4,48,128]{2,1,0:T(8,128)S(1)}, u32[]{:S(2)}) copy-start(f32[4,48,128]{2,1,0:T(8,128)S(1)} %collective-permute-done.10.got) | copy-start | bytes 294916

commit v2 on v1

--- a/solution.py
+++ b/solution.py
@@ -6,6 +6,7 @@
 from jax.experimental import pallas as pl
 from jax.experimental.pallas import tpu as pltpu
 from jax.sharding import PartitionSpec as P
+
 
 STEPS = 2
 NOFF = 17
@@ -99,7 +100,8 @@
 
 VMEM = pl.BlockSpec(memory_space=pltpu.VMEM)
 SMEM = pl.BlockSpec(memory_space=pltpu.SMEM)
-HBM = pl.BlockSpec(memory_space=pl.ANY)
+HBM = pl.BlockSpec(memory_space=pltpu.HBM)
+PARAMS = pltpu.CompilerParams(vmem_limit_bytes=16 << 20)
 
 
 class Plan:
@@ -183,6 +185,7 @@
         in_specs=[HBM] * len(sources),
         out_specs=(VMEM,) * 4,
         scratch_shapes=[pltpu.SemaphoreType.DMA((len(sources), 4))],
+        compiler_params=PARAMS,
         cost_estimate=cost(0, 4 * planes * p.rows * p.cols * 3),
     )(*sources)
 
@@ -226,11 +229,12 @@
         ),
         in_specs=[VMEM] * 4,
         out_specs=(VMEM,) * 3,
+        compiler_params=PARAMS,
         cost_estimate=cost(0, 8 * planes * p.e0 * p.ny),
     )(own, other, halo_own, halo_other)
 
 
-def spread_kernel(p, index, amp, out, row_hot, col_hot, total):
+def spread_kernel(p, step, index, amp, src_index, src_amp, out, row_hot, col_hot, total):
     lays, stride = p.lays, p.e0
     g = lax.axis_index("grp")
     first = p.base_row() - p.d1
@@ -242,61 +246,68 @@
     ]
     column = lax.broadcasted_iota(jnp.int32, (p.ny, 128), 0)
     for k in range(wide):
-        at = pl.ds(k * 128, 128)
+        at = slice(k * 128, (k + 1) * 128)
         flat = index[k : k + 1, :]
         row = jnp.floor((flat.astype(jnp.float32) + 0.5) * (1.0 / p.ny)).astype(jnp.int32)
         col = flat - row * p.ny
         col_hot[:, at] = jnp.where(column == col, 1.0, 0.0).astype(jnp.bfloat16)
-        for step in range(STEPS):
-            rest = amp[step, k : k + 1, :]
-            parts = []
-            for _ in range(3):
-                part = rest.astype(jnp.bfloat16).astype(jnp.float32)
-                parts.append(part)
-                rest = rest - part
-            for lay in range(lays):
-                hit = wanted[lay] == row
-                for i, part in enumerate(parts):
-                    start = ((step * 3 + i) * lays + lay) * stride
-                    row_hot[start : start + stride, at] = jnp.where(
-                        hit, part, 0.0
-                    ).astype(jnp.bfloat16)
+        rest = amp[step : step + 1, at]
+        parts = []
+        for _ in range(3):
+            part = rest.astype(jnp.bfloat16).astype(jnp.float32)
+            parts.append(part)
+            rest = rest - part
+        for lay in range(lays):
+            hit = wanted[lay] == row
+            for i, part in enumerate(parts):
+                start = (i * lays + lay) * stride
+                row_hot[start : start + stride, at] = jnp.where(hit, part, 0.0).astype(
+                    jnp.bfloat16
+                )
     total[...] = lax.dot_general(
         row_hot[...],
         col_hot[...],
         (((1,), (1,)), ((), ())),
         preferred_element_type=jnp.float32,
     )
-    for step in range(STEPS):
-        for lay in range(lays):
-            rows = [((step * 3 + i) * lays + lay) * stride for i in range(3)]
-            out[step, lay] = (
-                total[rows[0] : rows[0] + p.e1]
-                + total[rows[1] : rows[1] + p.e1]
-                + total[rows[2] : rows[2] + p.e1]
-            )
-
-
-def spread(p, index, amp):
-    count = index.shape[0]
-    wide = -(-count // 128)
-    extra = wide * 128 - count
-    if extra:
-        index = jnp.pad(index, (0, extra))
-        amp = jnp.pad(amp, ((0, 0), (0, extra)))
-    tall = STEPS * 3 * p.lays * p.e0
-    return pl.pallas_call(
-        functools.partial(spread_kernel, p),
-        out_shape=f32(STEPS, p.lays, p.e1, p.ny),
-        in_specs=[VMEM] * 2,
+    for lay in range(lays):
+        rows = [(i * lays + lay) * stride for i in range(3)]
+        out[1, lay] = (
+            total[rows[0] : rows[0] + p.e1]
+            + total[rows[1] : rows[1] + p.e1]
+            + total[rows[2] : rows[2] + p.e1]
+        )
+    out[0] = jnp.zeros((lays, p.e1, p.ny), jnp.float32)
+    for s in range(src_index.shape[0]):
+        flat = src_index[s]
+        line = lax.div(flat, p.ny)
+        lay = lax.div(line, p.nx) - g * lays
+        row = lax.rem(line, p.nx) - first
+        col = lax.rem(flat, p.ny)
+
+        @pl.when((lay >= 0) & (lay < lays) & (row >= 0) & (row < p.e1))
+        def _():
+            spot = lax.broadcasted_iota(jnp.int32, (1, p.ny), 1) == col
+            amount = src_amp[step * src_index.shape[0] + s]
+            out[0, lay, pl.ds(row, 1), :] += jnp.where(spot, amount, 0.0)
+
+
+def spread(p, step, index, amp, src_index, src_amp):
+    wide = index.shape[0]
+    tall = 3 * p.lays * p.e0
+    return pl.pallas_call(
+        functools.partial(spread_kernel, p, step),
+        out_shape=f32(p.fields, p.lays, p.e1, p.ny),
+        in_specs=[VMEM] * 2 + [SMEM] * 2,
         out_specs=VMEM,
         scratch_shapes=[
             pltpu.VMEM((tall, wide * 128), jnp.bfloat16),
             pltpu.VMEM((p.ny, wide * 128), jnp.bfloat16),
             pltpu.VMEM((tall, p.ny), jnp.float32),
         ],
+        compiler_params=PARAMS,
         cost_estimate=cost(2 * tall * wide * 128 * p.ny, 4 * wide * 128 * 3),
-    )(index.reshape(wide, 128), amp.reshape(STEPS, wide, 128))
+    )(index, amp, src_index, src_amp)
 
 
 def advance(p, now, before, before_at, coeff, coeff_at, recv_a, recv_b, added, added_at, out, margin):
@@ -346,32 +357,14 @@
                     - before[plane, before_at + r : before_at + r + 8, :]
                     + (w[0] * dxx + w[1] * dyy + w[2] * dzz)
                 )
-                if f == 1:
-                    new = new + added[lay, added_at + r : added_at + r + 8, :]
+                new = new + added[f, lay, added_at + r : added_at + r + 8, :]
                 if edge:
                     new = jnp.where(known, new, 0.0)
                 out[plane, rows, :] = new
 
 
-def add_source(p, step, index, amp, out, margin):
-    g = lax.axis_index("grp")
-    first = p.base_row() - margin
-    count = p.half + 2 * margin
-    for s in range(index.shape[0]):
-        flat = index[s]
-        line = lax.div(flat, p.ny)
-        lay = lax.div(line, p.nx) - g * p.lays
-        row = lax.rem(line, p.nx) - first
-        col = lax.rem(flat, p.ny)
-
-        @pl.when((lay >= 0) & (lay < p.lays) & (row >= 0) & (row < count))
-        def _():
-            spot = lax.broadcasted_iota(jnp.int32, (1, p.ny), 1) == col
-            out[lay, pl.ds(row, 1), :] += jnp.where(spot, amp[step, s], 0.0)
-
-
 def first_kernel(
-    p, now, recv_a, recv_b, own, other, halo_own, halo_other, added, index, amp,
+    p, now, recv_a, recv_b, own, other, halo_own, halo_other, added,
     out, coeff_out, send_a, send_b, rest,
 ):
     lay_out(p, rest, own, other, halo_own, halo_other)
@@ -379,13 +372,12 @@
     gap = p.d0 - p.d1
     coeff_out[...] = rest[planes:, p.d0 - p.d2 : p.d0 - p.d2 + p.e2, :]
     advance(
-        p, now, rest, gap, rest.at[planes:], gap, recv_a, recv_b, added.at[0], 0, out, p.d1
+        p, now, rest, gap, rest.at[planes:], gap, recv_a, recv_b, added, 0, out, p.d1
     )
-    add_source(p, 0, index, amp, out, p.d1)
     send_layers(p, out, send_a, send_b, p.d1 - p.d2, p.e2)
 
 
-def first_step(p, now, recv_a, recv_b, rest, added, index, amp):
+def first_step(p, now, recv_a, recv_b, rest, added):
     planes = p.fields * p.lays
     return pl.pallas_call(
         functools.partial(first_kernel, p),
@@ -395,19 +387,19 @@
             f32(p.fields, p.e2, p.ny),
             f32(p.fields, p.e2, p.ny),
         ),
-        in_specs=[VMEM] * 8 + [SMEM] * 2,
+        in_specs=[VMEM] * 8,
         out_specs=(VMEM,) * 4,
         scratch_shapes=[pltpu.VMEM((planes + 3 * p.lays, p.e0, p.ny), jnp.float32)],
+        compiler_params=PARAMS,
         cost_estimate=cost(60 * planes * p.e1 * p.ny, 8 * planes * p.e1 * p.ny),
-    )(now, recv_a, recv_b, *rest, added, index, amp)
-
-
-def second_kernel(p, now, before, coeff, recv_a, recv_b, added, index, amp, out, keep, give):
+    )(now, recv_a, recv_b, *rest, added)
+
+
+def second_kernel(p, now, before, coeff, recv_a, recv_b, added, out, keep, give):
     gap = p.d1 - p.d2
     advance(
-        p, now, before, p.d0 - p.d2, coeff, 0, recv_a, recv_b, added.at[1], gap, out, p.d2
+        p, now, before, p.d0 - p.d2, coeff, 0, recv_a, recv_b, added, gap, out, p.d2
     )
-    add_source(p, 1, index, amp, out, p.d2)
     b = lax.axis_index("gy")
     mine = pl.ds(pl.multiple_of(b * p.cols, p.cols), p.cols)
     theirs = pl.ds(pl.multiple_of((1 - b) * p.cols, p.cols), p.cols)
@@ -415,7 +407,7 @@
     give[...] = out[:, p.d2 : p.d2 + p.half, theirs]
 
 
-def second_step(p, now, before, coeff, recv_a, recv_b, added, index, amp):
+def second_step(p, now, before, coeff, recv_a, recv_b, added):
     planes = p.fields * p.lays
     return pl.pallas_call(
         functools.partial(second_kernel, p),
@@ -424,10 +416,11 @@
             f32(planes, p.half, p.cols),
             f32(planes, p.half, p.cols),
         ),
-        in_specs=[VMEM] * 6 + [SMEM] * 2,
+        in_specs=[VMEM] * 6,
         out_specs=(VMEM,) * 3,
+        compiler_params=PARAMS,
         cost_estimate=cost(60 * planes * p.e2 * p.ny, 8 * planes * p.e2 * p.ny),
-    )(now, before, coeff, recv_a, recv_b, added, index, amp)
+    )(now, before, coeff, recv_a, recv_b, added)
 
 
 def image_kernel(p, one, two, offsets, out, held, place, sems):
@@ -462,6 +455,7 @@
             pltpu.SMEM((NOFF,), jnp.int32),
             pltpu.SemaphoreType.DMA((NOFF,)),
         ],
+        compiler_params=PARAMS,
         cost_estimate=cost(3 * size, 4 * size),
     )(one, two, offsets)
 
@@ -490,6 +484,7 @@
         in_specs=[VMEM] * 2,
         out_specs=HBM,
         scratch_shapes=[pltpu.SemaphoreType.DMA((2,))],
+        compiler_params=PARAMS,
         cost_estimate=cost(0, 8 * planes * p.rows * p.cols),
     )(keep, got)
 
@@ -508,22 +503,32 @@
     return pairs
 
 
-def halo_straight(p):
-    pairs = []
-    for a in range(p.n_gx):
-        for b in range(2):
-            to = (a + 1 if b == 0 else a - 1) % p.n_gx
-            pairs.append((a * 2 + b, to * 2 + b))
-    return pairs
-
-
-def halo_across(p):
-    pairs = []
-    for a in range(p.n_gx):
-        for b in range(2):
-            to = (a - 1 if b == 0 else a + 1) % p.n_gx
-            pairs.append((a * 2 + b, to * 2 + 1 - b))
-    return pairs
+def halo_pairs(p, across):
+    size = (p.n_grp, p.n_gx, p.n_gy)
+
+    def flat(place):
+        return (place[0] * size[1] + place[1]) * size[2] + place[2]
+
+    goals = {}
+    for g in range(p.n_grp):
+        for a in range(p.n_gx):
+            for b in range(p.n_gy):
+                down = (b == 0) != across
+                goal = (g, a + 1 if down else a - 1, 1 - b if across else b)
+                if 0 <= goal[1] < p.n_gx:
+                    goals[(g, a, b)] = goal
+    taken = set(goals.values())
+    for g in range(p.n_grp):
+        for a in range(p.n_gx):
+            for b in range(p.n_gy):
+                if (g, a, b) not in goals:
+                    near = (g ^ 1, a, b) if across else (g, a, 1 - b)
+                    assert near not in taken
+                    goals[(g, a, b)] = near
+    return [(flat(k), flat(v)) for k, v in goals.items()]
+
+
+AXES = ("grp", "gx", "gy")
 
 
 def body_rows(p, previous, current, coeff, src_index, src_amp, rec_index, rec_amp, offsets):
@@ -533,8 +538,8 @@
     def redistribute(*sources):
         own, give, edge, corner = pack(p, *sources)
         other = lax.ppermute(give, "gy", [(0, 1), (1, 0)])
-        halo_own = lax.ppermute(edge, ("gx", "gy"), halo_straight(p))
-        halo_other = lax.ppermute(corner, ("gx", "gy"), halo_across(p))
+        halo_own = lax.ppermute(edge, AXES, halo_pairs(p, False))
+        halo_other = lax.ppermute(corner, AXES, halo_pairs(p, True))
         return own, other, halo_own, halo_other
 
     def swap_layers(send_a, send_b):
@@ -542,18 +547,23 @@
         recv_b = lax.ppermute(send_b, ("grp", "gx"), pairs_between(p))
         return recv_a, recv_b
 
+    count = rec_index.shape[0]
+    wide = -(-count // 128)
+    if wide * 128 > count:
+        rec_index = jnp.pad(rec_index, (0, wide * 128 - count))
+        rec_amp = jnp.pad(rec_amp, ((0, 0), (0, wide * 128 - count)))
+    points = (rec_index.reshape(wide, 128), rec_amp, src_index, src_amp.reshape(-1))
+
     now = redistribute(current.reshape(planes, *tile))
     rest = redistribute(previous.reshape(planes, *tile), coeff.reshape(3 * p.lays, *tile))
-    added = spread(p, rec_index, rec_amp)
+    added = []
+    for step in range(STEPS):
+        added.append(spread(p, step, *points))
     whole, send_a, send_b = join(p, *now)
     recv_a, recv_b = swap_layers(send_a, send_b)
-    one, weights, send_a, send_b = first_step(
-        p, whole, recv_a, recv_b, rest, added, src_index, src_amp
-    )
+    one, weights, send_a, send_b = first_step(p, whole, recv_a, recv_b, rest, added[0])
     recv_a, recv_b = swap_layers(send_a, send_b)
-    two, keep, give = second_step(
-        p, one, whole, weights, recv_a, recv_b, added, src_index, src_amp
-    )
+    two, keep, give = second_step(p, one, whole, weights, recv_a, recv_b, added[1])
     got = lax.ppermute(give, "gy", [(0, 1), (1, 0)])
     images = correlate_rows(p, one, two, offsets)
     advanced = settle(p, keep, got)
@@ -561,9 +571,11 @@
 
 
 def solution(mesh):
+    planned = mesh.shape["gy"] == 2 and mesh.shape["grp"] % 2 == 0 and mesh.shape["gx"] % 2 == 0
+
     def body(previous, *others):
         p = Plan(previous.shape, mesh.shape)
-        if p.fits():
+        if planned and p.fits():
             return body_rows(p, previous, *others)
         return body_tiles(previous, *others)
 

time: 54.1 us -> 39.8 us (0.74)
  Pallas kernels: 19.8 us -> 8.99 us
  starting transfers between devices: 16.5 us -> 14 us
    ppermute x4, starting transfers between devices: 10.5 us -> 3.45 us  [the longest x2 2.3 us: redistribute(): halo_own = lax.ppermute(edge, AXES, halo_pairs(p, False))]
    ppermute x4, waiting for transfers between devices: 3.52 us -> 7.98 us  [the longest x2 7.97 us: redistribute(): halo_own = lax.ppermute(edge, AXES, halo_pairs(p, False))]
    pallas_call x2, Pallas kernels: 3.87 us -> 0.42 us  [pack(): pl.pallas_call(functools.partial(pack_kernel, p, len(sources)), out_shape...]
    ppermute x1, starting transfers between devices: 0.01 us -> 2.69 us  [body_rows(): got = lax.ppermute(give, 'gy', [(0, 1), (1, 0)])]
    ppermute x2, waiting for transfers between devices: 3.67 us -> 1.21 us  [swap_layers(): recv_b = lax.ppermute(send_b, ('grp', 'gx'), pairs_between(p))]
    pallas_call x1, Pallas kernels: 3.55 us -> 1.24 us  [first_step(): pl.pallas_call(functools.partial(first_kernel, p), out_shape=(f32(planes,...]
    pallas_call x1, Pallas kernels: 3.18 us -> 1.04 us  [second_step(): pl.pallas_call(functools.partial(second_kernel, p), out_shape=(f32(planes...]
    pallas_call x1, Pallas kernels: 1.81 us -> 0.06 us  [join(): pl.pallas_call(functools.partial(join_kernel, p), out_shape=(f32(planes,...]
  transfers between devices with their start and end apart: 11 -> 11, of which waited for: 6 -> 3; matrix products, arithmetic and copies ran while one was open for 5% -> 0% of each run, Pallas kernels for 17% -> 15%
where the time goes in v2:
time: 39.8 us; the launch traced here: 39.5 us
  starting transfers between devices  14 us (35%)
  waiting for transfers between devices  10.2 us (26%)
  Pallas kernels  8.99 us (23%)
  local copies, waits for them, and re-layouts  4.88 us (12%)
  between operations  1.43 us (4%)
    ppermute x2, waiting for transfers between devices, redistribute(): halo_own = lax.ppermute(edge, AXES, halo_pairs(p, False))  7.97 us
    unnamed x14, local copies, waits for them, and re-layouts  4.88 us
    ppermute x2, starting transfers between devices, swap_layers(): recv_b = lax.ppermute(send_b, ('grp', 'gx'), pairs_between(p))  4.59 us
    pallas_call x2, Pallas kernels, spread(): pl.pallas_call(functools.partial(spread_kernel, p, step), out_shape=f32(p...  3.45 us
    ppermute x2, starting transfers between devices, redistribute(): other = lax.ppermute(give, 'gy', [(0, 1), (1, 0)])  3.11 us
    ppermute x1, starting transfers between devices, body_rows(): got = lax.ppermute(give, 'gy', [(0, 1), (1, 0)])  2.69 us
    ppermute x2, starting transfers between devices, redistribute(): halo_own = lax.ppermute(edge, AXES, halo_pairs(p, False))  2.3 us
    pallas_call x1, Pallas kernels, correlate_rows(): pl.pallas_call(functools.partial(image_kernel, p), out_shape=f32(NOFF, p....  2.09 us
  transfers between devices with their start and end apart: 11, of which 3 were waited for; matrix products, arithmetic and copies ran while one was open for 0% of the time, Pallas kernels for 15%

profile of v2, /device:TPU:0, one launch (start us, length us, event | category | flops | bytes accessed | tf_op | source)
XLA Modules:
  0.0 39.5 jit_solution(11060546296988484293)
XLA Ops:
  0.6 0.0 copy-start
  0.6 1.0 %copy-done = f32[3,2,96,128]{3,2,1,0:T(8,128)S(1)} copy-done((f32[3,2,96,128]{3,2,1,0:T(8,128)S(1)}, f32[3,2,96,128]{3,2,1,0:T(8,128)}, u32[]{:S(2)}) %copy-start) | copy-done | bytes 294936
  1.6 0.0 copy-start.2
  1.6 0.9 %copy-done.2 = f32[2,2,96,128]{3,2,1,0:T(8,128)S(1)} copy-done((f32[2,2,96,128]{3,2,1,0:T(8,128)S(1)}, f32[2,2,96,128]{3,2,1,0:T(8,128)}, u32[]{:S(2)}) %copy-start.2) | copy-done | bytes 196632
  2.5 0.3 shard_map.97
  2.8 3.0 %collective-permute-start.5 = (f32[10,64,128]{2,1,0:T(8,128)S(1)}, f32[10,64,128]{2,1,0:T(8,128)S(1)}, u32[]{:S(2)}, u32[]{:S(2)}) collective-permute-start(f32[10,64,128]{2,1,0:T(8,128)S(1)} %get-tuple-element.28), channel_id=1, source_target_pairs={{0,1},{1,0},{2,3},{3,2},{4,5},{5,4},{6,7},{7,6},{8,9},{9,8},{10,11... | collective-permute-start | bytes 983048 | tf_op jit(solution)/shard_map/ppermute | solution.py:540
  5.8 0.0 copy-start.1
  5.8 0.9 %copy-done.1 = f32[2,2,96,128]{3,2,1,0:T(8,128)S(1)} copy-done((f32[2,2,96,128]{3,2,1,0:T(8,128)S(1)}, f32[2,2,96,128]{3,2,1,0:T(8,128)}, u32[]{:S(2)}) %copy-start.1) | copy-done | bytes 196632
  6.8 0.1 shard_map.95
  6.9 0.1 collective-permute-start
  7.0 2.1 %collective-permute-start.1 = (f32[4,16,128]{2,1,0:T(8,128)S(1)}, f32[4,16,128]{2,1,0:T(8,128)S(1)}, u32[]{:S(2)}, u32[]{:S(2)}) collective-permute-start(f32[4,16,128]{2,1,0:T(8,128)S(1)} %get-tuple-element.22), channel_id=1, source_target_pairs={{0,2},{2,4},{3,1},{4,6},{5,3},{7,5},{8,10},{10,12},{11,9},{12,14},... | collective-permute-start | bytes 98312 | tf_op jit(solution)/shard_map/ppermute | solution.py:541
  9.1 0.0 collective-permute-start.2
  9.1 8.0 %collective-permute-done.1.halo_own = f32[4,16,128]{2,1,0:T(8,128)S(1)} collective-permute-done((f32[4,16,128]{2,1,0:T(8,128)S(1)}, f32[4,16,128]{2,1,0:T(8,128)S(1)}, u32[]{:S(2)}, u32[]{:S(2)}) %collective-permute-start.1) | collective-permute-done | bytes 32800 | tf_op jit(solution)/shard_map/ppermute | solution.py:541
  17.1 0.0 collective-permute-done.2.halo_other
  17.1 0.0 collective-permute-done.other
  17.1 0.1 shard_map.96
  17.1 0.1 collective-permute-start.3
  17.2 1.9 %collective-permute-start.4 = (f32[2,72,256]{2,1,0:T(8,128)S(1)}, f32[2,72,256]{2,1,0:T(8,128)S(1)}, u32[]{:S(2)}, u32[]{:S(2)}) collective-permute-start(f32[2,72,256]{2,1,0:T(8,128)S(1)} %get-tuple-element.26), channel_id=1, source_target_pairs={{0,2},{2,0},{4,6},{6,4},{8,16},{10,18},{12,20},{14,22},{16,8},{18,... | collective-permute-start | bytes 442376 | tf_op jit(solution)/shard_map/ppermute | solution.py:547
  19.1 0.2 collective-permute-start.6
  19.3 1.1 %collective-permute-start.7 = (f32[10,16,128]{2,1,0:T(8,128)S(1)}, f32[10,16,128]{2,1,0:T(8,128)S(1)}, u32[]{:S(2)}, u32[]{:S(2)}) collective-permute-start(f32[10,16,128]{2,1,0:T(8,128)S(1)} %get-tuple-element.30), channel_id=1, source_target_pairs={{1,2},{2,1},{3,4},{4,3},{5,6},{6,5},{9,10},{10,9},{11,12},{12,11},... | collective-permute-start | bytes 245768 | tf_op jit(solution)/shard_map/ppermute | solution.py:542
  21.1 0.0 copy-start.4
  21.1 0.7 %copy-done.4 = f32[2,2048]{1,0:T(2,128)S(1)} copy-done((f32[2,2048]{1,0:T(2,128)S(1)}, f32[2,2048]{1,0:T(2,128)}, u32[]{:S(2)}) %copy-start.4) | copy-done | bytes 16408
  21.8 0.0 copy-start.5
  21.8 0.7 %copy-done.5 = s32[2048]{0:T(1024)S(1)} copy-done((s32[2048]{0:T(1024)S(1)}, s32[2048]{0:T(1024)}, u32[]{:S(2)}) %copy-start.5) | copy-done | bytes 8216
  22.5 0.0 copy-start.6
  22.5 0.7 %copy-done.6 = f32[2,1]{0,1:T(1,128)S(1)} copy-done((f32[2,1]{0,1:T(1,128)S(1)}, f32[2,1]{0,1:T(1,128)}, u32[]{:S(2)}) %copy-start.6) | copy-done | bytes 32
  23.2 1.7 %shard_map.98.added = f32[2,2,72,256]{3,2,1,0:T(8,128)S(1)} custom-call(s32[16,128]{1,0:T(8,128)S(1)} %bitcast.9, f32[2,2048]{1,0:T(2,128)S(1)} %copy-done.4, s32[1]{0:T(128)S(6)} %copy.10.src_index, f32[2]{0:T(128)S(1)} %bitcast.11), custom_call_target="tpu_custom_call" | custom-call | flops 503316480 | bytes 24576 | tf_op jit(solution)/shard_map/pallas_call | solution.py:298
  24.9 0.0 collective-permute-done.6.halo_own
  24.9 0.0 collective-permute-done.7.halo_other
  24.9 0.0 collective-permute-done.3.recv_a
  25.0 0.0 collective-permute-done.4.recv_b
  25.0 0.0 collective-permute-done.5.other
  25.0 1.2 %shard_map.99 = (f32[4,72,256]{2,1,0:T(8,128)S(1)}, f32[6,64,256]{2,1,0:T(8,128)S(1)}, f32[2,64,256]{2,1,0:T(8,128)S(1)}, f32[2,64,256]{2,1,0:T(8,128)S(1)}) custom-call(f32[4,80,256]{2,1,0:T(8,128)S(1)} %get-tuple-element.24.now.before, f32[2,72,256]{2,1,0:T(8,128)S(1)} %collective-permute-done.3.recv_a, f32[2,72,256]{2,1,0:T(8,128)S(1)} %collective-permute-done.4.recv_b, ...), custom_call_target="tpu_custom_call" | custom-call | flops 4423680 | bytes 589824 | tf_op jit(solution)/shard_map/pallas_call | solution.py:382
  26.2 0.1 collective-permute-start.8
  26.3 0.0 copy-start.3
  26.3 2.7 %collective-permute-start.9 = (f32[2,64,256]{2,1,0:T(8,128)S(1)}, f32[2,64,256]{2,1,0:T(8,128)S(1)}, u32[]{:S(2)}, u32[]{:S(2)}) collective-permute-start(f32[2,64,256]{2,1,0:T(8,128)S(1)} %get-tuple-element.34), channel_id=1, source_target_pairs={{0,2},{2,0},{4,6},{6,4},{8,16},{10,18},{12,20},{14,22},{16,8},{18,... | collective-permute-start | bytes 393224 | tf_op jit(solution)/shard_map/ppermute | solution.py:547
  29.0 1.7 %shard_map.100.added = f32[2,2,72,256]{3,2,1,0:T(8,128)S(1)} custom-call(s32[16,128]{1,0:T(8,128)S(1)} %bitcast.10, f32[2,2048]{1,0:T(2,128)S(1)} %copy-done.4, s32[1]{0:T(128)S(6)} %copy.10.src_index, f32[2]{0:T(128)S(1)} %bitcast.12), custom_call_target="tpu_custom_call" | custom-call | flops 503316480 | bytes 24576 | tf_op jit(solution)/shard_map/pallas_call | solution.py:298
  30.7 0.0 collective-permute-done.8.recv_a
  30.8 1.2 %collective-permute-done.9.recv_b = f32[2,64,256]{2,1,0:T(8,128)S(1)} collective-permute-done((f32[2,64,256]{2,1,0:T(8,128)S(1)}, f32[2,64,256]{2,1,0:T(8,128)S(1)}, u32[]{:S(2)}, u32[]{:S(2)}) %collective-permute-start.9) | collective-permute-done | bytes 131104 | tf_op jit(solution)/shard_map/ppermute | solution.py:547
  32.0 1.0 %shard_map.101 = (f32[4,64,256]{2,1,0:T(8,128)S(1)}, f32[4,48,128]{2,1,0:T(8,128)S(1)}, f32[4,48,128]{2,1,0:T(8,128)S(1)}) custom-call(f32[4,72,256]{2,1,0:T(8,128)S(1)} %get-tuple-element.31.now.one, f32[4,80,256]{2,1,0:T(8,128)S(1)} %get-tuple-element.24.now.before, f32[6,64,256]{2,1,0:T(8,128)S(1)} %get-tuple-element.32.coeff, ...), custom_call_target="tpu_custom_call" | custom-call | flops 3932160 | bytes 524288 | tf_op jit(solution)/shard_map/pallas_call | solution.py:412
  33.0 2.7 %collective-permute-start.10 = (f32[4,48,128]{2,1,0:T(8,128)S(1)}, f32[4,48,128]{2,1,0:T(8,128)S(1)}, u32[]{:S(2)}, u32[]{:S(2)}) collective-permute-start(f32[4,48,128]{2,1,0:T(8,128)S(1)} %get-tuple-element.37), channel_id=1, source_target_pairs={{0,1},{1,0},{2,3},{3,2},{4,5},{5,4},{6,7},{7,6},{8,9},{9,8},{10,11... | collective-permute-start | bytes 294920 | tf_op jit(solution)/shard_map/ppermute | solution.py:567
  35.7 0.0 copy-done.3
  35.7 2.1 %shard_map.102 = f32[17,2,48,256]{3,2,1,0:T(8,128)} custom-call(f32[4,72,256]{2,1,0:T(8,128)S(1)} %get-tuple-element.31.now.one, f32[4,64,256]{2,1,0:T(8,128)S(1)} %get-tuple-element.35.two, s32[17]{0:T(128)S(1)} %copy-done.3), custom_call_target="tpu_custom_call" | custom-call | flops 1253376 | bytes 1671168 | tf_op jit(solution)/shard_map/pallas_call | solution.py:448
  37.8 1.0 %collective-permute-done.10.got = f32[4,48,128]{2,1,0:T(8,128)S(1)} collective-permute-done((f32[4,48,128]{2,1,0:T(8,128)S(1)}, f32[4,48,128]{2,1,0:T(8,128)S(1)}, u32[]{:S(2)}, u32[]{:S(2)}) %collective-permute-start.10) | collective-permute-done | bytes 98336 | tf_op jit(solution)/shard_map/ppermute | solution.py:567
  38.8 0.7 %shard_map.103 = f32[4,96,128]{2,1,0:T(8,128)} custom-call(f32[4,48,128]{2,1,0:T(8,128)S(1)} %get-tuple-element.36.keep, f32[4,48,128]{2,1,0:T(8,128)S(1)} %collective-permute-done.10.got), custom_call_target="tpu_custom_call" | custom-call | bytes 393216 | tf_op jit(solution)/shard_map/pallas_call | solution.py:481
Async XLA Ops:
  0.6 1.0 %copy-start = (f32[3,2,96,128]{3,2,1,0:T(8,128)S(1)}, f32[3,2,96,128]{3,2,1,0:T(8,128)}, u32[]{:S(2)}) copy-start(f32[3,2,96,128]{3,2,1,0:T(8,128)} %param.10) | copy-start | bytes 884740
  1.6 0.9 %copy-start.2 = (f32[2,2,96,128]{3,2,1,0:T(8,128)S(1)}, f32[2,2,96,128]{3,2,1,0:T(8,128)}, u32[]{:S(2)}) copy-start(f32[2,2,96,128]{3,2,1,0:T(8,128)} %param.8) | copy-start | bytes 589828
  2.8 22.1 %collective-permute-start.5 = (f32[10,64,128]{2,1,0:T(8,128)S(1)}, f32[10,64,128]{2,1,0:T(8,128)S(1)}, u32[]{:S(2)}, u32[]{:S(2)}) collective-permute-start(f32[10,64,128]{2,1,0:T(8,128)S(1)} %get-tuple-element.28), channel_id=1, source_target_pairs={{0,1},{1,0},{2,3},{3,2},{4,5},{5,4},{6,7},{7,6},{8,9},{9,8},{10,11... | collective-permute-start | bytes 983048 | tf_op jit(solution)/shard_map/ppermute | solution.py:540
  5.8 0.9 %copy-start.1 = (f32[2,2,96,128]{3,2,1,0:T(8,128)S(1)}, f32[2,2,96,128]{3,2,1,0:T(8,128)}, u32[]{:S(2)}) copy-start(f32[2,2,96,128]{3,2,1,0:T(8,128)} %param.9) | copy-start | bytes 589828
  6.9 10.2 %collective-permute-start = (f32[4,64,128]{2,1,0:T(8,128)S(1)}, f32[4,64,128]{2,1,0:T(8,128)S(1)}, u32[]{:S(2)}, u32[]{:S(2)}) collective-permute-start(f32[4,64,128]{2,1,0:T(8,128)S(1)} %get-tuple-element.21), channel_id=1, source_target_pairs={{0,1},{1,0},{2,3},{3,2},{4,5},{5,4},{6,7},{7,6},{8,9},{9,8},{10,11... | collective-permute-start | bytes 393224 | tf_op jit(solution)/shard_map/ppermute | solution.py:540
  7.0 10.1 %collective-permute-start.1 = (f32[4,16,128]{2,1,0:T(8,128)S(1)}, f32[4,16,128]{2,1,0:T(8,128)S(1)}, u32[]{:S(2)}, u32[]{:S(2)}) collective-permute-start(f32[4,16,128]{2,1,0:T(8,128)S(1)} %get-tuple-element.22), channel_id=1, source_target_pairs={{0,2},{2,4},{3,1},{4,6},{5,3},{7,5},{8,10},{10,12},{11,9},{12,14},... | collective-permute-start | bytes 98312 | tf_op jit(solution)/shard_map/ppermute | solution.py:541
  9.1 8.0 %collective-permute-start.2 = (f32[4,16,128]{2,1,0:T(8,128)S(1)}, f32[4,16,128]{2,1,0:T(8,128)S(1)}, u32[]{:S(2)}, u32[]{:S(2)}) collective-permute-start(f32[4,16,128]{2,1,0:T(8,128)S(1)} %get-tuple-element.23), channel_id=1, source_target_pairs={{1,2},{2,1},{3,4},{4,3},{5,6},{6,5},{9,10},{10,9},{11,12},{12,11},... | collective-permute-start | bytes 98312 | tf_op jit(solution)/shard_map/ppermute | solution.py:542
  17.1 7.8 %collective-permute-start.3 = (f32[2,72,256]{2,1,0:T(8,128)S(1)}, f32[2,72,256]{2,1,0:T(8,128)S(1)}, u32[]{:S(2)}, u32[]{:S(2)}) collective-permute-start(f32[2,72,256]{2,1,0:T(8,128)S(1)} %get-tuple-element.25), channel_id=1, source_target_pairs={{0,8},{8,0},{16,24},{24,16},{1,9},{9,1},{17,25},{25,17},{2,10},{10... | collective-permute-start | bytes 442376 | tf_op jit(solution)/shard_map/ppermute | solution.py:546
  17.2 7.7 %collective-permute-start.4 = (f32[2,72,256]{2,1,0:T(8,128)S(1)}, f32[2,72,256]{2,1,0:T(8,128)S(1)}, u32[]{:S(2)}, u32[]{:S(2)}) collective-permute-start(f32[2,72,256]{2,1,0:T(8,128)S(1)} %get-tuple-element.26), channel_id=1, source_target_pairs={{0,2},{2,0},{4,6},{6,4},{8,16},{10,18},{12,20},{14,22},{16,8},{18,... | collective-permute-start | bytes 442376 | tf_op jit(solution)/shard_map/ppermute | solution.py:547
  19.1 5.8 %collective-permute-start.6 = (f32[10,16,128]{2,1,0:T(8,128)S(1)}, f32[10,16,128]{2,1,0:T(8,128)S(1)}, u32[]{:S(2)}, u32[]{:S(2)}) collective-permute-start(f32[10,16,128]{2,1,0:T(8,128)S(1)} %get-tuple-element.29), channel_id=1, source_target_pairs={{0,2},{2,4},{3,1},{4,6},{5,3},{7,5},{8,10},{10,12},{11,9},{12,14},... | collective-permute-start | bytes 245768 | tf_op jit(solution)/shard_map/ppermute | solution.py:541
  19.3 5.6 %collective-permute-start.7 = (f32[10,16,128]{2,1,0:T(8,128)S(1)}, f32[10,16,128]{2,1,0:T(8,128)S(1)}, u32[]{:S(2)}, u32[]{:S(2)}) collective-permute-start(f32[10,16,128]{2,1,0:T(8,128)S(1)} %get-tuple-element.30), channel_id=1, source_target_pairs={{1,2},{2,1},{3,4},{4,3},{5,6},{6,5},{9,10},{10,9},{11,12},{12,11},... | collective-permute-start | bytes 245768 | tf_op jit(solution)/shard_map/ppermute | solution.py:542
  21.1 0.7 %copy-start.4 = (f32[2,2048]{1,0:T(2,128)S(1)}, f32[2,2048]{1,0:T(2,128)}, u32[]{:S(2)}) copy-start(f32[2,2048]{1,0:T(2,128)} %amp.3) | copy-start | bytes 49156
  21.8 0.7 %copy-start.5 = (s32[2048]{0:T(1024)S(1)}, s32[2048]{0:T(1024)}, u32[]{:S(2)}) copy-start(s32[2048]{0:T(1024)} %param.13) | copy-start | bytes 24580
  22.5 0.7 %copy-start.6 = (f32[2,1]{0,1:T(1,128)S(1)}, f32[2,1]{0,1:T(1,128)}, u32[]{:S(2)}) copy-start(f32[2,1]{0,1:T(1,128)} %param.12) | copy-start | bytes 28
  26.2 4.5 %collective-permute-start.8 = (f32[2,64,256]{2,1,0:T(8,128)S(1)}, f32[2,64,256]{2,1,0:T(8,128)S(1)}, u32[]{:S(2)}, u32[]{:S(2)}) collective-permute-start(f32[2,64,256]{2,1,0:T(8,128)S(1)} %get-tuple-element.33), channel_id=1, source_target_pairs={{0,8},{8,0},{16,24},{24,16},{1,9},{9,1},{17,25},{25,17},{2,10},{10... | collective-permute-start | bytes 393224 | tf_op jit(solution)/shard_map/ppermute | solution.py:546
  26.3 9.4 %copy-start.3 = (s32[17]{0:T(128)S(1)}, s32[17]{0:T(128)}, u32[]{:S(2)}) copy-start(s32[17]{0:T(128)} %offsets.1) | copy-start | bytes 208
  26.3 5.7 %collective-permute-start.9 = (f32[2,64,256]{2,1,0:T(8,128)S(1)}, f32[2,64,256]{2,1,0:T(8,128)S(1)}, u32[]{:S(2)}, u32[]{:S(2)}) collective-permute-start(f32[2,64,256]{2,1,0:T(8,128)S(1)} %get-tuple-element.34), channel_id=1, source_target_pairs={{0,2},{2,0},{4,6},{6,4},{8,16},{10,18},{12,20},{14,22},{16,8},{18,... | collective-permute-start | bytes 393224 | tf_op jit(solution)/shard_map/ppermute | solution.py:547
  33.0 5.8 %collective-permute-start.10 = (f32[4,48,128]{2,1,0:T(8,128)S(1)}, f32[4,48,128]{2,1,0:T(8,128)S(1)}, u32[]{:S(2)}, u32[]{:S(2)}) collective-permute-start(f32[4,48,128]{2,1,0:T(8,128)S(1)} %get-tuple-element.37), channel_id=1, source_target_pairs={{0,1},{1,0},{2,3},{3,2},{4,5},{5,4},{6,7},{7,6},{8,9},{9,8},{10,11... | collective-permute-start | bytes 294920 | tf_op jit(solution)/shard_map/ppermute | solution.py:567

commit v3 on v2

--- a/solution.py
+++ b/solution.py
@@ -99,8 +99,8 @@
 
 
 VMEM = pl.BlockSpec(memory_space=pltpu.VMEM)
-SMEM = pl.BlockSpec(memory_space=pltpu.SMEM)
 HBM = pl.BlockSpec(memory_space=pltpu.HBM)
+EARLY = 6
 PARAMS = pltpu.CompilerParams(vmem_limit_bytes=16 << 20)
 
 
@@ -142,52 +142,76 @@
     return jax.ShapeDtypeStruct(shape, jnp.float32)
 
 
-def pack_kernel(p, count, *refs):
-    sources = refs[:count]
-    outs = refs[count : count + 4]
-    sems = refs[count + 4]
+def pack_kernel(p, groups, extra, *refs):
+    refs = list(refs)
+
+    def take(n):
+        taken = refs[:n]
+        del refs[:n]
+        return taken
+
+    sources = [take(n) for n in groups]
+    smalls = take(extra)
+    outs = [take(4) for _ in groups]
+    held = take(extra)
+    sems, small_sems = refs
     b = lax.axis_index("gy")
     starts = (
+        ((1 - b) * (p.rows - p.inside), p.inside),
         (b * (p.rows - p.inside), p.inside),
-        ((1 - b) * (p.rows - p.inside), p.inside),
         ((1 - b) * (p.rows - p.d0), p.d0),
         (b * (p.rows - p.d0), p.d0),
     )
+    targets = (1, 0, 2, 3)
     copies = []
-    plane = 0
-    for i, source in enumerate(sources):
-        planes = source.shape[0]
-        for j, (start, size) in enumerate(starts):
-            copies.append(
-                pltpu.make_async_copy(
-                    source.at[:, pl.ds(pl.multiple_of(start, 8), size), :],
-                    outs[j].at[pl.ds(plane, planes)],
-                    sems.at[i, j],
+    i = 0
+    for members, out in zip(sources, outs):
+        plane = 0
+        for source in members:
+            planes = source.shape[0]
+            for j, (start, size) in zip(targets, starts):
+                copies.append(
+                    pltpu.make_async_copy(
+                        source.at[:, pl.ds(pl.multiple_of(start, 8), size), :],
+                        out[j].at[pl.ds(plane, planes)],
+                        sems.at[i, j],
+                    )
                 )
-            )
-        plane += planes
+            plane += planes
+            i += 1
+    for i in range(extra):
+        copies.append(pltpu.make_async_copy(smalls[i], held[i], small_sems.at[i]))
     for copy in copies:
         copy.start()
     for copy in copies:
         copy.wait()
 
 
-def pack(p, *sources):
-    planes = sum(s.shape[0] for s in sources)
-    return pl.pallas_call(
-        functools.partial(pack_kernel, p, len(sources)),
-        out_shape=(
-            f32(planes, p.inside, p.cols),
-            f32(planes, p.inside, p.cols),
-            f32(planes, p.d0, p.cols),
-            f32(planes, p.d0, p.cols),
-        ),
-        in_specs=[HBM] * len(sources),
-        out_specs=(VMEM,) * 4,
-        scratch_shapes=[pltpu.SemaphoreType.DMA((len(sources), 4))],
+def in_hbm(x):
+    return pltpu.with_memory_space_constraint(x, pltpu.HBM)
+
+
+def pack(p, groups, smalls):
+    flat = [x for group in groups for x in group]
+    shapes = []
+    for group in groups:
+        planes = sum(x.shape[0] for x in group)
+        shapes += [f32(planes, size, p.cols) for size in (p.inside, p.inside, p.d0, p.d0)]
+    shapes += [jax.ShapeDtypeStruct(x.shape, x.dtype) for x in smalls]
+    outs = pl.pallas_call(
+        functools.partial(pack_kernel, p, [len(group) for group in groups], len(smalls)),
+        out_shape=tuple(shapes),
+        in_specs=[HBM] * (len(flat) + len(smalls)),
+        out_specs=(VMEM,) * len(shapes),
+        scratch_shapes=[
+            pltpu.SemaphoreType.DMA((len(flat), 4)),
+            pltpu.SemaphoreType.DMA((max(1, len(smalls)),)),
+        ],
         compiler_params=PARAMS,
-        cost_estimate=cost(0, 4 * planes * p.rows * p.cols * 3),
-    )(*sources)
+        cost_estimate=cost(0, 4 * sum(x.size for x in flat) * 3),
+    )(*(in_hbm(x) for x in (*flat, *smalls)))
+    count = 4 * len(groups)
+    return [outs[i : i + 4] for i in range(0, count, 4)], outs[count:]
 
 
 def lay_out(p, target, own, other, halo_own, halo_other):
@@ -234,7 +258,16 @@
     )(own, other, halo_own, halo_other)
 
 
-def spread_kernel(p, step, index, amp, src_index, src_amp, out, row_hot, col_hot, total):
+def spread_kernel(
+    p, step, index, amp, src_index_in, src_amp_in,
+    out, row_hot, col_hot, total, src_index, src_amp, sems,
+):
+    fetches = [
+        pltpu.make_async_copy(src_index_in, src_index, sems.at[0]),
+        pltpu.make_async_copy(src_amp_in, src_amp, sems.at[1]),
+    ]
+    for fetch in fetches:
+        fetch.start()
     lays, stride = p.lays, p.e0
     g = lax.axis_index("grp")
     first = p.base_row() - p.d1
@@ -278,6 +311,8 @@
             + total[rows[2] : rows[2] + p.e1]
         )
     out[0] = jnp.zeros((lays, p.e1, p.ny), jnp.float32)
+    for fetch in fetches:
+        fetch.wait()
     for s in range(src_index.shape[0]):
         flat = src_index[s]
         line = lax.div(flat, p.ny)
@@ -288,8 +323,7 @@
         @pl.when((lay >= 0) & (lay < lays) & (row >= 0) & (row < p.e1))
         def _():
             spot = lax.broadcasted_iota(jnp.int32, (1, p.ny), 1) == col
-            amount = src_amp[step * src_index.shape[0] + s]
-            out[0, lay, pl.ds(row, 1), :] += jnp.where(spot, amount, 0.0)
+            out[0, lay, pl.ds(row, 1), :] += jnp.where(spot, src_amp[s, step], 0.0)
 
 
 def spread(p, step, index, amp, src_index, src_amp):
@@ -298,16 +332,19 @@
     return pl.pallas_call(
         functools.partial(spread_kernel, p, step),
         out_shape=f32(p.fields, p.lays, p.e1, p.ny),
-        in_specs=[VMEM] * 2 + [SMEM] * 2,
+        in_specs=[VMEM] * 2 + [HBM] * 2,
         out_specs=VMEM,
         scratch_shapes=[
             pltpu.VMEM((tall, wide * 128), jnp.bfloat16),
             pltpu.VMEM((p.ny, wide * 128), jnp.bfloat16),
             pltpu.VMEM((tall, p.ny), jnp.float32),
+            pltpu.SMEM(src_index.shape, jnp.int32),
+            pltpu.SMEM(src_amp.shape, jnp.float32),
+            pltpu.SemaphoreType.DMA((2,)),
         ],
         compiler_params=PARAMS,
         cost_estimate=cost(2 * tall * wide * 128 * p.ny, 4 * wide * 128 * 3),
-    )(index, amp, src_index, src_amp)
+    )(index, amp, src_index, in_hbm(src_amp))
 
 
 def advance(p, now, before, before_at, coeff, coeff_at, recv_a, recv_b, added, added_at, out, margin):
@@ -423,10 +460,17 @@
     )(now, before, coeff, recv_a, recv_b, added)
 
 
-def image_kernel(p, one, two, offsets, out, held, place, sems):
-    for k in range(NOFF):
-        place[offsets[k] + MAXOFF] = k
+def image_kernel(p, one, two, offsets, out, held, order, place, sems, order_sem):
+    fetch = pltpu.make_async_copy(offsets, order, order_sem)
+    fetch.start()
     copies = []
+    ready = 0
+
+    def launch(d):
+        copy = pltpu.make_async_copy(held.at[d], out.at[place[d]], sems.at[d])
+        copy.start()
+        copies.append(copy)
+
     for d in range(NOFF):
         shift = d - MAXOFF
         for lay in range(p.lays):
@@ -436,9 +480,15 @@
                 s2 = two[lay, p.d2 + r : p.d2 + r + 8, :]
                 r2 = two[p.lays + lay, p.d2 + r + shift : p.d2 + r + shift + 8, :]
                 held[d, lay, r : r + 8, :] = s1 * r1 + s2 * r2
-        copy = pltpu.make_async_copy(held.at[d], out.at[place[d]], sems.at[d])
-        copy.start()
-        copies.append(copy)
+        if d < EARLY:
+            continue
+        if d == EARLY:
+            fetch.wait()
+            for k in range(NOFF):
+                place[order[k] + MAXOFF] = k
+        while ready <= d:
+            launch(ready)
+            ready += 1
     for copy in copies:
         copy.wait()
 
@@ -448,16 +498,18 @@
     return pl.pallas_call(
         functools.partial(image_kernel, p),
         out_shape=f32(NOFF, p.lays, p.half, p.ny),
-        in_specs=[VMEM] * 2 + [SMEM],
+        in_specs=[VMEM] * 2 + [HBM],
         out_specs=HBM,
         scratch_shapes=[
             pltpu.VMEM((NOFF, p.lays, p.half, p.ny), jnp.float32),
             pltpu.SMEM((NOFF,), jnp.int32),
+            pltpu.SMEM((NOFF,), jnp.int32),
             pltpu.SemaphoreType.DMA((NOFF,)),
+            pltpu.SemaphoreType.DMA,
         ],
         compiler_params=PARAMS,
         cost_estimate=cost(3 * size, 4 * size),
-    )(one, two, offsets)
+    )(one, two, in_hbm(offsets))
 
 
 def settle_kernel(p, keep, got, out, sems):
@@ -535,8 +587,7 @@
     planes = p.fields * p.lays
     tile = (p.rows, p.cols)
 
-    def redistribute(*sources):
-        own, give, edge, corner = pack(p, *sources)
+    def redistribute(own, give, edge, corner):
         other = lax.ppermute(give, "gy", [(0, 1), (1, 0)])
         halo_own = lax.ppermute(edge, AXES, halo_pairs(p, False))
         halo_other = lax.ppermute(corner, AXES, halo_pairs(p, True))
@@ -552,13 +603,21 @@
     if wide * 128 > count:
         rec_index = jnp.pad(rec_index, (0, wide * 128 - count))
         rec_amp = jnp.pad(rec_amp, ((0, 0), (0, wide * 128 - count)))
-    points = (rec_index.reshape(wide, 128), rec_amp, src_index, src_amp.reshape(-1))
-
-    now = redistribute(current.reshape(planes, *tile))
-    rest = redistribute(previous.reshape(planes, *tile), coeff.reshape(3 * p.lays, *tile))
+    points = (rec_index.reshape(wide, 128), rec_amp)
+
+    (now, rest), points = pack(
+        p,
+        (
+            (current.reshape(planes, *tile),),
+            (previous.reshape(planes, *tile), coeff.reshape(3 * p.lays, *tile)),
+        ),
+        points,
+    )
+    now = redistribute(*now)
+    rest = redistribute(*rest)
     added = []
     for step in range(STEPS):
-        added.append(spread(p, step, *points))
+        added.append(spread(p, step, *points, src_index, src_amp.T))
     whole, send_a, send_b = join(p, *now)
     recv_a, recv_b = swap_layers(send_a, send_b)
     one, weights, send_a, send_b = first_step(p, whole, recv_a, recv_b, rest, added[0])

time: 39.8 us -> 37.8 us (0.950)
  local copies, waits for them, and re-layouts: 4.88 us -> 0 us
  waiting for transfers between devices: 10.2 us -> 12.7 us
  Pallas kernels: 8.99 us -> 9.98 us
  starting transfers between devices: 14 us -> 13.6 us
    unnamed x14 -> x0, local copies, waits for them, and re-layouts: 4.88 us -> none
    ppermute x2, waiting for transfers between devices: 7.97 us -> 9.78 us  [redistribute(): halo_own = lax.ppermute(edge, AXES, halo_pairs(p, False))]
    ppermute x1, starting transfers between devices: 2.69 us -> 0.95 us  [body_rows(): got = lax.ppermute(give, 'gy', [(0, 1), (1, 0)])]
    ppermute x2, starting transfers between devices: 4.59 us -> 5.99 us  [swap_layers(): recv_b = lax.ppermute(send_b, ('grp', 'gx'), pairs_between(p))]
    pallas_call x2 -> x1, Pallas kernels: 0.42 us -> 1.45 us  [pack(): pl.pallas_call(functools.partial(pack_kernel, p, [len(group) for group in...]
    ppermute x1, waiting for transfers between devices: 0.98 us -> 1.72 us  [body_rows(): got = lax.ppermute(give, 'gy', [(0, 1), (1, 0)])]
  transfers between devices with their start and end apart: 11 -> 11, of which waited for: 3 -> 4; matrix products, arithmetic and copies ran while one was open for 0% -> 0% of each run, Pallas kernels for 15% -> 15%
where the time goes in v3:
time: 37.8 us; the launch traced here: 37.6 us
  starting transfers between devices  13.6 us (36%)
  waiting for transfers between devices  12.7 us (34%)
  Pallas kernels  9.98 us (26%)
  between operations  1.37 us (4%)
    ppermute x2, waiting for transfers between devices, redistribute(): halo_own = lax.ppermute(edge, AXES, halo_pairs(p, False))  9.78 us
    ppermute x2, starting transfers between devices, swap_layers(): recv_b = lax.ppermute(send_b, ('grp', 'gx'), pairs_between(p))  5.99 us
    pallas_call x2, Pallas kernels, spread(): pl.pallas_call(functools.partial(spread_kernel, p, step), out_shape=f32(p...  3.49 us
    ppermute x2, starting transfers between devices, redistribute(): other = lax.ppermute(give, 'gy', [(0, 1), (1, 0)])  3.11 us
    ppermute x2, starting transfers between devices, redistribute(): halo_own = lax.ppermute(edge, AXES, halo_pairs(p, False))  2.24 us
    pallas_call x1, Pallas kernels, correlate_rows(): pl.pallas_call(functools.partial(image_kernel, p), out_shape=f32(NOFF, p....  2 us
    ppermute x1, waiting for transfers between devices, body_rows(): got = lax.ppermute(give, 'gy', [(0, 1), (1, 0)])  1.72 us
    pallas_call x1, Pallas kernels, pack(): pl.pallas_call(functools.partial(pack_kernel, p, [len(group) for group in...  1.45 us
  transfers between devices with their start and end apart: 11, of which 4 were waited for; matrix products, arithmetic and copies ran while one was open for 0% of the time, Pallas kernels for 15%

profile of v3, /device:TPU:0, one launch (start us, length us, event | category | flops | bytes accessed | tf_op | source)
XLA Modules:
  0.0 37.6 jit_solution(5581533882012387434)
XLA Ops:
  0.6 1.5 %shard_map.95 = (f32[4,64,128]{2,1,0:T(8,128)S(1)}, f32[4,64,128]{2,1,0:T(8,128)S(1)}, f32[4,16,128]{2,1,0:T(8,128)S(1)}, f32[4,16,128]{2,1,0:T(8,128)S(1)}, f32...) custom-call(f32[4,96,128]{2,1,0:T(8,128)} %bitcast.8, ...), custom_call_target="tpu_custom_call" | custom-call | bytes 2064384 | tf_op jit(solution)/shard_map/pallas_call | solution.py:201
  2.1 3.0 %collective-permute-start.5 = (f32[10,64,128]{2,1,0:T(8,128)S(1)}, f32[10,64,128]{2,1,0:T(8,128)S(1)}, u32[]{:S(2)}, u32[]{:S(2)}) collective-permute-start(f32[10,64,128]{2,1,0:T(8,128)S(1)} %get-tuple-element.30), channel_id=1, source_target_pairs={{0,1},{1,0},{2,3},{3,2},{4,5},{5,4},{6,7},{7,6},{8,9},{9,8},{10,11... | collective-permute-start | bytes 983048 | tf_op jit(solution)/shard_map/ppermute | solution.py:591
  5.1 0.1 collective-permute-start
  5.2 2.0 %collective-permute-start.1 = (f32[4,16,128]{2,1,0:T(8,128)S(1)}, f32[4,16,128]{2,1,0:T(8,128)S(1)}, u32[]{:S(2)}, u32[]{:S(2)}) collective-permute-start(f32[4,16,128]{2,1,0:T(8,128)S(1)} %get-tuple-element.24), channel_id=1, source_target_pairs={{0,2},{2,4},{3,1},{4,6},{5,3},{7,5},{8,10},{10,12},{11,9},{12,14},... | collective-permute-start | bytes 98312 | tf_op jit(solution)/shard_map/ppermute | solution.py:592
  7.2 0.0 collective-permute-start.2
  7.2 9.1 %collective-permute-done.1.halo_own = f32[4,16,128]{2,1,0:T(8,128)S(1)} collective-permute-done((f32[4,16,128]{2,1,0:T(8,128)S(1)}, f32[4,16,128]{2,1,0:T(8,128)S(1)}, u32[]{:S(2)}, u32[]{:S(2)}) %collective-permute-start.1) | collective-permute-done | bytes 32800 | tf_op jit(solution)/shard_map/ppermute | solution.py:592
  16.3 0.0 collective-permute-done.2.halo_other
  16.3 0.0 collective-permute-done.other
  16.4 0.1 shard_map.96
  16.4 0.1 collective-permute-start.3
  16.5 1.9 %collective-permute-start.4 = (f32[2,72,256]{2,1,0:T(8,128)S(1)}, f32[2,72,256]{2,1,0:T(8,128)S(1)}, u32[]{:S(2)}, u32[]{:S(2)}) collective-permute-start(f32[2,72,256]{2,1,0:T(8,128)S(1)} %get-tuple-element.28), channel_id=1, source_target_pairs={{0,2},{2,0},{4,6},{6,4},{8,16},{10,18},{12,20},{14,22},{16,8},{18,... | collective-permute-start | bytes 442376 | tf_op jit(solution)/shard_map/ppermute | solution.py:598
  18.4 0.2 collective-permute-start.6
  18.6 1.1 %collective-permute-start.7 = (f32[10,16,128]{2,1,0:T(8,128)S(1)}, f32[10,16,128]{2,1,0:T(8,128)S(1)}, u32[]{:S(2)}, u32[]{:S(2)}) collective-permute-start(f32[10,16,128]{2,1,0:T(8,128)S(1)} %get-tuple-element.32), channel_id=1, source_target_pairs={{1,2},{2,1},{3,4},{4,3},{5,6},{6,5},{9,10},{10,9},{11,12},{12,11},... | collective-permute-start | bytes 245768 | tf_op jit(solution)/shard_map/ppermute | solution.py:593
  20.4 1.7 %shard_map.97.added = f32[2,2,72,256]{3,2,1,0:T(8,128)S(1)} custom-call(s32[16,128]{1,0:T(8,128)S(1)} %get-tuple-element.33.index, f32[2,2048]{1,0:T(2,128)S(1)} %get-tuple-element.34.amp, s32[1]{0:T(128)S(6)} %copy.10.src_index_in, f32[1,2]{1,0:T(1,128)} %bitcast.11), custom_call_target="tpu_custom_call" | custom-call | flops 503316480 | bytes 24576 | tf_op jit(solution)/shard_map/pallas_call | solution.py:332
  22.1 0.7 %collective-permute-done.6.halo_own = f32[10,16,128]{2,1,0:T(8,128)S(1)} collective-permute-done((f32[10,16,128]{2,1,0:T(8,128)S(1)}, f32[10,16,128]{2,1,0:T(8,128)S(1)}, u32[]{:S(2)}, u32[]{:S(2)}) %collective-permute-start.6) | collective-permute-done | bytes 81952 | tf_op jit(solution)/shard_map/ppermute | solution.py:592
  22.8 0.0 collective-permute-done.7.halo_other
  22.8 0.0 collective-permute-done.3.recv_a
  22.8 0.0 collective-permute-done.4.recv_b
  22.8 0.0 collective-permute-done.5.other
  22.8 1.2 %shard_map.98 = (f32[4,72,256]{2,1,0:T(8,128)S(1)}, f32[6,64,256]{2,1,0:T(8,128)S(1)}, f32[2,64,256]{2,1,0:T(8,128)S(1)}, f32[2,64,256]{2,1,0:T(8,128)S(1)}) custom-call(f32[4,80,256]{2,1,0:T(8,128)S(1)} %get-tuple-element.26.now.before, f32[2,72,256]{2,1,0:T(8,128)S(1)} %collective-permute-done.3.recv_a, f32[2,72,256]{2,1,0:T(8,128)S(1)} %collective-permute-done.4.recv_b, ...), custom_call_target="tpu_custom_call" | custom-call | flops 4423680 | bytes 589824 | tf_op jit(solution)/shard_map/pallas_call | solution.py:419
  24.1 0.1 collective-permute-start.8
  24.2 4.1 %collective-permute-start.9 = (f32[2,64,256]{2,1,0:T(8,128)S(1)}, f32[2,64,256]{2,1,0:T(8,128)S(1)}, u32[]{:S(2)}, u32[]{:S(2)}) collective-permute-start(f32[2,64,256]{2,1,0:T(8,128)S(1)} %get-tuple-element.38), channel_id=1, source_target_pairs={{0,2},{2,0},{4,6},{6,4},{8,16},{10,18},{12,20},{14,22},{16,8},{18,... | collective-permute-start | bytes 393224 | tf_op jit(solution)/shard_map/ppermute | solution.py:598
  28.3 1.7 %shard_map.99.added = f32[2,2,72,256]{3,2,1,0:T(8,128)S(1)} custom-call(s32[16,128]{1,0:T(8,128)S(1)} %get-tuple-element.33.index, f32[2,2048]{1,0:T(2,128)S(1)} %get-tuple-element.34.amp, s32[1]{0:T(128)S(6)} %copy.10.src_index_in, f32[1,2]{1,0:T(1,128)} %bitcast.12), custom_call_target="tpu_custom_call" | custom-call | flops 503316480 | bytes 24576 | tf_op jit(solution)/shard_map/pallas_call | solution.py:332
  30.0 0.0 collective-permute-done.8.recv_a
  30.0 1.2 %collective-permute-done.9.recv_b = f32[2,64,256]{2,1,0:T(8,128)S(1)} collective-permute-done((f32[2,64,256]{2,1,0:T(8,128)S(1)}, f32[2,64,256]{2,1,0:T(8,128)S(1)}, u32[]{:S(2)}, u32[]{:S(2)}) %collective-permute-start.9) | collective-permute-done | bytes 131104 | tf_op jit(solution)/shard_map/ppermute | solution.py:598
  31.2 1.0 %shard_map.100 = (f32[4,64,256]{2,1,0:T(8,128)S(1)}, f32[4,48,128]{2,1,0:T(8,128)S(1)}, f32[4,48,128]{2,1,0:T(8,128)S(1)}) custom-call(f32[4,72,256]{2,1,0:T(8,128)S(1)} %get-tuple-element.35.now.one, f32[4,80,256]{2,1,0:T(8,128)S(1)} %get-tuple-element.26.now.before, f32[6,64,256]{2,1,0:T(8,128)S(1)} %get-tuple-element.36.coeff, ...), custom_call_target="tpu_custom_call" | custom-call | flops 3932160 | bytes 524288 | tf_op jit(solution)/shard_map/pallas_call | solution.py:449
  32.3 0.9 %collective-permute-start.10 = (f32[4,48,128]{2,1,0:T(8,128)S(1)}, f32[4,48,128]{2,1,0:T(8,128)S(1)}, u32[]{:S(2)}, u32[]{:S(2)}) collective-permute-start(f32[4,48,128]{2,1,0:T(8,128)S(1)} %get-tuple-element.41), channel_id=1, source_target_pairs={{0,1},{1,0},{2,3},{3,2},{4,5},{5,4},{6,7},{7,6},{8,9},{9,8},{10,11... | collective-permute-start | bytes 294920 | tf_op jit(solution)/shard_map/ppermute | solution.py:626
  33.2 2.0 %shard_map.101 = f32[17,2,48,256]{3,2,1,0:T(8,128)} custom-call(f32[4,72,256]{2,1,0:T(8,128)S(1)} %get-tuple-element.35.now.one, f32[4,64,256]{2,1,0:T(8,128)S(1)} %get-tuple-element.39.two, s32[17]{0:T(128)} %offsets.1), custom_call_target="tpu_custom_call" | custom-call | flops 1253376 | bytes 1671168 | tf_op jit(solution)/shard_map/pallas_call | solution.py:498
  35.2 1.7 %collective-permute-done.10.got = f32[4,48,128]{2,1,0:T(8,128)S(1)} collective-permute-done((f32[4,48,128]{2,1,0:T(8,128)S(1)}, f32[4,48,128]{2,1,0:T(8,128)S(1)}, u32[]{:S(2)}, u32[]{:S(2)}) %collective-permute-start.10) | collective-permute-done | bytes 98336 | tf_op jit(solution)/shard_map/ppermute | solution.py:626
  36.9 0.7 %shard_map.102 = f32[4,96,128]{2,1,0:T(8,128)} custom-call(f32[4,48,128]{2,1,0:T(8,128)S(1)} %get-tuple-element.40.keep, f32[4,48,128]{2,1,0:T(8,128)S(1)} %collective-permute-done.10.got), custom_call_target="tpu_custom_call" | custom-call | bytes 393216 | tf_op jit(solution)/shard_map/pallas_call | solution.py:533
Async XLA Ops:
  2.1 20.7 %collective-permute-start.5 = (f32[10,64,128]{2,1,0:T(8,128)S(1)}, f32[10,64,128]{2,1,0:T(8,128)S(1)}, u32[]{:S(2)}, u32[]{:S(2)}) collective-permute-start(f32[10,64,128]{2,1,0:T(8,128)S(1)} %get-tuple-element.30), channel_id=1, source_target_pairs={{0,1},{1,0},{2,3},{3,2},{4,5},{5,4},{6,7},{7,6},{8,9},{9,8},{10,11... | collective-permute-start | bytes 983048 | tf_op jit(solution)/shard_map/ppermute | solution.py:591
  5.1 11.2 %collective-permute-start = (f32[4,64,128]{2,1,0:T(8,128)S(1)}, f32[4,64,128]{2,1,0:T(8,128)S(1)}, u32[]{:S(2)}, u32[]{:S(2)}) collective-permute-start(f32[4,64,128]{2,1,0:T(8,128)S(1)} %get-tuple-element.23), channel_id=1, source_target_pairs={{0,1},{1,0},{2,3},{3,2},{4,5},{5,4},{6,7},{7,6},{8,9},{9,8},{10,11... | collective-permute-start | bytes 393224 | tf_op jit(solution)/shard_map/ppermute | solution.py:591
  5.2 11.1 %collective-permute-start.1 = (f32[4,16,128]{2,1,0:T(8,128)S(1)}, f32[4,16,128]{2,1,0:T(8,128)S(1)}, u32[]{:S(2)}, u32[]{:S(2)}) collective-permute-start(f32[4,16,128]{2,1,0:T(8,128)S(1)} %get-tuple-element.24), channel_id=1, source_target_pairs={{0,2},{2,4},{3,1},{4,6},{5,3},{7,5},{8,10},{10,12},{11,9},{12,14},... | collective-permute-start | bytes 98312 | tf_op jit(solution)/shard_map/ppermute | solution.py:592
  7.2 9.1 %collective-permute-start.2 = (f32[4,16,128]{2,1,0:T(8,128)S(1)}, f32[4,16,128]{2,1,0:T(8,128)S(1)}, u32[]{:S(2)}, u32[]{:S(2)}) collective-permute-start(f32[4,16,128]{2,1,0:T(8,128)S(1)} %get-tuple-element.25), channel_id=1, source_target_pairs={{1,2},{2,1},{3,4},{4,3},{5,6},{6,5},{9,10},{10,9},{11,12},{12,11},... | collective-permute-start | bytes 98312 | tf_op jit(solution)/shard_map/ppermute | solution.py:593
  16.4 6.4 %collective-permute-start.3 = (f32[2,72,256]{2,1,0:T(8,128)S(1)}, f32[2,72,256]{2,1,0:T(8,128)S(1)}, u32[]{:S(2)}, u32[]{:S(2)}) collective-permute-start(f32[2,72,256]{2,1,0:T(8,128)S(1)} %get-tuple-element.27), channel_id=1, source_target_pairs={{0,8},{8,0},{16,24},{24,16},{1,9},{9,1},{17,25},{25,17},{2,10},{10... | collective-permute-start | bytes 442376 | tf_op jit(solution)/shard_map/ppermute | solution.py:597
  16.5 6.3 %collective-permute-start.4 = (f32[2,72,256]{2,1,0:T(8,128)S(1)}, f32[2,72,256]{2,1,0:T(8,128)S(1)}, u32[]{:S(2)}, u32[]{:S(2)}) collective-permute-start(f32[2,72,256]{2,1,0:T(8,128)S(1)} %get-tuple-element.28), channel_id=1, source_target_pairs={{0,2},{2,0},{4,6},{6,4},{8,16},{10,18},{12,20},{14,22},{16,8},{18,... | collective-permute-start | bytes 442376 | tf_op jit(solution)/shard_map/ppermute | solution.py:598
  18.4 4.4 %collective-permute-start.6 = (f32[10,16,128]{2,1,0:T(8,128)S(1)}, f32[10,16,128]{2,1,0:T(8,128)S(1)}, u32[]{:S(2)}, u32[]{:S(2)}) collective-permute-start(f32[10,16,128]{2,1,0:T(8,128)S(1)} %get-tuple-element.31), channel_id=1, source_target_pairs={{0,2},{2,4},{3,1},{4,6},{5,3},{7,5},{8,10},{10,12},{11,9},{12,14},... | collective-permute-start | bytes 245768 | tf_op jit(solution)/shard_map/ppermute | solution.py:592
  18.6 4.2 %collective-permute-start.7 = (f32[10,16,128]{2,1,0:T(8,128)S(1)}, f32[10,16,128]{2,1,0:T(8,128)S(1)}, u32[]{:S(2)}, u32[]{:S(2)}) collective-permute-start(f32[10,16,128]{2,1,0:T(8,128)S(1)} %get-tuple-element.32), channel_id=1, source_target_pairs={{1,2},{2,1},{3,4},{4,3},{5,6},{6,5},{9,10},{10,9},{11,12},{12,11},... | collective-permute-start | bytes 245768 | tf_op jit(solution)/shard_map/ppermute | solution.py:593
  24.1 5.9 %collective-permute-start.8 = (f32[2,64,256]{2,1,0:T(8,128)S(1)}, f32[2,64,256]{2,1,0:T(8,128)S(1)}, u32[]{:S(2)}, u32[]{:S(2)}) collective-permute-start(f32[2,64,256]{2,1,0:T(8,128)S(1)} %get-tuple-element.37), channel_id=1, source_target_pairs={{0,8},{8,0},{16,24},{24,16},{1,9},{9,1},{17,25},{25,17},{2,10},{10... | collective-permute-start | bytes 393224 | tf_op jit(solution)/shard_map/ppermute | solution.py:597
  24.2 7.1 %collective-permute-start.9 = (f32[2,64,256]{2,1,0:T(8,128)S(1)}, f32[2,64,256]{2,1,0:T(8,128)S(1)}, u32[]{:S(2)}, u32[]{:S(2)}) collective-permute-start(f32[2,64,256]{2,1,0:T(8,128)S(1)} %get-tuple-element.38), channel_id=1, source_target_pairs={{0,2},{2,0},{4,6},{6,4},{8,16},{10,18},{12,20},{14,22},{16,8},{18,... | collective-permute-start | bytes 393224 | tf_op jit(solution)/shard_map/ppermute | solution.py:598
  32.3 4.7 %collective-permute-start.10 = (f32[4,48,128]{2,1,0:T(8,128)S(1)}, f32[4,48,128]{2,1,0:T(8,128)S(1)}, u32[]{:S(2)}, u32[]{:S(2)}) collective-permute-start(f32[4,48,128]{2,1,0:T(8,128)S(1)} %get-tuple-element.41), channel_id=1, source_target_pairs={{0,1},{1,0},{2,3},{3,2},{4,5},{5,4},{6,7},{7,6},{8,9},{9,8},{10,11... | collective-permute-start | bytes 294920 | tf_op jit(solution)/shard_map/ppermute | solution.py:626

commit v4 on v0

--- a/solution.py
+++ b/solution.py
@@ -1,11 +1,17 @@
+import functools
+
 import jax
 import jax.numpy as jnp
 from jax import lax
+from jax.experimental import pallas as pl
+from jax.experimental.pallas import tpu as pltpu
 from jax.sharding import PartitionSpec as P
+
 
 STEPS = 2
 NOFF = 17
 MAXOFF = 8
+REACH = 4
 
 
 STENCIL = (-205.0 / 72.0, 8.0 / 5.0, -1.0 / 5.0, 8.0 / 315.0, -1.0 / 560.0)
@@ -74,7 +80,7 @@
     return jnp.stack(pieces)
 
 
-def body(previous, current, coeff, src_index, src_amp, rec_index, rec_amp, offsets):
+def body_tiles(previous, current, coeff, src_index, src_amp, rec_index, rec_amp, offsets):
     prev, cur = (previous, current)
     snapshots = []
     for step in range(STEPS):
@@ -92,7 +98,640 @@
     return (images, cur)
 
 
+VMEM = pl.BlockSpec(memory_space=pltpu.VMEM)
+HBM = pl.BlockSpec(memory_space=pltpu.HBM)
+EARLY = 6
+PARAMS = pltpu.CompilerParams(vmem_limit_bytes=16 << 20)
+
+
+class Plan:
+    def __init__(self, shape, mesh_shape):
+        self.fields, self.lays, self.rows, self.cols = shape
+        self.n_grp, self.n_gx, self.n_gy = (mesh_shape[k] for k in ("grp", "gx", "gy"))
+        self.nx = self.rows * self.n_gx
+        self.ny = self.cols * self.n_gy
+        self.planes = self.fields * self.lays
+        self.half = self.rows // self.n_gy
+        self.d2 = MAXOFF
+        self.d1 = MAXOFF + REACH
+        self.d0 = MAXOFF + 2 * REACH
+        self.e0 = self.rows + 2 * self.d0
+        self.e1 = self.rows + 2 * self.d1
+        self.e2 = self.rows + 2 * self.d2
+        self.near = self.half + 2 * MAXOFF
+        self.lot = self.planes * REACH
+        self.lots = self.cols // self.lot
+        self.gift = self.lays * (self.half + self.near)
+
+    def fits(self):
+        return (
+            self.n_gy == 2
+            and self.n_grp % 2 == 0
+            and self.n_gx % 2 == 0
+            and self.rows % 16 == 0
+            and self.d0 <= self.rows
+            and self.cols == 128
+            and self.fields == 2
+            and self.lays * self.cols <= 256
+            and self.e0 <= 256
+            and self.cols % self.lot == 0
+            and STEPS == 2
+        )
+
+
+def cost(flops, moved):
+    return pl.CostEstimate(flops=flops, bytes_accessed=moved, transcendentals=0)
+
+
+def f32(*shape):
+    return jax.ShapeDtypeStruct(shape, jnp.float32)
+
+
+def in_hbm(x):
+    return pltpu.with_memory_space_constraint(x, pltpu.HBM)
+
+
+def parity(name):
+    return lax.rem(lax.axis_index(name), 2)
+
+
+def pack_kernel(p, groups, extra, *refs):
+    refs = list(refs)
+
+    def take(n):
+        taken = refs[:n]
+        del refs[:n]
+        return taken
+
+    sources = [take(n) for n in groups]
+    smalls = take(extra)
+    outs = [take(3) for _ in groups]
+    held = take(extra)
+    sems, small_sems = refs
+    odd = parity("gx")
+    starts = (
+        ((1 - odd) * (p.rows - p.d0), p.d0),
+        (odd * (p.rows - p.d0), p.d0),
+        (0, p.rows),
+    )
+    copies = []
+    i = 0
+    for members, out in zip(sources, outs):
+        plane = 0
+        for source in members:
+            planes = source.shape[0]
+            for j, (start, size) in enumerate(starts):
+                copies.append(
+                    pltpu.make_async_copy(
+                        source.at[:, pl.ds(pl.multiple_of(start, 8), size), :],
+                        out[j].at[pl.ds(plane, planes)],
+                        sems.at[i, j],
+                    )
+                )
+            plane += planes
+            i += 1
+    for i in range(extra):
+        copies.append(pltpu.make_async_copy(smalls[i], held[i], small_sems.at[i]))
+    for copy in copies:
+        copy.start()
+    for copy in copies:
+        copy.wait()
+
+
+def pack(p, groups, smalls):
+    flat = [x for group in groups for x in group]
+    shapes = []
+    for group in groups:
+        planes = sum(x.shape[0] for x in group)
+        shapes += [f32(planes, size, p.cols) for size in (p.d0, p.d0, p.rows)]
+    shapes += [jax.ShapeDtypeStruct(x.shape, x.dtype) for x in smalls]
+    outs = pl.pallas_call(
+        functools.partial(pack_kernel, p, [len(group) for group in groups], len(smalls)),
+        out_shape=tuple(shapes),
+        in_specs=[HBM] * (len(flat) + len(smalls)),
+        out_specs=(VMEM,) * len(shapes),
+        scratch_shapes=[
+            pltpu.SemaphoreType.DMA((len(flat), 3)),
+            pltpu.SemaphoreType.DMA((max(1, len(smalls)),)),
+        ],
+        compiler_params=PARAMS,
+        cost_estimate=cost(0, 4 * sum(x.size for x in flat) * 3),
+    )(*(in_hbm(x) for x in (*flat, *smalls)))
+    count = 3 * len(groups)
+    return [outs[i : i + 3] for i in range(0, count, 3)], outs[count:]
+
+
+def lot_rows(p, count):
+    return -(-count // (8 * p.lots)) * 8
+
+
+def lay_out(p, target, own, got_a, got_b):
+    a = lax.axis_index("gx")
+    odd = parity("gx")
+    upper = pl.ds(0, p.d0)
+    lower = pl.ds(p.d0 + p.rows, p.d0)
+    target[:, p.d0 : p.d0 + p.rows, :] = own[...]
+
+    @pl.when(odd == 0)
+    def _():
+        target[:, lower, :] = got_a[...]
+        target[:, upper, :] = jnp.where(a > 0, got_b[...], 0.0)
+
+    @pl.when(odd == 1)
+    def _():
+        target[:, upper, :] = got_a[...]
+        target[:, lower, :] = jnp.where(a < p.n_gx - 1, got_b[...], 0.0)
+
+
+def send_edges(p, whole, send_x, send_a, send_b, shift, count):
+    odd = parity("grp")
+    lay_a = (1 - odd) * (p.lays - 1)
+    lay_b = odd * (p.lays - 1)
+    for f in range(p.fields):
+        send_a[f] = whole[f * p.lays + lay_a, shift : shift + count, :]
+        send_b[f] = whole[f * p.lays + lay_b, shift : shift + count, :]
+    b = lax.axis_index("gy")
+    tall = lot_rows(p, count)
+    lane = lax.broadcasted_iota(jnp.int32, (8, p.cols), 1)
+
+    def packed(first):
+        for r in range(0, tall, 8):
+            block = jnp.zeros((8, p.cols), jnp.float32)
+            for lot in range(p.lots):
+                row = lot * tall + r
+                if row >= count:
+                    continue
+                for plane in range(p.planes):
+                    at = lot * p.lot + plane * REACH
+                    moved = (at - first) % p.cols
+                    x = whole[plane, shift + row : shift + row + 8, :]
+                    x = pltpu.roll(x, moved, 1) if moved else x
+                    block = jnp.where((lane >= at) & (lane < at + REACH), x, block)
+            send_x[r : r + 8, :] = block
+
+    @pl.when(b == 0)
+    def _():
+        packed(p.cols - REACH)
+
+    @pl.when(b == 1)
+    def _():
+        packed(0)
+
+
+def join_kernel(p, own, got_a, got_b, whole, send_x, send_a, send_b):
+    lay_out(p, whole, own, got_a, got_b)
+    send_edges(p, whole, send_x, send_a, send_b, p.d0 - p.d1, p.e1)
+
+
+def edges_shape(p, count):
+    return (f32(lot_rows(p, count), p.cols), f32(p.fields, count, p.cols), f32(p.fields, count, p.cols))
+
+
+def join(p, own, got_a, got_b):
+    return pl.pallas_call(
+        functools.partial(join_kernel, p),
+        out_shape=(f32(p.planes, p.e0, p.cols), *edges_shape(p, p.e1)),
+        in_specs=[VMEM] * 3,
+        out_specs=(VMEM,) * 4,
+        compiler_params=PARAMS,
+        cost_estimate=cost(0, 8 * p.planes * p.e0 * p.cols),
+    )(own, got_a, got_b)
+
+
+def whole_part(x, divisor):
+    return jnp.floor((x.astype(jnp.float32) + 0.5) * (1.0 / divisor)).astype(jnp.int32)
+
+
+def mark_kernel(
+    p, index, amp, src_index_in, src_amp_in, row_hot, col_hot, source, src_index, src_amp, sems
+):
+    fetches = [
+        pltpu.make_async_copy(src_index_in, src_index, sems.at[0]),
+        pltpu.make_async_copy(src_amp_in, src_amp, sems.at[1]),
+    ]
+    for fetch in fetches:
+        fetch.start()
+    lays, stride = p.lays, p.e0
+    first_lay = lax.axis_index("grp") * lays
+    first_row = lax.axis_index("gx") * p.rows - p.d1
+    first_col = lax.axis_index("gy") * p.cols
+    narrow = jnp.bfloat16
+    one, zero = jnp.ones((), narrow), jnp.zeros((), narrow)
+    tall = lax.broadcasted_iota(jnp.int32, (stride, 128), 0).astype(jnp.float32).astype(narrow)
+    spot = lax.broadcasted_iota(jnp.int32, (lays * p.cols, 128), 0)
+    spot = spot.astype(jnp.float32).astype(narrow)
+
+    def whole_number(x, count):
+        return jnp.where((x >= 0) & (x < count), x, -1).astype(jnp.float32).astype(narrow)
+
+    for k in range(index.shape[0]):
+        at = slice(k * 128, (k + 1) * 128)
+        flat = index[k : k + 1, :]
+        line = whole_part(flat, p.ny)
+        lay = whole_part(line, p.nx)
+        row = line - lay * p.nx - first_row
+        col = flat - line * p.ny - first_col
+        inside = (col >= 0) & (col < p.cols)
+        place = whole_number(
+            jnp.where(inside, (lay - first_lay) * p.cols + col, -1), lays * p.cols
+        )
+        col_hot[:, at] = jnp.where(spot == place, one, zero)
+        hit = tall == whole_number(row, p.e1)
+        for step in range(STEPS):
+            rest = amp[step : step + 1, at]
+            for i in range(3):
+                part = rest.astype(narrow)
+                row_hot[step, i * stride : (i + 1) * stride, at] = jnp.where(hit, part, zero)
+                rest = rest - part.astype(jnp.float32)
+    source[...] = jnp.zeros((STEPS, lays, p.e1, p.cols), jnp.float32)
+    for fetch in fetches:
+        fetch.wait()
+    for s in range(src_index.shape[0]):
+        flat = src_index[s]
+        line = lax.div(flat, p.ny)
+        lay = lax.div(line, p.nx) - first_lay
+        row = lax.rem(line, p.nx) - first_row
+        col = lax.rem(flat, p.ny) - first_col
+
+        @pl.when((lay >= 0) & (lay < lays) & (row >= 0) & (row < p.e1))
+        def _():
+            hit = lax.broadcasted_iota(jnp.int32, (1, p.cols), 1) == col
+            for step in range(STEPS):
+                source[step, lay, pl.ds(row, 1), :] += jnp.where(hit, src_amp[s, step], 0.0)
+
+
+def mark(p, index, amp, src_index, src_amp):
+    wide = index.shape[0] * 128
+    return pl.pallas_call(
+        functools.partial(mark_kernel, p),
+        out_shape=(
+            jax.ShapeDtypeStruct((STEPS, 3 * p.e0, wide), jnp.bfloat16),
+            jax.ShapeDtypeStruct((p.lays * p.cols, wide), jnp.bfloat16),
+            f32(STEPS, p.lays, p.e1, p.cols),
+        ),
+        in_specs=[VMEM] * 3 + [HBM],
+        out_specs=(VMEM,) * 3,
+        scratch_shapes=[
+            pltpu.SMEM(src_index.shape, jnp.int32),
+            pltpu.SMEM(src_amp.shape, jnp.float32),
+            pltpu.SemaphoreType.DMA((2,)),
+        ],
+        compiler_params=PARAMS,
+        cost_estimate=cost(10 * p.e0 * wide * p.lays, 12 * wide),
+    )(index, amp, src_index, in_hbm(src_amp))
+
+
+def spread_kernel(p, step, row_hot, col_hot, out, total):
+    total[...] = lax.dot_general(
+        row_hot[step],
+        col_hot[...],
+        (((1,), (1,)), ((), ())),
+        preferred_element_type=jnp.float32,
+    )
+    for lay in range(p.lays):
+        lanes = slice(lay * p.cols, (lay + 1) * p.cols)
+        out[lay] = (
+            total[0 : p.e1, lanes]
+            + total[p.e0 : p.e0 + p.e1, lanes]
+            + total[2 * p.e0 : 2 * p.e0 + p.e1, lanes]
+        )
+
+
+def spread(p, step, row_hot, col_hot):
+    wide = col_hot.shape[1]
+    return pl.pallas_call(
+        functools.partial(spread_kernel, p, step),
+        out_shape=f32(p.lays, p.e1, p.cols),
+        in_specs=[VMEM] * 2,
+        out_specs=VMEM,
+        scratch_shapes=[pltpu.VMEM((3 * p.e0, p.lays * p.cols), jnp.float32)],
+        compiler_params=PARAMS,
+        cost_estimate=cost(6 * p.e0 * wide * p.lays * p.cols, 12 * wide),
+    )(row_hot, col_hot)
+
+
+def advance(
+    p, side, now, before, before_at, coeff, coeff_at, recv_x, recv_a, recv_b, source, added, added_at,
+    out, margin, wanted=None,
+):
+    even = parity("grp") == 0
+    g = lax.axis_index("grp")
+    beyond = jnp.where(even, g > 0, g < p.n_grp - 1)
+    first = lax.axis_index("gx") * p.rows - margin
+    count = p.rows + 2 * margin
+    lane = lax.broadcasted_iota(jnp.int32, (8, p.cols), 1)
+    line = lax.broadcasted_iota(jnp.int32, (8, p.cols), 0)
+    for r in range(0, count, 8):
+        rows = slice(r, r + 8)
+        weights = [
+            [coeff[i * p.lays + lay, coeff_at + r : coeff_at + r + 8, :] for i in range(3)]
+            for lay in range(p.lays)
+        ]
+        tall = lot_rows(p, count)
+        lot = r // tall
+        strip = recv_x[r - lot * tall : r - lot * tall + 8, :]
+        edge = r < margin or r + 8 > p.rows + margin
+        if edge:
+            grid_row = first + r + line
+            known = (grid_row >= 0) & (grid_row < p.nx)
+        for f in range(p.fields):
+            reach = margin if f == 1 else margin - MAXOFF
+            if r + 8 <= margin - reach or r >= p.rows + margin + reach:
+                continue
+            if wanted is not None and not wanted(f, r):
+                continue
+            far = jnp.where(beyond, recv_b[f, rows, :], 0.0)
+            near = recv_a[f, rows, :]
+            below = jnp.where(even, far, near)
+            above = jnp.where(even, near, far)
+            mids = [
+                now[f * p.lays + lay, REACH + r : REACH + r + 8, :] for lay in range(p.lays)
+            ]
+            stack = [below] + mids + [above]
+            for lay in range(p.lays):
+                plane = f * p.lays + lay
+                x = mids[lay]
+                mid = STENCIL[0] * x
+                dxx = mid
+                dyy = mid
+                for j in range(1, REACH + 1):
+                    dxx = dxx + STENCIL[j] * (
+                        now[plane, REACH + r + j : REACH + r + j + 8, :]
+                        + now[plane, REACH + r - j : REACH + r - j + 8, :]
+                    )
+                    at = lot * p.lot + plane * REACH
+                    shift = (p.cols - j - at if side == 0 else j - at - REACH) % p.cols
+                    fill = pltpu.roll(strip, shift, 1) if shift else strip
+                    right = jnp.where(
+                        lane < p.cols - j, pltpu.roll(x, p.cols - j, 1), fill if side == 0 else 0.0
+                    )
+                    left = jnp.where(lane >= j, pltpu.roll(x, j, 1), fill if side == 1 else 0.0)
+                    dyy = dyy + STENCIL[j] * (right + left)
+                dzz = stack[lay] + stack[lay + 2] - 2.0 * x
+                w = weights[lay]
+                new = (
+                    2.0 * x
+                    - before[plane, before_at + r : before_at + r + 8, :]
+                    + (w[0] * dxx + w[1] * dyy + w[2] * dzz)
+                )
+                extra = added if f == 1 else source
+                new = new + extra[lay, added_at + r : added_at + r + 8, :]
+                if edge:
+                    new = jnp.where(known, new, 0.0)
+                out[plane, rows, :] = new
+
+
+def cut(p, out, target, part, margin):
+    start = margin + part * p.half
+    for lay in range(p.lays):
+        target[lay * p.half : (lay + 1) * p.half, :] = out[lay, start : start + p.half, :]
+        at = p.lays * p.half + lay * p.near
+        start_r = start - MAXOFF
+        target[at : at + p.near, :] = out[p.lays + lay, start_r : start_r + p.near, :]
+
+
+def extend(p, own, got_a, got_b):
+    return pl.pallas_call(
+        lambda own, got_a, got_b, out: lay_out(p, out, own, got_a, got_b),
+        out_shape=f32(own.shape[0], p.e0, p.cols),
+        in_specs=[VMEM] * 3,
+        out_specs=VMEM,
+        compiler_params=PARAMS,
+        cost_estimate=cost(0, 8 * own.shape[0] * p.e0 * p.cols),
+    )(own, got_a, got_b)
+
+
+def first_kernel(p, now, rest, recv_x, recv_a, recv_b, source, added, out, send_x, send_a, send_b):
+    gap = p.d0 - p.d1
+    for side in range(2):
+
+        @pl.when(lax.axis_index("gy") == side)
+        def _():
+            advance(
+                p, side, now, rest, gap, rest.at[p.planes :], gap, recv_x, recv_a, recv_b,
+                source.at[0], added, 0, out, p.d1,
+            )
+
+    send_edges(p, out, send_x, send_a, send_b, p.d1 - p.d2, p.e2)
+
+
+def first_step(p, now, rest, edges, source, added):
+    return pl.pallas_call(
+        functools.partial(first_kernel, p),
+        out_shape=(f32(p.planes, p.e1, p.cols), *edges_shape(p, p.e2)),
+        in_specs=[VMEM] * 7,
+        out_specs=(VMEM,) * 4,
+        compiler_params=PARAMS,
+        cost_estimate=cost(60 * p.planes * p.e1 * p.cols, 8 * p.planes * p.e1 * p.cols),
+    )(now, rest, *edges, source, added)
+
+
+def share_kernel(p, out, keep, give):
+    for side in range(2):
+
+        @pl.when(lax.axis_index("gy") == side)
+        def _():
+            cut(p, out, keep, side, p.d1)
+            cut(p, out, give, 1 - side, p.d1)
+
+
+def share(p, one):
+    return pl.pallas_call(
+        functools.partial(share_kernel, p),
+        out_shape=(f32(p.gift, p.cols), f32(p.gift, p.cols)),
+        in_specs=[VMEM],
+        out_specs=(VMEM,) * 2,
+        compiler_params=PARAMS,
+        cost_estimate=cost(0, 16 * p.gift * p.cols),
+    )(one)
+
+
+def second_kernel(p, giving, now, before, rest, recv_x, recv_a, recv_b, source, added, *refs):
+    out, share = refs[-2:]
+    for side in range(2):
+
+        def wanted(f, r, part=1 - side):
+            start = p.d2 + part * p.half - (MAXOFF if f == 1 else 0)
+            size = p.half + (2 * MAXOFF if f == 1 else 0)
+            return (start <= r < start + size) == giving
+
+        @pl.when(lax.axis_index("gy") == side)
+        def _():
+            advance(
+                p, side, now, before, p.d0 - p.d2, rest.at[p.planes :], p.d0 - p.d2,
+                recv_x, recv_a, recv_b, source.at[1], added, p.d1 - p.d2, out, p.d2, wanted,
+            )
+            cut(p, out, share, 1 - side if giving else side, p.d2)
+
+
+def second_step(p, giving, now, before, rest, edges, source, added, *fields):
+    return pl.pallas_call(
+        functools.partial(second_kernel, p, giving),
+        out_shape=(f32(p.planes, p.e2, p.cols), f32(p.gift, p.cols)),
+        in_specs=[VMEM] * (8 + len(fields)),
+        out_specs=(VMEM,) * 2,
+        input_output_aliases={} if giving else {8: 0},
+        compiler_params=PARAMS,
+        cost_estimate=cost(30 * p.planes * p.e2 * p.cols, 8 * p.planes * p.e2 * p.cols),
+    )(now, before, rest, *edges, source, added, *fields)
+
+
+def image_kernel(p, mine, one, two, offsets, *refs):
+    if mine:
+        fields, out, advanced, held, order, place, sems, order_sem, done_sem = refs
+    else:
+        _, out, held, order, place, sems, order_sem = refs
+    fetch = pltpu.make_async_copy(offsets, order, order_sem)
+    fetch.start()
+    b = lax.axis_index("gy")
+    block = pl.multiple_of((b if mine else 1 - b) * p.cols, p.cols)
+    copies = []
+    if mine:
+        copies.append(
+            pltpu.make_async_copy(fields.at[:, pl.ds(p.d2, p.rows), :], advanced, done_sem)
+        )
+        copies[0].start()
+    ready = 0
+
+    def launch(d):
+        copy = pltpu.make_async_copy(
+            held.at[d], out.at[place[d], :, :, pl.ds(block, p.cols)], sems.at[d]
+        )
+        copy.start()
+        copies.append(copy)
+
+    for d in range(NOFF):
+        for lay in range(p.lays):
+            for r in range(0, p.half, 8):
+                s = lay * p.half + r
+                at = p.lays * p.half + lay * p.near + r + d
+                held[d, lay, r : r + 8, :] = (
+                    one[s : s + 8, :] * one[at : at + 8, :]
+                    + two[s : s + 8, :] * two[at : at + 8, :]
+                )
+        if d < EARLY:
+            continue
+        if d == EARLY:
+            fetch.wait()
+            for k in range(NOFF):
+                place[order[k] + MAXOFF] = k
+        while ready <= d:
+            launch(ready)
+            ready += 1
+    for copy in copies:
+        copy.wait()
+
+
+def image_call(p, mine, one, two, offsets, last):
+    size = NOFF * p.lays * p.half * p.cols
+    images = f32(NOFF, p.lays, p.half, p.ny)
+    scratch = [
+        pltpu.VMEM((NOFF, p.lays, p.half, p.cols), jnp.float32),
+        pltpu.SMEM((NOFF,), jnp.int32),
+        pltpu.SMEM((NOFF,), jnp.int32),
+        pltpu.SemaphoreType.DMA((NOFF,)),
+        pltpu.SemaphoreType.DMA,
+    ]
+    return pl.pallas_call(
+        functools.partial(image_kernel, p, mine),
+        out_shape=(images, f32(p.planes, p.rows, p.cols)) if mine else images,
+        in_specs=[VMEM] * 3 + ([VMEM] if mine else [HBM]),
+        out_specs=(HBM, HBM) if mine else HBM,
+        scratch_shapes=scratch + ([pltpu.SemaphoreType.DMA] if mine else []),
+        input_output_aliases={} if mine else {3: 0},
+        compiler_params=PARAMS,
+        cost_estimate=cost(3 * size, 4 * size),
+    )(one, two, offsets, last)
+
+
+def pairs_grp(p):
+    return [(g, g ^ 1) for g in range(p.n_grp)]
+
+
+def pairs_between(p):
+    pairs = []
+    for g in range(p.n_grp):
+        to = g + 1 if g % 2 else g - 1
+        for a in range(p.n_gx):
+            goal = (to, a) if 0 <= to < p.n_grp else (g, a ^ 1)
+            pairs.append((g * p.n_gx + a, goal[0] * p.n_gx + goal[1]))
+    return pairs
+
+
+def pairs_rows(p, odd):
+    pairs = []
+    for g in range(p.n_grp):
+        for a in range(p.n_gx):
+            to = a + 1 if a % 2 == odd else a - 1
+            goal = (g, to) if 0 <= to < p.n_gx else (g ^ 1, a)
+            pairs.append((g * p.n_gx + a, goal[0] * p.n_gx + goal[1]))
+    return pairs
+
+
+BESIDE = [(0, 1), (1, 0)]
+
+
+def body_tile_deep(
+    p, previous, current, coeff, src_index, src_amp, rec_index, rec_amp, offsets
+):
+    tile = (p.rows, p.cols)
+
+    def rows_around(low, high, own):
+        got_a = lax.ppermute(low, ("grp", "gx"), pairs_rows(p, 0))
+        got_b = lax.ppermute(high, ("grp", "gx"), pairs_rows(p, 1))
+        return own, got_a, got_b
+
+    def edges_around(send_x, send_a, send_b):
+        recv_x = lax.ppermute(send_x, "gy", BESIDE)
+        recv_b = lax.ppermute(send_b, ("grp", "gx"), pairs_between(p))
+        recv_a = lax.ppermute(send_a, "grp", pairs_grp(p))
+        return recv_x, recv_a, recv_b
+
+    count = rec_index.shape[0]
+    wide = -(-count // 128)
+    if wide * 128 > count:
+        rec_index = jnp.pad(rec_index, (0, wide * 128 - count))
+        rec_amp = jnp.pad(rec_amp, ((0, 0), (0, wide * 128 - count)))
+    (now, rest), points = pack(
+        p,
+        (
+            (current.reshape(p.planes, *tile),),
+            (previous.reshape(p.planes, *tile), coeff.reshape(3 * p.lays, *tile)),
+        ),
+        (rec_index.reshape(wide, 128), rec_amp, offsets),
+    )
+    *points, offsets = points
+    now = rows_around(*now)
+    rest = rows_around(*rest)
+    row_hot, col_hot, source = mark(p, *points, src_index, src_amp.T)
+    added = []
+    for step in range(STEPS):
+        added.append(spread(p, step, row_hot, col_hot))
+    whole, *edges = join(p, *now)
+    edges = edges_around(*edges)
+    rest = extend(p, *rest)
+    one, *edges = first_step(p, whole, rest, edges, source, added[0])
+    edges = edges_around(*edges)
+    keep_one, give = share(p, one)
+    got_one = lax.ppermute(give, "gy", BESIDE)
+    inputs = (one, whole, rest, edges, source, added[1])
+    two, give = second_step(p, True, *inputs)
+    got_two = lax.ppermute(give, "gy", BESIDE)
+    two, keep_two = second_step(p, False, *inputs, two)
+    images, advanced = image_call(p, True, keep_one, keep_two, offsets, two)
+    images = image_call(p, False, got_one, got_two, offsets, images)
+    return images, advanced.reshape(p.fields, p.lays, *tile)
+
+
 def solution(mesh):
+    planned = mesh.shape["gy"] == 2 and mesh.shape["grp"] % 2 == 0 and mesh.shape["gx"] % 2 == 0
+
+    def body(previous, *others):
+        p = Plan(previous.shape, mesh.shape)
+        if planned and p.fits():
+            return body_tile_deep(p, previous, *others)
+        return body_tiles(previous, *others)
+
     return jax.shard_map(
         body,
         mesh=mesh,

time: 127 us -> 32.1 us (0.25)
  other arithmetic: 30 us -> 0 us
  between operations: 28.4 us -> 1.41 us
  starting transfers between devices: 42.2 us -> 15.7 us
  local copies, waits for them, and re-layouts: 10.7 us -> 0 us
  Pallas kernels: 0 us -> 9.08 us
  waiting for transfers between devices: 14.5 us -> 5.77 us
    unnamed x5 -> x0, other arithmetic: 24.9 us -> none
    ppermute x14 -> x12, starting transfers between devices: 38.6 us -> 15.7 us  [the longest x2 5.97 us: edges_around(): recv_b = lax.ppermute(send_b, ('grp', 'gx'), pairs_between(p))]
    pallas_call x0 -> x12, Pallas kernels: none -> 9.08 us  [the longest x2 3.22 us: image_call(): pl.pallas_call(functools.partial(image_kernel, p, mine), out_shape=(image...]
    ppermute x14 -> x12, waiting for transfers between devices: 14.4 us -> 5.77 us  [the longest x2 2.47 us: edges_around(): recv_x = lax.ppermute(send_x, 'gy', BESIDE)]
    slice x10 -> x0, local copies, waits for them, and re-layouts: 4.15 us -> none  [the longest x4 1.97 us: padded_2(): lax.slice_in_dim(block, 0, width, axis=dim)]
    all_to_all x1 -> x0, starting transfers between devices: 3.68 us -> none  [body(): moved = lax.all_to_all(snaps, 'gy', split_axis=3, concat_axis=4, tiled=True)]
    another operation x4 -> x0, local copies, waits for them, and re-layouts: 2.34 us -> none
    unnamed x29 -> x0, local copies, waits for them, and re-layouts: 2.29 us -> none
  transfers between devices with their start and end apart: 15 -> 12, of which waited for: 5 -> 5; matrix products, arithmetic and copies ran while one was open for 8% -> 0% of each run, Pallas kernels for 0% -> 16%
where the time goes in v4:
time: 32.1 us; the launch traced here: 31.9 us
  starting transfers between devices  15.7 us (49%)
  Pallas kernels  9.08 us (28%)
  waiting for transfers between devices  5.77 us (18%)
  between operations  1.41 us (4%)
    ppermute x2, starting transfers between devices, edges_around(): recv_b = lax.ppermute(send_b, ('grp', 'gx'), pairs_between(p))  5.97 us
    pallas_call x2, Pallas kernels, image_call(): pl.pallas_call(functools.partial(image_kernel, p, mine), out_shape=(image...  3.22 us
    ppermute x2, starting transfers between devices, rows_around(): got_a = lax.ppermute(low, ('grp', 'gx'), pairs_rows(p, 0))  3.2 us
    ppermute x2, starting transfers between devices, edges_around(): recv_x = lax.ppermute(send_x, 'gy', BESIDE)  3.04 us
    ppermute x2, waiting for transfers between devices, edges_around(): recv_x = lax.ppermute(send_x, 'gy', BESIDE)  2.47 us
    ppermute x2, waiting for transfers between devices, rows_around(): got_a = lax.ppermute(low, ('grp', 'gx'), pairs_rows(p, 0))  1.89 us
    ppermute x1, starting transfers between devices, body_tile_deep(): got_two = lax.ppermute(give, 'gy', BESIDE)  1.46 us
    pallas_call x1, Pallas kernels, pack(): pl.pallas_call(functools.partial(pack_kernel, p, [len(group) for group in...  1.39 us
  transfers between devices with their start and end apart: 12, of which 5 were waited for; matrix products, arithmetic and copies ran while one was open for 0% of the time, Pallas kernels for 16%

profile of v4, /device:TPU:0, one launch (start us, length us, event | category | flops | bytes accessed | tf_op | source)
XLA Modules:
  0.0 31.9 jit_solution(8766073378982057972)
XLA Ops:
  0.6 1.4 %shard_map.95 = (f32[4,16,128]{2,1,0:T(8,128)S(1)}, f32[4,16,128]{2,1,0:T(8,128)S(1)}, f32[4,96,128]{2,1,0:T(8,128)S(1)}, f32[10,16,128]{2,1,0:T(8,128)S(1)}, f3...) custom-call(f32[4,96,128]{2,1,0:T(8,128)} %bitcast.7, ...), custom_call_target="tpu_custom_call" | custom-call | bytes 2064384 | tf_op jit(solution)/shard_map/pallas_call | solution.py:208
  2.0 3.1 %collective-permute-start = (f32[4,16,128]{2,1,0:T(8,128)S(1)}, f32[4,16,128]{2,1,0:T(8,128)S(1)}, u32[]{:S(2)}, u32[]{:S(2)}) collective-permute-start(f32[4,16,128]{2,1,0:T(8,128)S(1)} %get-tuple-element.31), channel_id=1, source_target_pairs={{0,2},{2,0},{4,6},{6,4},{8,10},{10,8},{12,14},{14,12},{16,18},{18,... | collective-permute-start | bytes 98312 | tf_op jit(solution)/shard_map/ppermute | solution.py:680
  5.1 0.0 collective-permute-start.1
  5.2 1.9 %collective-permute-done.got_a = f32[4,16,128]{2,1,0:T(8,128)S(1)} collective-permute-done((f32[4,16,128]{2,1,0:T(8,128)S(1)}, f32[4,16,128]{2,1,0:T(8,128)S(1)}, u32[]{:S(2)}, u32[]{:S(2)}) %collective-permute-start) | collective-permute-done | bytes 32800 | tf_op jit(solution)/shard_map/ppermute | solution.py:680
  7.0 0.0 collective-permute-done.1.got_b
  7.0 0.2 shard_map.96
  7.2 0.1 collective-permute-start.5
  7.3 3.2 %collective-permute-start.6 = (f32[2,120,128]{2,1,0:T(8,128)S(1)}, f32[2,120,128]{2,1,0:T(8,128)S(1)}, u32[]{:S(2)}, u32[]{:S(2)}) collective-permute-start(f32[2,120,128]{2,1,0:T(8,128)S(1)} %get-tuple-element.39), channel_id=1, source_target_pairs={{0,2},{2,0},{4,6},{6,4},{8,16},{10,18},{12,20},{14,22},{16,8},{18,... | collective-permute-start | bytes 368648 | tf_op jit(solution)/shard_map/ppermute | solution.py:686
  10.5 0.1 collective-permute-start.2
  10.6 1.3 %collective-permute-start.3 = (f32[10,16,128]{2,1,0:T(8,128)S(1)}, f32[10,16,128]{2,1,0:T(8,128)S(1)}, u32[]{:S(2)}, u32[]{:S(2)}) collective-permute-start(f32[10,16,128]{2,1,0:T(8,128)S(1)} %get-tuple-element.36), channel_id=1, source_target_pairs={{0,8},{2,4},{4,2},{6,14},{8,0},{10,12},{12,10},{14,6},{16,24},{18,... | collective-permute-start | bytes 245768 | tf_op jit(solution)/shard_map/ppermute | solution.py:681
  12.5 1.3 %shard_map.98 = (bf16[2,384,2048]{2,1,0:T(8,128)(2,1)S(1)}, bf16[256,2048]{1,0:T(8,128)(2,1)S(1)}, f32[2,2,120,128]{3,2,1,0:T(8,128)S(1)}) custom-call(s32[16,128]{1,0:T(8,128)S(1)} %get-tuple-element.40.index, f32[2,2048]{1,0:T(2,128)S(1)} %get-tuple-element.41.amp, s32[1]{0:T(128)S(6)} %copy.14.src_index_in, f32[1,2]{1,0:T(1,128)} %bitcast.10), custom_call_target="tpu_custom_call" | custom-call | flops 5242880 | bytes 24576 | tf_op jit(solution)/shard_map/pallas_call | solution.py:365
  13.8 1.6 %collective-permute-start.4 = (f32[16,128]{1,0:T(8,128)S(1)}, f32[16,128]{1,0:T(8,128)S(1)}, u32[]{:S(2)}, u32[]{:S(2)}) collective-permute-start(f32[16,128]{1,0:T(8,128)S(1)} %get-tuple-element.37), channel_id=1, source_target_pairs={{0,1},{1,0},{2,3},{3,2},{4,5},{5,4},{6,7},{7,6},{8,9},{9,8},{10,11... | collective-permute-start | bytes 24584 | tf_op jit(solution)/shard_map/ppermute | solution.py:685
  15.4 0.6 %shard_map.99.added = f32[2,120,128]{2,1,0:T(8,128)S(1)} custom-call(bf16[2,384,2048]{2,1,0:T(8,128)(2,1)S(1)} %get-tuple-element.43.row_hot, bf16[256,2048]{1,0:T(8,128)(2,1)S(1)} %get-tuple-element.44.col_hot), custom_call_target="tpu_custom_call" | custom-call | flops 402653184 | bytes 24576 | tf_op jit(solution)/shard_map/pallas_call | solution.py:402
  16.0 0.0 collective-permute-done.2.got_a
  16.0 0.0 collective-permute-done.3.got_b
  16.0 0.1 shard_map.97.rest
  16.0 1.5 %collective-permute-done.4.recv_x = f32[16,128]{1,0:T(8,128)S(1)} collective-permute-done((f32[16,128]{1,0:T(8,128)S(1)}, f32[16,128]{1,0:T(8,128)S(1)}, u32[]{:S(2)}, u32[]{:S(2)}) %collective-permute-start.4) | collective-permute-done | bytes 8224 | tf_op jit(solution)/shard_map/ppermute | solution.py:685
  17.5 0.0 collective-permute-done.5.recv_a
  17.5 0.0 collective-permute-done.6.recv_b
  17.5 0.9 %shard_map.100 = (f32[4,120,128]{2,1,0:T(8,128)S(1)}, f32[16,128]{1,0:T(8,128)S(1)}, f32[2,112,128]{2,1,0:T(8,128)S(1)}, f32[2,112,128]{2,1,0:T(8,128)S(1)}) custom-call(f32[4,128,128]{2,1,0:T(8,128)S(1)} %get-tuple-element.33.now.before, f32[10,128,128]{2,1,0:T(8,128)S(1)} %shard_map.97.rest, f32[16,128]{1,0:T(8,128)S(1)} %collective-permute-done.4.recv_x, ...), custom_call_target="tpu_custom_call" | custom-call | flops 3686400 | bytes 491520 | tf_op jit(solution)/shard_map/pallas_call | solution.py:519
  18.5 0.1 collective-permute-start.9
  18.5 2.8 %collective-permute-start.10 = (f32[2,112,128]{2,1,0:T(8,128)S(1)}, f32[2,112,128]{2,1,0:T(8,128)S(1)}, u32[]{:S(2)}, u32[]{:S(2)}) collective-permute-start(f32[2,112,128]{2,1,0:T(8,128)S(1)} %get-tuple-element.49), channel_id=1, source_target_pairs={{0,2},{2,0},{4,6},{6,4},{8,16},{10,18},{12,20},{14,22},{16,8},{18,... | collective-permute-start | bytes 344072 | tf_op jit(solution)/shard_map/ppermute | solution.py:686
  21.3 1.5 %collective-permute-start.8 = (f32[16,128]{1,0:T(8,128)S(1)}, f32[16,128]{1,0:T(8,128)S(1)}, u32[]{:S(2)}, u32[]{:S(2)}) collective-permute-start(f32[16,128]{1,0:T(8,128)S(1)} %get-tuple-element.47), channel_id=1, source_target_pairs={{0,1},{1,0},{2,3},{3,2},{4,5},{5,4},{6,7},{7,6},{8,9},{9,8},{10,11... | collective-permute-start | bytes 24584 | tf_op jit(solution)/shard_map/ppermute | solution.py:685
  22.8 0.6 %shard_map.102.added = f32[2,120,128]{2,1,0:T(8,128)S(1)} custom-call(bf16[2,384,2048]{2,1,0:T(8,128)(2,1)S(1)} %get-tuple-element.43.row_hot, bf16[256,2048]{1,0:T(8,128)(2,1)S(1)} %get-tuple-element.44.col_hot), custom_call_target="tpu_custom_call" | custom-call | flops 402653184 | bytes 24576 | tf_op jit(solution)/shard_map/pallas_call | solution.py:402
  23.4 0.6 %collective-permute-start.7 = (f32[224,128]{1,0:T(8,128)S(1)}, f32[224,128]{1,0:T(8,128)S(1)}, u32[]{:S(2)}, u32[]{:S(2)}) collective-permute-start(f32[224,128]{1,0:T(8,128)S(1)} %get-tuple-element.46), channel_id=1, source_target_pairs={{0,1},{1,0},{2,3},{3,2},{4,5},{5,4},{6,7},{7,6},{8,9},{9,8},{10,11... | collective-permute-start | bytes 344072 | tf_op jit(solution)/shard_map/ppermute | solution.py:716
  24.0 1.0 %collective-permute-done.8.recv_x = f32[16,128]{1,0:T(8,128)S(1)} collective-permute-done((f32[16,128]{1,0:T(8,128)S(1)}, f32[16,128]{1,0:T(8,128)S(1)}, u32[]{:S(2)}, u32[]{:S(2)}) %collective-permute-start.8) | collective-permute-done | bytes 8224 | tf_op jit(solution)/shard_map/ppermute | solution.py:685
  25.0 0.0 collective-permute-done.9.recv_a
  25.0 0.0 collective-permute-done.10.recv_b
  25.0 0.4 %shard_map.103 = (f32[4,112,128]{2,1,0:T(8,128)S(1)}, f32[224,128]{1,0:T(8,128)S(1)}) custom-call(f32[4,120,128]{2,1,0:T(8,128)S(1)} %get-tuple-element.45.out.now, f32[4,128,128]{2,1,0:T(8,128)S(1)} %get-tuple-element.33.now.before, f32[10,128,128]{2,1,0:T(8,128)S(1)} %shard_map.97.rest, f32[16,128]{1,0:T(8,128)S(1)} %collective-permute-done.8.recv_x, ...), custom_call_target="tpu_custom_call" | custom-call | flops 1720320 | bytes 458752 | tf_op jit(solution)/shard_map/pallas_call | solution.py:568
  25.5 1.5 %collective-permute-start.11 = (f32[224,128]{1,0:T(8,128)S(1)}, f32[224,128]{1,0:T(8,128)S(1)}, u32[]{:S(2)}, u32[]{:S(2)}) collective-permute-start(f32[224,128]{1,0:T(8,128)S(1)} %get-tuple-element.50), channel_id=1, source_target_pairs={{0,1},{1,0},{2,3},{3,2},{4,5},{5,4},{6,7},{7,6},{8,9},{9,8},{10,11... | collective-permute-start | bytes 344072 | tf_op jit(solution)/shard_map/ppermute | solution.py:719
  26.9 0.4 %shard_map.104 = (f32[4,112,128]{2,1,0:T(8,128)S(1)}, f32[224,128]{1,0:T(8,128)S(1)}) custom-call(f32[4,120,128]{2,1,0:T(8,128)S(1)} %get-tuple-element.45.out.now, f32[4,128,128]{2,1,0:T(8,128)S(1)} %get-tuple-element.33.now.before, f32[10,128,128]{2,1,0:T(8,128)S(1)} %shard_map.97.rest, ...), custom_call_target="tpu_custom_call", output_to_operand_aliasing={{0}: (8, {})} | custom-call | flops 1720320 | bytes 458752 | tf_op jit(solution)/shard_map/pallas_call | solution.py:568
  27.3 1.6 %shard_map.105 = (f32[17,2,48,256]{3,2,1,0:T(8,128)}, f32[4,96,128]{2,1,0:T(8,128)}) custom-call(f32[224,128]{1,0:T(8,128)S(1)} %get-tuple-element.52.one, f32[224,128]{1,0:T(8,128)S(1)} %get-tuple-element.54.two, s32[17]{0:T(128)S(1)} %get-tuple-element.51.offsets, f32[4,112,128]{2,1,0:T(8,128)S(1)} %get-tuple-element.55.refs_0_), custom_call_target="tpu_custom_call" | custom-call | flops 626688 | bytes 835584 | tf_op jit(solution)/shard_map/pallas_call | solution.py:635
  28.9 0.2 collective-permute-done.7.one
  29.1 1.2 %collective-permute-done.11.two = f32[224,128]{1,0:T(8,128)S(1)} collective-permute-done((f32[224,128]{1,0:T(8,128)S(1)}, f32[224,128]{1,0:T(8,128)S(1)}, u32[]{:S(2)}, u32[]{:S(2)}) %collective-permute-start.11) | collective-permute-done | bytes 114720 | tf_op jit(solution)/shard_map/ppermute | solution.py:719
  30.3 1.6 %shard_map.106 = f32[17,2,48,256]{3,2,1,0:T(8,128)} custom-call(f32[224,128]{1,0:T(8,128)S(1)} %collective-permute-done.7.one, f32[224,128]{1,0:T(8,128)S(1)} %collective-permute-done.11.two, s32[17]{0:T(128)S(1)} %get-tuple-element.51.offsets, f32[17,2,48,256]{3,2,1,0:T(8,128)} %get-tuple-element.56.refs_0_), custom_call_target="tpu_custom_call", output_to_operand_aliasing={{}: (3, {})} | custom-call | flops 626688 | bytes 835584 | tf_op jit(solution)/shard_map/pallas_call | solution.py:635
  (1 shorter events, 0.0 us)
Async XLA Ops:
  2.0 5.0 %collective-permute-start = (f32[4,16,128]{2,1,0:T(8,128)S(1)}, f32[4,16,128]{2,1,0:T(8,128)S(1)}, u32[]{:S(2)}, u32[]{:S(2)}) collective-permute-start(f32[4,16,128]{2,1,0:T(8,128)S(1)} %get-tuple-element.31), channel_id=1, source_target_pairs={{0,2},{2,0},{4,6},{6,4},{8,10},{10,8},{12,14},{14,12},{16,18},{18,... | collective-permute-start | bytes 98312 | tf_op jit(solution)/shard_map/ppermute | solution.py:680
  5.1 1.9 %collective-permute-start.1 = (f32[4,16,128]{2,1,0:T(8,128)S(1)}, f32[4,16,128]{2,1,0:T(8,128)S(1)}, u32[]{:S(2)}, u32[]{:S(2)}) collective-permute-start(f32[4,16,128]{2,1,0:T(8,128)S(1)} %get-tuple-element.32), channel_id=1, source_target_pairs={{0,8},{2,4},{4,2},{6,14},{8,0},{10,12},{12,10},{14,6},{16,24},{18,... | collective-permute-start | bytes 98312 | tf_op jit(solution)/shard_map/ppermute | solution.py:681
  7.2 10.3 %collective-permute-start.5 = (f32[2,120,128]{2,1,0:T(8,128)S(1)}, f32[2,120,128]{2,1,0:T(8,128)S(1)}, u32[]{:S(2)}, u32[]{:S(2)}) collective-permute-start(f32[2,120,128]{2,1,0:T(8,128)S(1)} %get-tuple-element.38), channel_id=1, source_target_pairs={{0,8},{8,0},{16,24},{24,16},{1,9},{9,1},{17,25},{25,17},{2,10},{10... | collective-permute-start | bytes 368648 | tf_op jit(solution)/shard_map/ppermute | solution.py:687
  7.3 10.2 %collective-permute-start.6 = (f32[2,120,128]{2,1,0:T(8,128)S(1)}, f32[2,120,128]{2,1,0:T(8,128)S(1)}, u32[]{:S(2)}, u32[]{:S(2)}) collective-permute-start(f32[2,120,128]{2,1,0:T(8,128)S(1)} %get-tuple-element.39), channel_id=1, source_target_pairs={{0,2},{2,0},{4,6},{6,4},{8,16},{10,18},{12,20},{14,22},{16,8},{18,... | collective-permute-start | bytes 368648 | tf_op jit(solution)/shard_map/ppermute | solution.py:686
  10.5 5.4 %collective-permute-start.2 = (f32[10,16,128]{2,1,0:T(8,128)S(1)}, f32[10,16,128]{2,1,0:T(8,128)S(1)}, u32[]{:S(2)}, u32[]{:S(2)}) collective-permute-start(f32[10,16,128]{2,1,0:T(8,128)S(1)} %get-tuple-element.35), channel_id=1, source_target_pairs={{0,2},{2,0},{4,6},{6,4},{8,10},{10,8},{12,14},{14,12},{16,18},{18,... | collective-permute-start | bytes 245768 | tf_op jit(solution)/shard_map/ppermute | solution.py:680
  10.6 5.4 %collective-permute-start.3 = (f32[10,16,128]{2,1,0:T(8,128)S(1)}, f32[10,16,128]{2,1,0:T(8,128)S(1)}, u32[]{:S(2)}, u32[]{:S(2)}) collective-permute-start(f32[10,16,128]{2,1,0:T(8,128)S(1)} %get-tuple-element.36), channel_id=1, source_target_pairs={{0,8},{2,4},{4,2},{6,14},{8,0},{10,12},{12,10},{14,6},{16,24},{18,... | collective-permute-start | bytes 245768 | tf_op jit(solution)/shard_map/ppermute | solution.py:681
  13.8 3.7 %collective-permute-start.4 = (f32[16,128]{1,0:T(8,128)S(1)}, f32[16,128]{1,0:T(8,128)S(1)}, u32[]{:S(2)}, u32[]{:S(2)}) collective-permute-start(f32[16,128]{1,0:T(8,128)S(1)} %get-tuple-element.37), channel_id=1, source_target_pairs={{0,1},{1,0},{2,3},{3,2},{4,5},{5,4},{6,7},{7,6},{8,9},{9,8},{10,11... | collective-permute-start | bytes 24584 | tf_op jit(solution)/shard_map/ppermute | solution.py:685
  18.5 6.6 %collective-permute-start.9 = (f32[2,112,128]{2,1,0:T(8,128)S(1)}, f32[2,112,128]{2,1,0:T(8,128)S(1)}, u32[]{:S(2)}, u32[]{:S(2)}) collective-permute-start(f32[2,112,128]{2,1,0:T(8,128)S(1)} %get-tuple-element.48), channel_id=1, source_target_pairs={{0,8},{8,0},{16,24},{24,16},{1,9},{9,1},{17,25},{25,17},{2,10},{10... | collective-permute-start | bytes 344072 | tf_op jit(solution)/shard_map/ppermute | solution.py:687
  18.5 6.5 %collective-permute-start.10 = (f32[2,112,128]{2,1,0:T(8,128)S(1)}, f32[2,112,128]{2,1,0:T(8,128)S(1)}, u32[]{:S(2)}, u32[]{:S(2)}) collective-permute-start(f32[2,112,128]{2,1,0:T(8,128)S(1)} %get-tuple-element.49), channel_id=1, source_target_pairs={{0,2},{2,0},{4,6},{6,4},{8,16},{10,18},{12,20},{14,22},{16,8},{18,... | collective-permute-start | bytes 344072 | tf_op jit(solution)/shard_map/ppermute | solution.py:686
  21.3 3.7 %collective-permute-start.8 = (f32[16,128]{1,0:T(8,128)S(1)}, f32[16,128]{1,0:T(8,128)S(1)}, u32[]{:S(2)}, u32[]{:S(2)}) collective-permute-start(f32[16,128]{1,0:T(8,128)S(1)} %get-tuple-element.47), channel_id=1, source_target_pairs={{0,1},{1,0},{2,3},{3,2},{4,5},{5,4},{6,7},{7,6},{8,9},{9,8},{10,11... | collective-permute-start | bytes 24584 | tf_op jit(solution)/shard_map/ppermute | solution.py:685
  23.4 5.7 %collective-permute-start.7 = (f32[224,128]{1,0:T(8,128)S(1)}, f32[224,128]{1,0:T(8,128)S(1)}, u32[]{:S(2)}, u32[]{:S(2)}) collective-permute-start(f32[224,128]{1,0:T(8,128)S(1)} %get-tuple-element.46), channel_id=1, source_target_pairs={{0,1},{1,0},{2,3},{3,2},{4,5},{5,4},{6,7},{7,6},{8,9},{9,8},{10,11... | collective-permute-start | bytes 344072 | tf_op jit(solution)/shard_map/ppermute | solution.py:716
  25.5 4.9 %collective-permute-start.11 = (f32[224,128]{1,0:T(8,128)S(1)}, f32[224,128]{1,0:T(8,128)S(1)}, u32[]{:S(2)}, u32[]{:S(2)}) collective-permute-start(f32[224,128]{1,0:T(8,128)S(1)} %get-tuple-element.50), channel_id=1, source_target_pairs={{0,1},{1,0},{2,3},{3,2},{4,5},{5,4},{6,7},{7,6},{8,9},{9,8},{10,11... | collective-permute-start | bytes 344072 | tf_op jit(solution)/shard_map/ppermute | solution.py:719

commit v5 on v4

--- a/solution.py
+++ b/solution.py
@@ -100,7 +100,7 @@
 
 VMEM = pl.BlockSpec(memory_space=pltpu.VMEM)
 HBM = pl.BlockSpec(memory_space=pltpu.HBM)
-EARLY = 6
+SMEM = pl.BlockSpec(memory_space=pltpu.SMEM)
 PARAMS = pltpu.CompilerParams(vmem_limit_bytes=16 << 20)
 
 
@@ -155,70 +155,50 @@
     return lax.rem(lax.axis_index(name), 2)
 
 
-def pack_kernel(p, groups, extra, *refs):
-    refs = list(refs)
-
-    def take(n):
-        taken = refs[:n]
-        del refs[:n]
-        return taken
-
-    sources = [take(n) for n in groups]
-    smalls = take(extra)
-    outs = [take(3) for _ in groups]
-    held = take(extra)
-    sems, small_sems = refs
+def pack_kernel(p, current, previous, coeff, *refs):
+    cur_low, cur_high, rest_low, rest_high, own = refs[4:9]
+    sems = refs[-1]
     odd = parity("gx")
-    starts = (
-        ((1 - odd) * (p.rows - p.d0), p.d0),
-        (odd * (p.rows - p.d0), p.d0),
-        (0, p.rows),
-    )
-    copies = []
-    i = 0
-    for members, out in zip(sources, outs):
-        plane = 0
-        for source in members:
-            planes = source.shape[0]
-            for j, (start, size) in enumerate(starts):
-                copies.append(
-                    pltpu.make_async_copy(
-                        source.at[:, pl.ds(pl.multiple_of(start, 8), size), :],
-                        out[j].at[pl.ds(plane, planes)],
-                        sems.at[i, j],
-                    )
-                )
-            plane += planes
-            i += 1
-    for i in range(extra):
-        copies.append(pltpu.make_async_copy(smalls[i], held[i], small_sems.at[i]))
+    low = pl.ds(pl.multiple_of((1 - odd) * (p.rows - p.d0), 8), p.d0)
+    high = pl.ds(pl.multiple_of(odd * (p.rows - p.d0), 8), p.d0)
+    first, last = pl.ds(0, p.planes), pl.ds(p.planes, coeff.shape[0])
+    moves = [
+        (current.at[:, low, :], cur_low),
+        (current.at[:, high, :], cur_high),
+        (previous.at[:, low, :], rest_low.at[first]),
+        (coeff.at[:, low, :], rest_low.at[last]),
+        (previous.at[:, high, :], rest_high.at[first]),
+        (coeff.at[:, high, :], rest_high.at[last]),
+        (current, own),
+        *zip(refs[:4], refs[9:13]),
+    ]
+    copies = [pltpu.make_async_copy(*move, sems.at[i]) for i, move in enumerate(moves)]
     for copy in copies:
         copy.start()
     for copy in copies:
         copy.wait()
 
 
-def pack(p, groups, smalls):
-    flat = [x for group in groups for x in group]
-    shapes = []
-    for group in groups:
-        planes = sum(x.shape[0] for x in group)
-        shapes += [f32(planes, size, p.cols) for size in (p.d0, p.d0, p.rows)]
-    shapes += [jax.ShapeDtypeStruct(x.shape, x.dtype) for x in smalls]
-    outs = pl.pallas_call(
-        functools.partial(pack_kernel, p, [len(group) for group in groups], len(smalls)),
-        out_shape=tuple(shapes),
-        in_specs=[HBM] * (len(flat) + len(smalls)),
-        out_specs=(VMEM,) * len(shapes),
-        scratch_shapes=[
-            pltpu.SemaphoreType.DMA((len(flat), 3)),
-            pltpu.SemaphoreType.DMA((max(1, len(smalls)),)),
-        ],
-        compiler_params=PARAMS,
-        cost_estimate=cost(0, 4 * sum(x.size for x in flat) * 3),
-    )(*(in_hbm(x) for x in (*flat, *smalls)))
-    count = 3 * len(groups)
-    return [outs[i : i + 3] for i in range(0, count, 3)], outs[count:]
+def pack(p, current, previous, coeff, smalls):
+    planes = p.planes + coeff.shape[0]
+    arrays = (current, previous, coeff, *smalls)
+    return pl.pallas_call(
+        functools.partial(pack_kernel, p),
+        out_shape=(
+            f32(p.planes, p.d0, p.cols),
+            f32(p.planes, p.d0, p.cols),
+            f32(planes, p.d0, p.cols),
+            f32(planes, p.d0, p.cols),
+            f32(p.planes, p.rows, p.cols),
+            *(jax.ShapeDtypeStruct(x.shape, x.dtype) for x in smalls[:-1]),
+            pltpu.SMEM(smalls[-1].shape, smalls[-1].dtype),
+        ),
+        in_specs=[HBM] * len(arrays),
+        out_specs=(VMEM,) * (4 + len(smalls)) + (SMEM,),
+        scratch_shapes=[pltpu.SemaphoreType.DMA((7 + len(smalls),))],
+        compiler_params=PARAMS,
+        cost_estimate=cost(0, 4 * p.planes * p.rows * p.cols * 3),
+    )(*(in_hbm(x) for x in arrays))
 
 
 def lot_rows(p, count):
@@ -302,12 +282,40 @@
     return jnp.floor((x.astype(jnp.float32) + 0.5) * (1.0 / divisor)).astype(jnp.int32)
 
 
-def mark_kernel(
-    p, index, amp, src_index_in, src_amp_in, row_hot, col_hot, source, src_index, src_amp, sems
-):
+def source_kernel(p, src_index, src_amp, source):
+    first_lay = lax.axis_index("grp") * p.lays
+    first_row = lax.axis_index("gx") * p.rows - p.d1
+    first_col = lax.axis_index("gy") * p.cols
+    source[...] = jnp.zeros((STEPS, p.lays, p.e1, p.cols), jnp.float32)
+    for s in range(src_index.shape[0]):
+        flat = src_index[s]
+        line = lax.div(flat, p.ny)
+        lay = lax.div(line, p.nx) - first_lay
+        row = lax.rem(line, p.nx) - first_row
+        col = lax.rem(flat, p.ny) - first_col
+
+        @pl.when((lay >= 0) & (lay < p.lays) & (row >= 0) & (row < p.e1))
+        def _():
+            hit = lax.broadcasted_iota(jnp.int32, (1, p.cols), 1) == col
+            for step in range(STEPS):
+                source[step, lay, pl.ds(row, 1), :] += jnp.where(hit, src_amp[s, step], 0.0)
+
+
+def source_map(p, src_index, src_amp):
+    return pl.pallas_call(
+        functools.partial(source_kernel, p),
+        out_shape=f32(STEPS, p.lays, p.e1, p.cols),
+        in_specs=[SMEM, SMEM],
+        out_specs=VMEM,
+        compiler_params=PARAMS,
+        cost_estimate=cost(0, 4 * STEPS * p.lays * p.e1 * p.cols),
+    )(src_index, pltpu.with_memory_space_constraint(src_amp, pltpu.SMEM))
+
+
+def mark_kernel(p, index, amp, previous, coeff, row_hot, col_hot, own, sems):
     fetches = [
-        pltpu.make_async_copy(src_index_in, src_index, sems.at[0]),
-        pltpu.make_async_copy(src_amp_in, src_amp, sems.at[1]),
+        pltpu.make_async_copy(previous, own.at[pl.ds(0, p.planes)], sems.at[0]),
+        pltpu.make_async_copy(coeff, own.at[pl.ds(p.planes, coeff.shape[0])], sems.at[1]),
     ]
     for fetch in fetches:
         fetch.start()
@@ -343,42 +351,25 @@
                 part = rest.astype(narrow)
                 row_hot[step, i * stride : (i + 1) * stride, at] = jnp.where(hit, part, zero)
                 rest = rest - part.astype(jnp.float32)
-    source[...] = jnp.zeros((STEPS, lays, p.e1, p.cols), jnp.float32)
     for fetch in fetches:
         fetch.wait()
-    for s in range(src_index.shape[0]):
-        flat = src_index[s]
-        line = lax.div(flat, p.ny)
-        lay = lax.div(line, p.nx) - first_lay
-        row = lax.rem(line, p.nx) - first_row
-        col = lax.rem(flat, p.ny) - first_col
-
-        @pl.when((lay >= 0) & (lay < lays) & (row >= 0) & (row < p.e1))
-        def _():
-            hit = lax.broadcasted_iota(jnp.int32, (1, p.cols), 1) == col
-            for step in range(STEPS):
-                source[step, lay, pl.ds(row, 1), :] += jnp.where(hit, src_amp[s, step], 0.0)
-
-
-def mark(p, index, amp, src_index, src_amp):
+
+
+def mark(p, index, amp, previous, coeff):
     wide = index.shape[0] * 128
     return pl.pallas_call(
         functools.partial(mark_kernel, p),
         out_shape=(
             jax.ShapeDtypeStruct((STEPS, 3 * p.e0, wide), jnp.bfloat16),
             jax.ShapeDtypeStruct((p.lays * p.cols, wide), jnp.bfloat16),
-            f32(STEPS, p.lays, p.e1, p.cols),
+            f32(p.planes + coeff.shape[0], p.rows, p.cols),
         ),
-        in_specs=[VMEM] * 3 + [HBM],
+        in_specs=[VMEM] * 2 + [HBM] * 2,
         out_specs=(VMEM,) * 3,
-        scratch_shapes=[
-            pltpu.SMEM(src_index.shape, jnp.int32),
-            pltpu.SMEM(src_amp.shape, jnp.float32),
-            pltpu.SemaphoreType.DMA((2,)),
-        ],
+        scratch_shapes=[pltpu.SemaphoreType.DMA((2,))],
         compiler_params=PARAMS,
         cost_estimate=cost(10 * p.e0 * wide * p.lays, 12 * wide),
-    )(index, amp, src_index, in_hbm(src_amp))
+    )(index, amp, in_hbm(previous), in_hbm(coeff))
 
 
 def spread_kernel(p, step, row_hot, col_hot, out, total):
@@ -578,20 +569,17 @@
 
 def image_kernel(p, mine, one, two, offsets, *refs):
     if mine:
-        fields, out, advanced, held, order, place, sems, order_sem, done_sem = refs
+        fields, out, advanced, place, held, sems, order, order_sem, done_sem = refs
+        fetch = pltpu.make_async_copy(offsets, order, order_sem)
+        fetch.start()
+        settle = pltpu.make_async_copy(fields.at[:, pl.ds(p.d2, p.rows), :], advanced, done_sem)
+        settle.start()
     else:
-        _, out, held, order, place, sems, order_sem = refs
-    fetch = pltpu.make_async_copy(offsets, order, order_sem)
-    fetch.start()
+        place = offsets
+        _, out, held, sems = refs
     b = lax.axis_index("gy")
     block = pl.multiple_of((b if mine else 1 - b) * p.cols, p.cols)
     copies = []
-    if mine:
-        copies.append(
-            pltpu.make_async_copy(fields.at[:, pl.ds(p.d2, p.rows), :], advanced, done_sem)
-        )
-        copies[0].start()
-    ready = 0
 
     def launch(d):
         copy = pltpu.make_async_copy(
@@ -609,15 +597,15 @@
                     one[s : s + 8, :] * one[at : at + 8, :]
                     + two[s : s + 8, :] * two[at : at + 8, :]
                 )
-        if d < EARLY:
-            continue
-        if d == EARLY:
-            fetch.wait()
-            for k in range(NOFF):
-                place[order[k] + MAXOFF] = k
-        while ready <= d:
-            launch(ready)
-            ready += 1
+        if not mine:
+            launch(d)
+    if mine:
+        fetch.wait()
+        for k in range(NOFF):
+            place[order[k] + MAXOFF] = k
+        for d in range(NOFF):
+            launch(d)
+        settle.wait()
     for copy in copies:
         copy.wait()
 
@@ -627,17 +615,24 @@
     images = f32(NOFF, p.lays, p.half, p.ny)
     scratch = [
         pltpu.VMEM((NOFF, p.lays, p.half, p.cols), jnp.float32),
-        pltpu.SMEM((NOFF,), jnp.int32),
-        pltpu.SMEM((NOFF,), jnp.int32),
         pltpu.SemaphoreType.DMA((NOFF,)),
-        pltpu.SemaphoreType.DMA,
     ]
+    if mine:
+        scratch += [
+            pltpu.SMEM((NOFF,), jnp.int32),
+            pltpu.SemaphoreType.DMA,
+            pltpu.SemaphoreType.DMA,
+        ]
+        shapes = (images, f32(p.planes, p.rows, p.cols), pltpu.SMEM((NOFF,), jnp.int32))
+    else:
+        offsets = pltpu.with_memory_space_constraint(offsets, pltpu.SMEM)
+        shapes = images
     return pl.pallas_call(
         functools.partial(image_kernel, p, mine),
-        out_shape=(images, f32(p.planes, p.rows, p.cols)) if mine else images,
-        in_specs=[VMEM] * 3 + ([VMEM] if mine else [HBM]),
-        out_specs=(HBM, HBM) if mine else HBM,
-        scratch_shapes=scratch + ([pltpu.SemaphoreType.DMA] if mine else []),
+        out_shape=shapes,
+        in_specs=[VMEM] * 2 + ([VMEM] * 2 if mine else [SMEM, HBM]),
+        out_specs=(HBM, HBM, SMEM) if mine else HBM,
+        scratch_shapes=scratch,
         input_output_aliases={} if mine else {3: 0},
         compiler_params=PARAMS,
         cost_estimate=cost(3 * size, 4 * size),
@@ -676,10 +671,10 @@
 ):
     tile = (p.rows, p.cols)
 
-    def rows_around(low, high, own):
+    def rows_around(low, high):
         got_a = lax.ppermute(low, ("grp", "gx"), pairs_rows(p, 0))
         got_b = lax.ppermute(high, ("grp", "gx"), pairs_rows(p, 1))
-        return own, got_a, got_b
+        return got_a, got_b
 
     def edges_around(send_x, send_a, send_b):
         recv_x = lax.ppermute(send_x, "gy", BESIDE)
@@ -692,24 +687,21 @@
     if wide * 128 > count:
         rec_index = jnp.pad(rec_index, (0, wide * 128 - count))
         rec_amp = jnp.pad(rec_amp, ((0, 0), (0, wide * 128 - count)))
-    (now, rest), points = pack(
-        p,
-        (
-            (current.reshape(p.planes, *tile),),
-            (previous.reshape(p.planes, *tile), coeff.reshape(3 * p.lays, *tile)),
-        ),
-        (rec_index.reshape(wide, 128), rec_amp, offsets),
-    )
-    *points, offsets = points
-    now = rows_around(*now)
-    rest = rows_around(*rest)
-    row_hot, col_hot, source = mark(p, *points, src_index, src_amp.T)
+    current = current.reshape(p.planes, *tile)
+    previous = previous.reshape(p.planes, *tile)
+    coeff = coeff.reshape(3 * p.lays, *tile)
+    smalls = (rec_index.reshape(wide, 128), rec_amp, offsets, src_amp.T)
+    *edges, own, rec_index, rec_amp, offsets, src_amp = pack(p, current, previous, coeff, smalls)
+    now = rows_around(*edges[:2])
+    rest = rows_around(*edges[2:])
+    row_hot, col_hot, rest_own = mark(p, rec_index, rec_amp, previous, coeff)
+    source = source_map(p, src_index, src_amp)
     added = []
     for step in range(STEPS):
         added.append(spread(p, step, row_hot, col_hot))
-    whole, *edges = join(p, *now)
+    whole, *edges = join(p, own, *now)
     edges = edges_around(*edges)
-    rest = extend(p, *rest)
+    rest = extend(p, rest_own, *rest)
     one, *edges = first_step(p, whole, rest, edges, source, added[0])
     edges = edges_around(*edges)
     keep_one, give = share(p, one)
@@ -718,8 +710,8 @@
     two, give = second_step(p, True, *inputs)
     got_two = lax.ppermute(give, "gy", BESIDE)
     two, keep_two = second_step(p, False, *inputs, two)
-    images, advanced = image_call(p, True, keep_one, keep_two, offsets, two)
-    images = image_call(p, False, got_one, got_two, offsets, images)
+    images, advanced, place = image_call(p, True, keep_one, keep_two, offsets, two)
+    images = image_call(p, False, got_one, got_two, place, images)
     return images, advanced.reshape(p.fields, p.lays, *tile)
 
 

time: 32.1 us -> 31.5 us (0.981)
  Pallas kernels: 9.08 us -> 8.28 us
    ppermute x2, waiting for transfers between devices: 2.47 us -> 1.7 us  [edges_around(): recv_x = lax.ppermute(send_x, 'gy', BESIDE)]
    pallas_call x3 -> x4, Pallas kernels: 4.61 us -> 3.87 us  [the longest x2 2.66 us: image_call(): pl.pallas_call(functools.partial(image_kernel, p, mine), out_shape=shapes...]
    ppermute x1, waiting for transfers between devices: 1.23 us -> 1.72 us  [body_tile_deep(): got_two = lax.ppermute(give, 'gy', BESIDE)]
    ppermute x1, waiting for transfers between devices: 0.16 us -> 0.56 us  [body_tile_deep(): got_one = lax.ppermute(give, 'gy', BESIDE)]
where the time goes in v5:
time: 31.5 us; the launch traced here: 31.3 us
  starting transfers between devices  15.7 us (50%)
  Pallas kernels  8.28 us (26%)
  waiting for transfers between devices  5.9 us (19%)
  between operations  1.41 us (4%)
    ppermute x2, starting transfers between devices, edges_around(): recv_b = lax.ppermute(send_b, ('grp', 'gx'), pairs_between(p))  5.97 us
    ppermute x2, starting transfers between devices, rows_around(): got_a = lax.ppermute(low, ('grp', 'gx'), pairs_rows(p, 0))  3.2 us
    ppermute x2, starting transfers between devices, edges_around(): recv_x = lax.ppermute(send_x, 'gy', BESIDE)  3.03 us
    pallas_call x2, Pallas kernels, image_call(): pl.pallas_call(functools.partial(image_kernel, p, mine), out_shape=shapes...  2.66 us
    ppermute x2, waiting for transfers between devices, rows_around(): got_a = lax.ppermute(low, ('grp', 'gx'), pairs_rows(p, 0))  1.89 us
    ppermute x1, waiting for transfers between devices, body_tile_deep(): got_two = lax.ppermute(give, 'gy', BESIDE)  1.72 us
    ppermute x2, waiting for transfers between devices, edges_around(): recv_x = lax.ppermute(send_x, 'gy', BESIDE)  1.7 us
    ppermute x1, starting transfers between devices, body_tile_deep(): got_two = lax.ppermute(give, 'gy', BESIDE)  1.54 us
  transfers between devices with their start and end apart: 12, of which 5 were waited for; matrix products, arithmetic and copies ran while one was open for 0% of the time, Pallas kernels for 16%

profile of v5, /device:TPU:0, one launch (start us, length us, event | category | flops | bytes accessed | tf_op | source)
XLA Modules:
  0.0 31.3 jit_solution(15099880704530480599)
XLA Ops:
  0.6 1.2 %shard_map.95 = (f32[4,16,128]{2,1,0:T(8,128)S(1)}, f32[4,16,128]{2,1,0:T(8,128)S(1)}, f32[10,16,128]{2,1,0:T(8,128)S(1)}, f32[10,16,128]{2,1,0:T(8,128)S(1)}, f...) custom-call(f32[4,96,128]{2,1,0:T(8,128)} %bitcast.10, ...), custom_call_target="tpu_custom_call" | custom-call | bytes 589824 | tf_op jit(solution)/shard_map/pallas_call | solution.py:185
  1.8 3.1 %collective-permute-start = (f32[4,16,128]{2,1,0:T(8,128)S(1)}, f32[4,16,128]{2,1,0:T(8,128)S(1)}, u32[]{:S(2)}, u32[]{:S(2)}) collective-permute-start(f32[4,16,128]{2,1,0:T(8,128)S(1)} %get-tuple-element.32), channel_id=1, source_target_pairs={{0,2},{2,0},{4,6},{6,4},{8,10},{10,8},{12,14},{14,12},{16,18},{18,... | collective-permute-start | bytes 98312 | tf_op jit(solution)/shard_map/ppermute | solution.py:675
  4.9 0.0 collective-permute-start.1
  4.9 1.9 %collective-permute-done.got_a = f32[4,16,128]{2,1,0:T(8,128)S(1)} collective-permute-done((f32[4,16,128]{2,1,0:T(8,128)S(1)}, f32[4,16,128]{2,1,0:T(8,128)S(1)}, u32[]{:S(2)}, u32[]{:S(2)}) %collective-permute-start) | collective-permute-done | bytes 32800 | tf_op jit(solution)/shard_map/ppermute | solution.py:675
  6.8 0.0 collective-permute-done.1.got_b
  6.8 0.2 shard_map.96
  7.0 0.1 collective-permute-start.5
  7.1 3.2 %collective-permute-start.6 = (f32[2,120,128]{2,1,0:T(8,128)S(1)}, f32[2,120,128]{2,1,0:T(8,128)S(1)}, u32[]{:S(2)}, u32[]{:S(2)}) collective-permute-start(f32[2,120,128]{2,1,0:T(8,128)S(1)} %get-tuple-element.42), channel_id=1, source_target_pairs={{0,2},{2,0},{4,6},{6,4},{8,16},{10,18},{12,20},{14,22},{16,8},{18,... | collective-permute-start | bytes 368648 | tf_op jit(solution)/shard_map/ppermute | solution.py:681
  10.3 0.1 collective-permute-start.2
  10.4 1.3 %collective-permute-start.3 = (f32[10,16,128]{2,1,0:T(8,128)S(1)}, f32[10,16,128]{2,1,0:T(8,128)S(1)}, u32[]{:S(2)}, u32[]{:S(2)}) collective-permute-start(f32[10,16,128]{2,1,0:T(8,128)S(1)} %get-tuple-element.39), channel_id=1, source_target_pairs={{0,8},{2,4},{4,2},{6,14},{8,0},{10,12},{12,10},{14,6},{16,24},{18,... | collective-permute-start | bytes 245768 | tf_op jit(solution)/shard_map/ppermute | solution.py:676
  11.7 1.2 %shard_map.97 = (bf16[2,384,2048]{2,1,0:T(8,128)(2,1)S(1)}, bf16[256,2048]{1,0:T(8,128)(2,1)S(1)}, f32[10,96,128]{2,1,0:T(8,128)S(1)}) custom-call(s32[16,128]{1,0:T(8,128)S(1)} %get-tuple-element.35.index, f32[2,2048]{1,0:T(2,128)S(1)} %get-tuple-element.36.amp, f32[4,96,128]{2,1,0:T(8,128)} %bitcast.9, f32[6,96,128]{2,1,0:T(8,128)} %bitcast.7), custom_call_target="tpu_custom_call" | custom-call | flops 5242880 | bytes 24576 | tf_op jit(solution)/shard_map/pallas_call | solution.py:360
  12.9 1.6 %collective-permute-start.4 = (f32[16,128]{1,0:T(8,128)S(1)}, f32[16,128]{1,0:T(8,128)S(1)}, u32[]{:S(2)}, u32[]{:S(2)}) collective-permute-start(f32[16,128]{1,0:T(8,128)S(1)} %get-tuple-element.40), channel_id=1, source_target_pairs={{0,1},{1,0},{2,3},{3,2},{4,5},{5,4},{6,7},{7,6},{8,9},{9,8},{10,11... | collective-permute-start | bytes 24584 | tf_op jit(solution)/shard_map/ppermute | solution.py:680
  14.4 0.6 %shard_map.100.added = f32[2,120,128]{2,1,0:T(8,128)S(1)} custom-call(bf16[2,384,2048]{2,1,0:T(8,128)(2,1)S(1)} %get-tuple-element.44.row_hot, bf16[256,2048]{1,0:T(8,128)(2,1)S(1)} %get-tuple-element.45.col_hot), custom_call_target="tpu_custom_call" | custom-call | flops 402653184 | bytes 24576 | tf_op jit(solution)/shard_map/pallas_call | solution.py:393
  15.7 0.0 collective-permute-done.2.got_a
  15.7 0.0 collective-permute-done.3.got_b
  15.8 0.1 shard_map.98.rest
  15.8 0.8 %collective-permute-done.4.recv_x = f32[16,128]{1,0:T(8,128)S(1)} collective-permute-done((f32[16,128]{1,0:T(8,128)S(1)}, f32[16,128]{1,0:T(8,128)S(1)}, u32[]{:S(2)}, u32[]{:S(2)}) %collective-permute-start.4) | collective-permute-done | bytes 8224 | tf_op jit(solution)/shard_map/ppermute | solution.py:680
  16.6 0.0 collective-permute-done.5.recv_a
  16.6 0.0 collective-permute-done.6.recv_b
  16.6 0.9 %shard_map.101 = (f32[4,120,128]{2,1,0:T(8,128)S(1)}, f32[16,128]{1,0:T(8,128)S(1)}, f32[2,112,128]{2,1,0:T(8,128)S(1)}, f32[2,112,128]{2,1,0:T(8,128)S(1)}) custom-call(f32[4,128,128]{2,1,0:T(8,128)S(1)} %get-tuple-element.34.now.before, f32[10,128,128]{2,1,0:T(8,128)S(1)} %shard_map.98.rest, f32[16,128]{1,0:T(8,128)S(1)} %collective-permute-done.4.recv_x, ...), custom_call_target="tpu_custom_call" | custom-call | flops 3686400 | bytes 491520 | tf_op jit(solution)/shard_map/pallas_call | solution.py:510
  17.6 2.8 %collective-permute-start.10 = (f32[2,112,128]{2,1,0:T(8,128)S(1)}, f32[2,112,128]{2,1,0:T(8,128)S(1)}, u32[]{:S(2)}, u32[]{:S(2)}) collective-permute-start(f32[2,112,128]{2,1,0:T(8,128)S(1)} %get-tuple-element.50), channel_id=1, source_target_pairs={{0,2},{2,0},{4,6},{6,4},{8,16},{10,18},{12,20},{14,22},{16,8},{18,... | collective-permute-start | bytes 344072 | tf_op jit(solution)/shard_map/ppermute | solution.py:681
  20.3 0.0 collective-permute-start.9
  20.3 1.5 %collective-permute-start.8 = (f32[16,128]{1,0:T(8,128)S(1)}, f32[16,128]{1,0:T(8,128)S(1)}, u32[]{:S(2)}, u32[]{:S(2)}) collective-permute-start(f32[16,128]{1,0:T(8,128)S(1)} %get-tuple-element.48), channel_id=1, source_target_pairs={{0,1},{1,0},{2,3},{3,2},{4,5},{5,4},{6,7},{7,6},{8,9},{9,8},{10,11... | collective-permute-start | bytes 24584 | tf_op jit(solution)/shard_map/ppermute | solution.py:680
  21.8 0.6 %shard_map.103.added = f32[2,120,128]{2,1,0:T(8,128)S(1)} custom-call(bf16[2,384,2048]{2,1,0:T(8,128)(2,1)S(1)} %get-tuple-element.44.row_hot, bf16[256,2048]{1,0:T(8,128)(2,1)S(1)} %get-tuple-element.45.col_hot), custom_call_target="tpu_custom_call" | custom-call | flops 402653184 | bytes 24576 | tf_op jit(solution)/shard_map/pallas_call | solution.py:393
  22.4 0.6 %collective-permute-start.7 = (f32[224,128]{1,0:T(8,128)S(1)}, f32[224,128]{1,0:T(8,128)S(1)}, u32[]{:S(2)}, u32[]{:S(2)}) collective-permute-start(f32[224,128]{1,0:T(8,128)S(1)} %get-tuple-element.47), channel_id=1, source_target_pairs={{0,1},{1,0},{2,3},{3,2},{4,5},{5,4},{6,7},{7,6},{8,9},{9,8},{10,11... | collective-permute-start | bytes 344072 | tf_op jit(solution)/shard_map/ppermute | solution.py:708
  23.1 0.9 %collective-permute-done.8.recv_x = f32[16,128]{1,0:T(8,128)S(1)} collective-permute-done((f32[16,128]{1,0:T(8,128)S(1)}, f32[16,128]{1,0:T(8,128)S(1)}, u32[]{:S(2)}, u32[]{:S(2)}) %collective-permute-start.8) | collective-permute-done | bytes 8224 | tf_op jit(solution)/shard_map/ppermute | solution.py:680
  24.0 0.0 collective-permute-done.10.recv_b
  24.0 0.0 collective-permute-done.9.recv_a
  24.0 0.4 %shard_map.104 = (f32[4,112,128]{2,1,0:T(8,128)S(1)}, f32[224,128]{1,0:T(8,128)S(1)}) custom-call(f32[4,120,128]{2,1,0:T(8,128)S(1)} %get-tuple-element.46.out.now, f32[4,128,128]{2,1,0:T(8,128)S(1)} %get-tuple-element.34.now.before, f32[10,128,128]{2,1,0:T(8,128)S(1)} %shard_map.98.rest, f32[16,128]{1,0:T(8,128)S(1)} %collective-permute-done.8.recv_x, ...), custom_call_target="tpu_custom_call" | custom-call | flops 1720320 | bytes 458752 | tf_op jit(solution)/shard_map/pallas_call | solution.py:559
  24.4 1.5 %collective-permute-start.11 = (f32[224,128]{1,0:T(8,128)S(1)}, f32[224,128]{1,0:T(8,128)S(1)}, u32[]{:S(2)}, u32[]{:S(2)}) collective-permute-start(f32[224,128]{1,0:T(8,128)S(1)} %get-tuple-element.51), channel_id=1, source_target_pairs={{0,1},{1,0},{2,3},{3,2},{4,5},{5,4},{6,7},{7,6},{8,9},{9,8},{10,11... | collective-permute-start | bytes 344072 | tf_op jit(solution)/shard_map/ppermute | solution.py:711
  26.0 0.4 %shard_map.105 = (f32[4,112,128]{2,1,0:T(8,128)S(1)}, f32[224,128]{1,0:T(8,128)S(1)}) custom-call(f32[4,120,128]{2,1,0:T(8,128)S(1)} %get-tuple-element.46.out.now, f32[4,128,128]{2,1,0:T(8,128)S(1)} %get-tuple-element.34.now.before, f32[10,128,128]{2,1,0:T(8,128)S(1)} %shard_map.98.rest, ...), custom_call_target="tpu_custom_call", output_to_operand_aliasing={{0}: (8, {})} | custom-call | flops 1720320 | bytes 458752 | tf_op jit(solution)/shard_map/pallas_call | solution.py:559
  26.3 1.6 %shard_map.106 = (f32[17,2,48,256]{3,2,1,0:T(8,128)}, f32[4,96,128]{2,1,0:T(8,128)}, s32[17]{0:T(128)S(4)}) custom-call(f32[224,128]{1,0:T(8,128)S(1)} %get-tuple-element.52.one, f32[224,128]{1,0:T(8,128)S(1)} %get-tuple-element.54.two, s32[17]{0:T(128)S(1)} %get-tuple-element.55.offsets, f32[4,112,128]{2,1,0:T(8,128)S(1)} %get-tuple-element.56.refs_0_), custom_call_target="tpu_custom_call" | custom-call | flops 626688 | bytes 835584 | tf_op jit(solution)/shard_map/pallas_call | solution.py:630
  28.0 0.6 %collective-permute-done.7.one = f32[224,128]{1,0:T(8,128)S(1)} collective-permute-done((f32[224,128]{1,0:T(8,128)S(1)}, f32[224,128]{1,0:T(8,128)S(1)}, u32[]{:S(2)}, u32[]{:S(2)}) %collective-permute-start.7) | collective-permute-done | bytes 114720 | tf_op jit(solution)/shard_map/ppermute | solution.py:708
  28.5 1.7 %collective-permute-done.11.two = f32[224,128]{1,0:T(8,128)S(1)} collective-permute-done((f32[224,128]{1,0:T(8,128)S(1)}, f32[224,128]{1,0:T(8,128)S(1)}, u32[]{:S(2)}, u32[]{:S(2)}) %collective-permute-start.11) | collective-permute-done | bytes 114720 | tf_op jit(solution)/shard_map/ppermute | solution.py:711
  30.2 1.0 %shard_map.107 = f32[17,2,48,256]{3,2,1,0:T(8,128)} custom-call(f32[224,128]{1,0:T(8,128)S(1)} %collective-permute-done.7.one, f32[224,128]{1,0:T(8,128)S(1)} %collective-permute-done.11.two, s32[17]{0:T(128)S(4)} %get-tuple-element.57.offsets, f32[17,2,48,256]{3,2,1,0:T(8,128)} %get-tuple-element.58.refs_0_), custom_call_target="tpu_custom_call", output_to_operand_aliasing={{}: (3, {})} | custom-call | flops 626688 | bytes 835584 | tf_op jit(solution)/shard_map/pallas_call | solution.py:630
  (2 shorter events, 0.1 us)
Async XLA Ops:
  1.8 5.0 %collective-permute-start = (f32[4,16,128]{2,1,0:T(8,128)S(1)}, f32[4,16,128]{2,1,0:T(8,128)S(1)}, u32[]{:S(2)}, u32[]{:S(2)}) collective-permute-start(f32[4,16,128]{2,1,0:T(8,128)S(1)} %get-tuple-element.32), channel_id=1, source_target_pairs={{0,2},{2,0},{4,6},{6,4},{8,10},{10,8},{12,14},{14,12},{16,18},{18,... | collective-permute-start | bytes 98312 | tf_op jit(solution)/shard_map/ppermute | solution.py:675
  4.9 1.9 %collective-permute-start.1 = (f32[4,16,128]{2,1,0:T(8,128)S(1)}, f32[4,16,128]{2,1,0:T(8,128)S(1)}, u32[]{:S(2)}, u32[]{:S(2)}) collective-permute-start(f32[4,16,128]{2,1,0:T(8,128)S(1)} %get-tuple-element.33), channel_id=1, source_target_pairs={{0,8},{2,4},{4,2},{6,14},{8,0},{10,12},{12,10},{14,6},{16,24},{18,... | collective-permute-start | bytes 98312 | tf_op jit(solution)/shard_map/ppermute | solution.py:676
  7.0 9.6 %collective-permute-start.5 = (f32[2,120,128]{2,1,0:T(8,128)S(1)}, f32[2,120,128]{2,1,0:T(8,128)S(1)}, u32[]{:S(2)}, u32[]{:S(2)}) collective-permute-start(f32[2,120,128]{2,1,0:T(8,128)S(1)} %get-tuple-element.41), channel_id=1, source_target_pairs={{0,8},{8,0},{16,24},{24,16},{1,9},{9,1},{17,25},{25,17},{2,10},{10... | collective-permute-start | bytes 368648 | tf_op jit(solution)/shard_map/ppermute | solution.py:682
  7.1 9.5 %collective-permute-start.6 = (f32[2,120,128]{2,1,0:T(8,128)S(1)}, f32[2,120,128]{2,1,0:T(8,128)S(1)}, u32[]{:S(2)}, u32[]{:S(2)}) collective-permute-start(f32[2,120,128]{2,1,0:T(8,128)S(1)} %get-tuple-element.42), channel_id=1, source_target_pairs={{0,2},{2,0},{4,6},{6,4},{8,16},{10,18},{12,20},{14,22},{16,8},{18,... | collective-permute-start | bytes 368648 | tf_op jit(solution)/shard_map/ppermute | solution.py:681
  10.3 5.4 %collective-permute-start.2 = (f32[10,16,128]{2,1,0:T(8,128)S(1)}, f32[10,16,128]{2,1,0:T(8,128)S(1)}, u32[]{:S(2)}, u32[]{:S(2)}) collective-permute-start(f32[10,16,128]{2,1,0:T(8,128)S(1)} %get-tuple-element.38), channel_id=1, source_target_pairs={{0,2},{2,0},{4,6},{6,4},{8,10},{10,8},{12,14},{14,12},{16,18},{18,... | collective-permute-start | bytes 245768 | tf_op jit(solution)/shard_map/ppermute | solution.py:675
  10.4 5.4 %collective-permute-start.3 = (f32[10,16,128]{2,1,0:T(8,128)S(1)}, f32[10,16,128]{2,1,0:T(8,128)S(1)}, u32[]{:S(2)}, u32[]{:S(2)}) collective-permute-start(f32[10,16,128]{2,1,0:T(8,128)S(1)} %get-tuple-element.39), channel_id=1, source_target_pairs={{0,8},{2,4},{4,2},{6,14},{8,0},{10,12},{12,10},{14,6},{16,24},{18,... | collective-permute-start | bytes 245768 | tf_op jit(solution)/shard_map/ppermute | solution.py:676
  12.9 3.7 %collective-permute-start.4 = (f32[16,128]{1,0:T(8,128)S(1)}, f32[16,128]{1,0:T(8,128)S(1)}, u32[]{:S(2)}, u32[]{:S(2)}) collective-permute-start(f32[16,128]{1,0:T(8,128)S(1)} %get-tuple-element.40), channel_id=1, source_target_pairs={{0,1},{1,0},{2,3},{3,2},{4,5},{5,4},{6,7},{7,6},{8,9},{9,8},{10,11... | collective-permute-start | bytes 24584 | tf_op jit(solution)/shard_map/ppermute | solution.py:680
  17.6 6.4 %collective-permute-start.10 = (f32[2,112,128]{2,1,0:T(8,128)S(1)}, f32[2,112,128]{2,1,0:T(8,128)S(1)}, u32[]{:S(2)}, u32[]{:S(2)}) collective-permute-start(f32[2,112,128]{2,1,0:T(8,128)S(1)} %get-tuple-element.50), channel_id=1, source_target_pairs={{0,2},{2,0},{4,6},{6,4},{8,16},{10,18},{12,20},{14,22},{16,8},{18,... | collective-permute-start | bytes 344072 | tf_op jit(solution)/shard_map/ppermute | solution.py:681
  20.3 3.7 %collective-permute-start.9 = (f32[2,112,128]{2,1,0:T(8,128)S(1)}, f32[2,112,128]{2,1,0:T(8,128)S(1)}, u32[]{:S(2)}, u32[]{:S(2)}) collective-permute-start(f32[2,112,128]{2,1,0:T(8,128)S(1)} %get-tuple-element.49), channel_id=1, source_target_pairs={{0,8},{8,0},{16,24},{24,16},{1,9},{9,1},{17,25},{25,17},{2,10},{10... | collective-permute-start | bytes 344072 | tf_op jit(solution)/shard_map/ppermute | solution.py:682
  20.3 3.7 %collective-permute-start.8 = (f32[16,128]{1,0:T(8,128)S(1)}, f32[16,128]{1,0:T(8,128)S(1)}, u32[]{:S(2)}, u32[]{:S(2)}) collective-permute-start(f32[16,128]{1,0:T(8,128)S(1)} %get-tuple-element.48), channel_id=1, source_target_pairs={{0,1},{1,0},{2,3},{3,2},{4,5},{5,4},{6,7},{7,6},{8,9},{9,8},{10,11... | collective-permute-start | bytes 24584 | tf_op jit(solution)/shard_map/ppermute | solution.py:680
  22.4 6.1 %collective-permute-start.7 = (f32[224,128]{1,0:T(8,128)S(1)}, f32[224,128]{1,0:T(8,128)S(1)}, u32[]{:S(2)}, u32[]{:S(2)}) collective-permute-start(f32[224,128]{1,0:T(8,128)S(1)} %get-tuple-element.47), channel_id=1, source_target_pairs={{0,1},{1,0},{2,3},{3,2},{4,5},{5,4},{6,7},{7,6},{8,9},{9,8},{10,11... | collective-permute-start | bytes 344072 | tf_op jit(solution)/shard_map/ppermute | solution.py:708
  24.4 5.8 %collective-permute-start.11 = (f32[224,128]{1,0:T(8,128)S(1)}, f32[224,128]{1,0:T(8,128)S(1)}, u32[]{:S(2)}, u32[]{:S(2)}) collective-permute-start(f32[224,128]{1,0:T(8,128)S(1)} %get-tuple-element.51), channel_id=1, source_target_pairs={{0,1},{1,0},{2,3},{3,2},{4,5},{5,4},{6,7},{7,6},{8,9},{9,8},{10,11... | collective-permute-start | bytes 344072 | tf_op jit(solution)/shard_map/ppermute | solution.py:711
